TPU v7x, 32 devices: a whole 2x2x4 slice. The times are simulated.
32 devices in a mesh: dp: 4 (over x, core), seq: 8 (over z, y).
Axes of the slice: x: 2, y: 2, z: 4, core: 2. Of those that a mesh axis runs over, the one named last changes fastest.
Arguments:
- tokens: bfloat16 [4, 4096, 1024], P('dp', 'seq'), may hold values from -6 to 6
- cotangent: bfloat16 [4, 4096, 1024], P('dp', 'seq'), may hold values from -6 to 6
- norm1_gain: float32 [1024], replicated, may hold values from 0.5 to 1.5
- norm1_bias: float32 [1024], replicated, may hold values from -1.25 to 1.25
- in_weight: bfloat16 [1024, 3072], replicated, may hold values from -0.1875 to 0.1875
- in_bias: float32 [3072], replicated, may hold values from -1.25 to 1.25
- short_weight: float32 [3, 3, 1024], P(None, None, 'seq'), may hold values from -3.5 to 3.5
- short_bias: float32 [3, 1024], P(None, 'seq'), may hold values from -1.25 to 1.25
- filter_in: float32 [33, 64], replicated, may hold values from -2 to 2
- filter_in_bias: float32 [64], replicated, may hold values from -3 to 3
- sine_freq: float32 [64], replicated, may hold values from 0.5 to 2
- filter_out: float32 [64, 1024], P(None, 'seq'), may hold values from -0.03125 to 0.03125
- decay_rates: float32 [1024], P('seq'), may hold values from 2 to 64
- filter_bias: float32 [1024], P('seq'), may hold values from -6 to 6
- out_weight: bfloat16 [1024, 1024], replicated, may hold values from -0.1875 to 0.1875
- out_bias: float32 [1024], replicated, may hold values from -1.25 to 1.25
- norm2_gain: float32 [1024], replicated, may hold values from 0.5 to 1.5
- norm2_bias: float32 [1024], replicated, may hold values from -1.25 to 1.25
- up_weight: bfloat16 [1024, 4096], replicated, may hold values from -0.1875 to 0.1875
- up_bias: float32 [4096], replicated, may hold values from -1.25 to 1.25
- down_weight: bfloat16 [4096, 1024], replicated, may hold values from -0.125 to 0.125
- down_bias: float32 [1024], replicated, may hold values from -1.25 to 1.25
Outputs:
- block_output: bfloat16 [4, 4096, 1024], P('dp', 'seq')
- grad_tokens: float32 [4, 4096, 1024], P('dp', 'seq')
- grad_norm1_gain: float32 [1024], replicated
- grad_norm1_bias: float32 [1024], replicated
- grad_in_weight: float32 [1024, 3072], P('seq', 'dp')
- grad_in_bias: float32 [3072], replicated
- grad_short_weight: float32 [3, 3, 1024], P(None, None, 'seq')
- grad_short_bias: float32 [3, 1024], P(None, 'seq')
- grad_filter_in: float32 [33, 64], replicated
- grad_filter_in_bias: float32 [64], replicated
- grad_sine_freq: float32 [64], replicated
- grad_filter_out: float32 [64, 1024], P(None, 'seq')
- grad_filter_bias: float32 [1024], P('seq')
- grad_out_weight: float32 [1024, 1024], P('seq', 'dp')
- grad_out_bias: float32 [1024], replicated
- grad_norm2_gain: float32 [1024], replicated
- grad_norm2_bias: float32 [1024], replicated
- grad_up_weight: float32 [1024, 4096], P('seq', 'dp')
- grad_up_bias: float32 [4096], replicated
- grad_down_weight: float32 [4096, 1024], P('seq', 'dp')
- grad_down_bias: float32 [1024], replicated
All inputs are finite; a program needn't handle non-finite values.
Results may differ from a plain program's by a relative error of at most 0.014.
Values may be sent and summed in bfloat16 or wider, within the bound.
No kernel may reach another device: no remote copies, remote signals or barrier semaphores. Data moves between devices by JAX's collectives and lax.ppermute only.
A program may use at most 320 MiB of HBM per device.

v0:
```python
import math

import jax
import jax.numpy as jnp
from jax import lax
from jax.sharding import PartitionSpec as P

EMB = 33


HIGH = lax.Precision.HIGHEST
EPSILON = 1e-05


def layer_norm(values, scale_vec, shift_vec):
    average = jnp.mean(values, axis=-1, keepdims=True)
    centred = values - average
    variance = jnp.mean(centred * centred, axis=-1, keepdims=True)
    return centred * lax.rsqrt(variance + EPSILON) * scale_vec + shift_vec


def position_features(length):
    steps = jnp.arange(length, dtype=jnp.float32)
    scaled = steps / (length - 1)
    angles = 2.0 * math.pi * steps / length
    bands = (EMB - 1) // 2
    freqs = 0.0001 + jnp.arange(bands, dtype=jnp.float32) * (bands - 1 - 0.0001) / (bands - 1)
    phase = freqs[:, None] * angles[None, :]
    return jnp.concatenate([scaled[None, :], jnp.cos(phase), -jnp.sin(phase)], axis=0)


def make_filter(filter_in, in_shift, sine_freq, filter_out, decay_rates, features):
    hidden_pre = jnp.dot(filter_in.T, features, precision=HIGH) + in_shift[:, None]
    hidden = jnp.sin(sine_freq[:, None] * hidden_pre)
    raw_kernel = jnp.dot(filter_out.T, hidden, precision=HIGH)
    return raw_kernel * jnp.exp(-decay_rates[:, None] * features[0][None, :])


def split_length(full_length):
    leading = 2
    while leading * leading * 2 <= full_length and full_length % (leading * 2) == 0:
        leading = leading * 2
    return (leading, full_length // leading)


def dft_tables(count_p, count_q):
    full_length = count_p * count_q
    index_p = jnp.arange(count_p, dtype=jnp.int32)
    index_q = jnp.arange(count_q, dtype=jnp.int32)
    prod_p = index_p[:, None] * index_p[None, :] % count_p
    prod_q = index_q[:, None] * index_q[None, :] % count_q
    prod_t = index_p[:, None] * index_q[None, :] % full_length
    angle_p = 2.0 * math.pi * prod_p.astype(jnp.float32) / count_p
    angle_q = 2.0 * math.pi * prod_q.astype(jnp.float32) / count_q
    angle_t = 2.0 * math.pi * prod_t.astype(jnp.float32) / full_length
    return (
        jnp.cos(angle_p),
        jnp.sin(angle_p),
        jnp.cos(angle_q),
        jnp.sin(angle_q),
        jnp.cos(angle_t),
        jnp.sin(angle_t),
    )


def forward_real(signal, tables):
    cos_p, sin_p, cos_q, sin_q, cos_t, sin_t = tables
    half_rows = cos_p.shape[0] // 2
    count_q = cos_q.shape[0]
    blocked = signal.reshape(signal.shape[0], half_rows, count_q)
    part_re = jnp.einsum("kn,cnq->ckq", cos_p[:, :half_rows], blocked, precision=HIGH)
    part_im = -jnp.einsum("kn,cnq->ckq", sin_p[:, :half_rows], blocked, precision=HIGH)
    turned_re = part_re * cos_t + part_im * sin_t
    turned_im = part_im * cos_t - part_re * sin_t
    spec_re = jnp.einsum("ckn,nm->ckm", turned_re, cos_q, precision=HIGH) + jnp.einsum(
        "ckn,nm->ckm", turned_im, sin_q, precision=HIGH
    )
    spec_im = jnp.einsum("ckn,nm->ckm", turned_im, cos_q, precision=HIGH) - jnp.einsum(
        "ckn,nm->ckm", turned_re, sin_q, precision=HIGH
    )
    return (spec_re, spec_im)


def inverse_real(spec_re, spec_im, tables):
    cos_p, sin_p, cos_q, sin_q, cos_t, sin_t = tables
    half_rows = cos_p.shape[0] // 2
    full_length = cos_p.shape[0] * cos_q.shape[0]
    back_re = jnp.einsum("ckm,nm->ckn", spec_re, cos_q, precision=HIGH) - jnp.einsum(
        "ckm,nm->ckn", spec_im, sin_q, precision=HIGH
    )
    back_im = jnp.einsum("ckm,nm->ckn", spec_im, cos_q, precision=HIGH) + jnp.einsum(
        "ckm,nm->ckn", spec_re, sin_q, precision=HIGH
    )
    twist_re = back_re * cos_t - back_im * sin_t
    twist_im = back_im * cos_t + back_re * sin_t
    result = jnp.einsum("nk,ckq->cnq", cos_p[:half_rows], twist_re, precision=HIGH) - jnp.einsum(
        "nk,ckq->cnq", sin_p[:half_rows], twist_im, precision=HIGH
    )
    return result.reshape(spec_re.shape[0], full_length // 2) / full_length


def mixer(
    received,
    short_taps,
    tap_shift,
    filter_in,
    in_shift,
    sine_freq,
    filter_out,
    filter_shift,
    decay_rates,
    features,
    tables,
):
    length = received.shape[2]
    shifted_one = jnp.pad(received, ((0, 0), (0, 0), (1, 0)))[:, :, :length]
    shifted_two = jnp.pad(received, ((0, 0), (0, 0), (2, 0)))[:, :, :length]
    short = (
        tap_shift[:, :, None]
        + short_taps[0][:, :, None] * shifted_two
        + short_taps[1][:, :, None] * shifted_one
        + short_taps[2][:, :, None] * received
    )
    gate_out, gate_in, values = (short[0], short[1], short[2])
    kernel = make_filter(filter_in, in_shift, sine_freq, filter_out, decay_rates, features)
    inner = values * gate_in
    inner_re, inner_im = forward_real(inner, tables)
    kernel_re, kernel_im = forward_real(kernel, tables)
    conv = inverse_real(
        inner_re * kernel_re - inner_im * kernel_im,
        inner_re * kernel_im + inner_im * kernel_re,
        tables,
    )
    conv = conv + inner * filter_shift[:, None]
    return conv * gate_out


def reduce_matrices(matrix_grads):
    partial_sums = (
        lax.psum_scatter(matrix_grads[0], "seq", scatter_dimension=0, tiled=True),
        lax.psum_scatter(matrix_grads[1], "seq", scatter_dimension=0, tiled=True),
        lax.psum_scatter(matrix_grads[2], "seq", scatter_dimension=0, tiled=True),
        lax.psum_scatter(matrix_grads[3], "seq", scatter_dimension=0, tiled=True),
    )
    reduced = (
        lax.psum_scatter(partial_sums[0], "dp", scatter_dimension=1, tiled=True),
        lax.psum_scatter(partial_sums[1], "dp", scatter_dimension=1, tiled=True),
        lax.psum_scatter(partial_sums[2], "dp", scatter_dimension=1, tiled=True),
        lax.psum_scatter(partial_sums[3], "dp", scatter_dimension=1, tiled=True),
    )
    return reduced


def on_device(
    tokens,
    cotangent,
    norm1_gain,
    norm1_bias,
    in_weight,
    in_bias,
    short_weight,
    short_bias,
    filter_in,
    filter_in_bias,
    sine_freq,
    filter_out,
    decay_rates,
    filter_bias,
    out_weight,
    out_bias,
    norm2_gain,
    norm2_bias,
    up_weight,
    up_bias,
    down_weight,
    down_bias,
):
    model_width = in_weight.shape[0]
    tok_rows = tokens.shape[1]
    group_size = lax.axis_size("seq")
    length = tok_rows * group_size
    local_tokens = tokens[0].astype(jnp.float32)
    normed, norm1_pull = jax.vjp(layer_norm, local_tokens, norm1_gain, norm1_bias)
    normed_low = normed.astype(jnp.bfloat16)
    in_three = in_weight.reshape(model_width, 3, model_width)
    projected = jnp.einsum("td,dkc->kct", normed_low, in_three, preferred_element_type=jnp.float32)
    projected = projected + in_bias.reshape(3, model_width)[:, :, None]
    received = lax.all_to_all(
        projected.astype(jnp.bfloat16), "seq", split_axis=1, concat_axis=2, tiled=True
    )
    features = position_features(length)
    count_p, count_q = split_length(2 * length)
    tables = dft_tables(count_p, count_q)

    def local_mixer(
        recv_values, taps, tap_shift, first_layer, first_shift, freqs, last_layer, direct_shift
    ):
        return mixer(
            recv_values,
            taps,
            tap_shift,
            first_layer,
            first_shift,
            freqs,
            last_layer,
            direct_shift,
            decay_rates,
            features,
            tables,
        )

    mixed, mixer_pull = jax.vjp(
        local_mixer,
        received.astype(jnp.float32),
        short_weight,
        short_bias,
        filter_in,
        filter_in_bias,
        sine_freq,
        filter_out,
        filter_bias,
    )
    returned = lax.all_to_all(
        mixed.astype(jnp.bfloat16), "seq", split_axis=1, concat_axis=0, tiled=True
    )
    attended = (
        jnp.einsum("ct,ce->te", returned, out_weight, preferred_element_type=jnp.float32) + out_bias
    )
    resid = local_tokens + attended
    normed2, norm2_pull = jax.vjp(layer_norm, resid, norm2_gain, norm2_bias)
    normed2_low = normed2.astype(jnp.bfloat16)
    up_pre = jnp.dot(normed2_low, up_weight, preferred_element_type=jnp.float32) + up_bias
    activated, gelu_pull = jax.vjp(jax.nn.gelu, up_pre)
    activated_low = activated.astype(jnp.bfloat16)
    block_out = (
        resid + jnp.dot(activated_low, down_weight, preferred_element_type=jnp.float32) + down_bias
    )
    grad_out = cotangent[0]
    grad_down = jnp.einsum("tf,td->fd", activated_low, grad_out, preferred_element_type=jnp.float32)
    grad_down_bias = jnp.sum(grad_out.astype(jnp.float32), axis=0)
    grad_activated = jnp.einsum(
        "td,fd->tf", grad_out, down_weight, preferred_element_type=jnp.float32
    )
    grad_up_pre = gelu_pull(grad_activated)[0].astype(jnp.bfloat16)
    grad_up = jnp.einsum("td,tf->df", normed2_low, grad_up_pre, preferred_element_type=jnp.float32)
    grad_up_bias = jnp.sum(grad_up_pre.astype(jnp.float32), axis=0)
    grad_normed2 = jnp.einsum(
        "tf,df->td", grad_up_pre, up_weight, preferred_element_type=jnp.float32
    )
    grad_resid_norm, grad_gain2, grad_shift2 = norm2_pull(grad_normed2)
    grad_resid = grad_out.astype(jnp.float32) + grad_resid_norm
    grad_attn = grad_resid.astype(jnp.bfloat16)
    grad_out_weight = jnp.einsum(
        "ct,te->ce", returned, grad_attn, preferred_element_type=jnp.float32
    )
    grad_out_bias = jnp.sum(grad_attn.astype(jnp.float32), axis=0)
    grad_mixed_rows = jnp.einsum(
        "te,ce->ct", grad_attn, out_weight, preferred_element_type=jnp.float32
    )
    grad_mixed = lax.all_to_all(
        grad_mixed_rows.astype(jnp.bfloat16), "seq", split_axis=0, concat_axis=1, tiled=True
    )
    (
        grad_received,
        grad_taps,
        grad_tap_shift,
        grad_first,
        grad_first_shift,
        grad_freqs,
        grad_last,
        grad_direct,
    ) = mixer_pull(grad_mixed.astype(jnp.float32))
    grad_proj = lax.all_to_all(
        grad_received.astype(jnp.bfloat16), "seq", split_axis=2, concat_axis=1, tiled=True
    )
    grad_in = jnp.einsum("td,kct->dkc", normed_low, grad_proj, preferred_element_type=jnp.float32)
    grad_in = grad_in.reshape(model_width, 3 * model_width)
    grad_in_bias = jnp.sum(grad_proj.astype(jnp.float32), axis=2).reshape(3 * model_width)
    grad_normed = jnp.einsum("kct,dkc->td", grad_proj, in_three, preferred_element_type=jnp.float32)
    grad_tokens_norm, grad_gain1, grad_shift1 = norm1_pull(grad_normed)
    grad_tokens = grad_resid + grad_tokens_norm
    matrix_sums = reduce_matrices((grad_in, grad_out_weight, grad_up, grad_down))
    shared = lax.psum(
        (
            grad_gain1,
            grad_shift1,
            grad_in_bias,
            grad_out_bias,
            grad_gain2,
            grad_shift2,
            grad_up_bias,
            grad_down_bias,
            grad_first,
            grad_first_shift,
            grad_freqs,
        ),
        ("dp", "seq"),
    )
    channel = lax.psum((grad_taps, grad_tap_shift, grad_last, grad_direct), "dp")
    return (
        block_out.astype(jnp.bfloat16)[None],
        grad_tokens[None],
        shared[0],
        shared[1],
        matrix_sums[0],
        shared[2],
        channel[0],
        channel[1],
        shared[8],
        shared[9],
        shared[10],
        channel[2],
        channel[3],
        matrix_sums[1],
        shared[3],
        shared[4],
        shared[5],
        matrix_sums[2],
        shared[6],
        matrix_sums[3],
        shared[7],
    )


def solution(mesh):
    in_specs = (
        P("dp", "seq", None),
        P("dp", "seq", None),
        P(),
        P(),
        P(),
        P(),
        P(None, None, "seq"),
        P(None, "seq"),
        P(),
        P(),
        P(),
        P(None, "seq"),
        P("seq"),
        P("seq"),
        P(),
        P(),
        P(),
        P(),
        P(),
        P(),
        P(),
        P(),
    )
    out_specs = (
        P("dp", "seq", None),
        P("dp", "seq", None),
        P(),
        P(),
        P("seq", "dp"),
        P(),
        P(None, None, "seq"),
        P(None, "seq"),
        P(),
        P(),
        P(),
        P(None, "seq"),
        P("seq"),
        P("seq", "dp"),
        P(),
        P(),
        P(),
        P("seq", "dp"),
        P(),
        P("seq", "dp"),
        P(),
    )
    return jax.shard_map(
        on_device, mesh=mesh, in_specs=in_specs, out_specs=out_specs, check_vma=False
    )
```

profile of v0, /device:TPU:0, one launch (start us, length us, event | category | flops | bytes accessed | tf_op | source)
XLA Modules:
  0.0 1629.5 jit_solution(7584546690204504811)
XLA Ops:
  65.9 70.4 %all-to-all-done = bf16[3,1024,512]{2,0,1:T(4,128)(2,1)} async-done(((bf16[3,1024,512]{2,0,1:T(4,128)(2,1)}), bf16[3,1024,512]{2,0,1:T(4,128)(2,1)}, u32[]{:S(2)}, u32[]{:S(2)}) %all-to-all-start) | async-done | bytes 3145760 | tf_op jit(solution)/shard_map/all_to_all | solution.py:188
  169.5 9.8 fusion.134
  179.3 12.1 fusion.24
  248.7 14.4 multiply_subtract_fusion
  280.7 17.9 %fusion.44 = f32[128,64,64]{0,2,1:T(8,128)S(1)} fusion(f32[128,64]{0,1:T(8,128)S(1)} %get-tuple-element.104, f32[128,64]{0,1:T(8,128)S(1)} %get-tuple-element.105, f32[128,128,64]{1,2,0:T(8,128)S(1)} %fusion.185, f32[128,128,64]{1,2,0:T(8,128)S(1)} %fusion.203, f32[128,128,64]{1,2,0:T(8,128)S(1)} %fusion.183, f32[128,128,64]{1,2,0:T(8,128)S(1)} %fusion.201, ...), kind=kOutput, calls=%fused_computation.89 | convolution fusion | flops 810549248 | bytes 19005440 | tf_op jit(solution)/shard_map/jvp(nk,ckq->cnq)/dot_general | solution.py:96
  298.6 21.2 %multiply_bitcast_fusion = f32[128,64,64]{0,1,2:T(8,128)S(1)} fusion(f32[128,64,64]{0,2,1:T(8,128)S(1)} %fusion.44, f32[128,64]{0,1:T(8,128)S(1)} %get-tuple-element.104, f32[128,64]{0,1:T(8,128)S(1)} %get-tuple-element.105, f32[128,128,64]{1,2,0:T(8,128)S(1)} %fusion.185, f32[128,128,64]{1,2,0:T(8,128)S(1)} %fusion.203, f32[128,128,64]{1,2,0:T(8,128)S(1)} %fusion.183, ...), kind=kOutput, calls=%fused_computation.185 | convolution fusion | flops 811597824 | bytes 21102592 | tf_op jit(solution)/shard_map/jvp(nk,ckq->cnq)/dot_general | solution.py:96
  321.7 29.4 %all_to_all.56 = bf16[128,8,512]{0,2,1:T(8,128)(2,1)} all-to-all(bf16[128,8,512]{0,2,1:T(8,128)(2,1)S(1)} %fusion.119), channel_id=1, replica_groups=mesh['dp'=4,'seq'=8] {'seq'}, dimensions={1} | all-to-all | bytes 2097152 | tf_op jit(solution)/shard_map/all_to_all | solution.py:223
  356.5 10.8 fusion.354
  367.3 16.2 convert_reduce_fusion
  405.5 35.8 %all-to-all-done.2 = bf16[8,128,512]{1,2,0:T(8,128)(2,1)} async-done(((bf16[8,128,512]{1,2,0:T(8,128)(2,1)}), bf16[8,128,512]{1,2,0:T(8,128)(2,1)}, u32[]{:S(2)}, u32[]{:S(2)}) %all-to-all-start.2) | async-done | bytes 1048608 | tf_op jit(solution)/shard_map/all_to_all | solution.py:260
  484.9 17.7 %multiply_add_fusion.2 = (f32[128,128,64]{1,2,0:T(8,128)S(1)}, f32[128,128,64]{1,2,0:T(8,128)}, f32[128,128,64]{1,2,0:T(8,128)}, f32[128,128,64]{1,2,0:T(8,128)}) fusion(f32[128,128,64]{1,2,0:T(8,128)} %get-tuple-element.96, f32[128,128,64]{1,2,0:T(8,128)} %fusion.82, f32[128,128,64]{1,2,0:T(8,128)} %fusion.97, f32[128,128,64]{1,2,0:T(8,128)} %fusion.88, ...), kind=kOutput, calls=%fused_computation.84 | convolution fusion | flops 820043776 | bytes 46137344 | tf_op jit(solution)/shard_map/transpose(jvp(ckm,nm->ckn))/dot_general | solution.py:91
  538.4 12.2 fusion.14
  550.6 9.6 fusion.32
  589.5 20.0 %copy.246 = bf16[3,128,4096]{1,0,2:T(4,128)(2,1)S(1)} copy(bf16[3,128,4096]{1,2,0:T(8,128)(2,1)S(1)} %fusion.9) | data formatting | bytes 6291456 | tf_op jit(solution)/shard_map/convert_element_type | solution.py:274
  609.6 93.3 %all_to_all.57 = bf16[3,128,4096]{1,0,2:T(4,128)(2,1)S(1)} all-to-all(bf16[3,128,4096]{1,0,2:T(4,128)(2,1)S(1)} %copy.246), channel_id=1, replica_groups=mesh['dp'=4,'seq'=8] {'seq'}, dimensions={2} | all-to-all | bytes 6291456 | tf_op jit(solution)/shard_map/all_to_all | solution.py:273
  718.8 13.3 fusion.353
  732.1 15.8 fusion.145
  748.6 176.8 %reduce-scatter.9.cloned.1.call-done = f32[128,3072]{1,0:T(8,128)} async-done(((f32[1024,3072]{1,0:T(8,128)}), f32[128,3072]{1,0:T(8,128)}) %reduce-scatter.9.cloned.1.call-update) | async-done | bytes 1572880 | tf_op jit(solution)/shard_map/reduce_scatter | solution.py:140
  925.5 286.0 %reduce-scatter.17.cloned.1.call-done = f32[128,4096]{1,0:T(8,128)} async-done(((f32[1024,4096]{1,0:T(8,128)}), f32[128,4096]{1,0:T(8,128)}) %reduce-scatter.17.cloned.1.call-update) | async-done | bytes 2097168 | tf_op jit(solution)/shard_map/reduce_scatter | solution.py:142
  1212.0 12.9 fusion.143
  1241.7 255.2 %reduce-scatter.21.cloned.1.call-done = f32[512,1024]{1,0:T(8,128)} async-done(((f32[4096,1024]{1,0:T(8,128)}), f32[512,1024]{1,0:T(8,128)}) %reduce-scatter.21.cloned.1.call-update) | async-done | bytes 2097168 | tf_op jit(solution)/shard_map/reduce_scatter | solution.py:143
  1509.6 12.7 all-reduce.11
  1540.6 41.1 %all-reduce.10 = (f32[1024]{0:T(1024)}, f32[1024]{0:T(1024)}, f32[3072]{0:T(1024)}, f32[33,64]{1,0:T(8,128)}, f32[64]{0:T(128)}, /*index=5*/f32[64]{0:T(128)}, f...) all-reduce(f32[1024]{0:T(1024)S(1)} %get-tuple-element.29, ...), channel_id=1, replica_groups=mesh['dp'=4,'seq'=8] {'dp','seq'}, use_global_device_ids=true, to_apply=%region_9.10 | all-reduce | flops 15552 | bytes 124416 | tf_op jit(solution)/shard_map/psum | solution.py:283
  1587.9 34.5 %reduce-scatter.23.cloned.1.call-done = f32[512,256]{1,0:T(8,128)} async-done(((f32[512,1024]{1,0:T(8,128)}), f32[512,256]{1,0:T(8,128)}) %reduce-scatter.23.cloned.1.call-update) | async-done | bytes 524304 | tf_op jit(solution)/shard_map/reduce_scatter | solution.py:149
  (284 shorter events, 374.8 us)
Async XLA Ops:
  7.2 346.2 %copy-start = (bf16[1024,1024]{1,0:T(8,128)(2,1)S(1)}, bf16[1024,1024]{1,0:T(8,128)(2,1)}, u32[]{:S(2)}) copy-start(bf16[1024,1024]{1,0:T(8,128)(2,1)} %param.36) | copy-start | bytes 6291460
  35.4 100.9 %all-to-all-start = ((bf16[3,1024,512]{2,0,1:T(4,128)(2,1)}), bf16[3,1024,512]{2,0,1:T(4,128)(2,1)}, u32[]{:S(2)}, u32[]{:S(2)}) async-start(bf16[3,1024,512]{2,0,1:T(4,128)(2,1)} %copy.198), calls=%async_computation | async-start | bytes 8388608 | tf_op jit(solution)/shard_map/all_to_all | solution.py:188
  43.9 105.5 %copy-start.50 = (f32[3,128]{1,0:T(4,128)}, f32[3,128]{1,0:T(4,128)S(1)}, u32[]{:S(2)}) copy-start(f32[3,128]{1,0:T(4,128)S(1)} %get-tuple-element.94) | copy-start | bytes 4612
  43.9 105.5 %copy-start.52 = (f32[3,128]{1,0:T(4,128)}, f32[3,128]{1,0:T(4,128)S(1)}, u32[]{:S(2)}) copy-start(f32[3,128]{1,0:T(4,128)S(1)} %get-tuple-element.93) | copy-start | bytes 4612
  43.9 105.5 %copy-start.54 = (f32[3,128]{1,0:T(4,128)}, f32[3,128]{1,0:T(4,128)S(1)}, u32[]{:S(2)}) copy-start(f32[3,128]{1,0:T(4,128)S(1)} %get-tuple-element.95) | copy-start | bytes 4612
  160.2 160.9 %copy-start.2 = (f32[1,128,4096]{1,2,0:T(8,128)}, f32[1,128,4096]{1,2,0:T(8,128)S(1)}, u32[]{:S(2)}) copy-start(f32[1,128,4096]{1,2,0:T(8,128)S(1)} %get-tuple-element.80) | copy-start | bytes 6291460
  321.1 30.1 %copy-start.17 = (f32[128,64,64]{0,2,1:T(8,128)}, f32[128,64,64]{0,2,1:T(8,128)S(1)}, u32[]{:S(2)}) copy-start(f32[128,64,64]{0,2,1:T(8,128)S(1)} %copy.227) | copy-start | bytes 6291460
  321.4 32.0 %copy-start.40 = (f32[1024]{0:T(1024)S(1)}, f32[1024]{0:T(1024)}, u32[]{:S(2)}) copy-start(f32[1024]{0:T(1024)} %param.37) | copy-start | bytes 12292
  356.1 35.5 %copy-start.14 = (f32[512,1024]{1,0:T(8,128)}, f32[512,1024]{1,0:T(8,128)S(1)}, u32[]{:S(2)}) copy-start(f32[512,1024]{1,0:T(8,128)S(1)} %get-tuple-element.98) | copy-start | bytes 6291460
  396.1 45.3 %all-to-all-start.2 = ((bf16[8,128,512]{1,2,0:T(8,128)(2,1)}), bf16[8,128,512]{1,2,0:T(8,128)(2,1)}, u32[]{:S(2)}, u32[]{:S(2)}) async-start(bf16[8,128,512]{1,2,0:T(8,128)(2,1)} %bitcast.369), calls=%async_computation.2 | async-start | bytes 2097152 | tf_op jit(solution)/shard_map/all_to_all | solution.py:260
  400.3 347.7 %reduce-scatter.13.cloned.1.call-start = ((), (), s32[]{:S(2)}) async-start(), calls=%async_computation.14 | async-start | bytes 4718592 | tf_op jit(solution)/shard_map/reduce_scatter | solution.py:141
  405.0 37.7 %copy-start.16 = (f32[1,128,4096]{1,2,0:T(8,128)S(1)}, f32[1,128,4096]{1,2,0:T(8,128)}, u32[]{:S(2)}) copy-start(f32[1,128,4096]{1,2,0:T(8,128)} %get-tuple-element.81) | copy-start | bytes 6291460
  405.0 520.4 %reduce-scatter.9.cloned.1.call-start = ((), (), s32[]{:S(2)}) async-start(), calls=%async_computation.12 | async-start | bytes 14155776 | tf_op jit(solution)/shard_map/reduce_scatter | solution.py:140
  718.7 492.8 %reduce-scatter.17.cloned.1.call-start = ((), (), s32[]{:S(2)}) async-start(), calls=%async_computation.16 | async-start | bytes 18874368 | tf_op jit(solution)/shard_map/reduce_scatter | solution.py:142
  732.1 764.8 %reduce-scatter.21.cloned.1.call-start = ((), (), s32[]{:S(2)}) async-start(), calls=%async_computation.18 | async-start | bytes 18874368 | tf_op jit(solution)/shard_map/reduce_scatter | solution.py:143
  747.9 464.0 %copy-start.76 = (f32[1024]{0:T(1024)S(1)}, f32[1024]{0:T(1024)}, u32[]{:S(2)}) copy-start(f32[1024]{0:T(1024)} %param.43) | copy-start | bytes 12292
  748.0 833.8 %reduce-scatter.15.cloned.1.call-start = ((), (), s32[]{:S(2)}) async-start(), calls=%async_computation.15 | async-start | bytes 655360 | tf_op jit(solution)/shard_map/reduce_scatter | solution.py:147
  748.5 833.2 %reduce-scatter.11.cloned.1.call-start = ((), (), s32[]{:S(2)}) async-start(), calls=%async_computation.13 | async-start | bytes 1966080 | tf_op jit(solution)/shard_map/reduce_scatter | solution.py:146
  925.4 662.5 %reduce-scatter.19.cloned.1.call-start = ((), (), s32[]{:S(2)}) async-start(), calls=%async_computation.17 | async-start | bytes 2621440 | tf_op jit(solution)/shard_map/reduce_scatter | solution.py:148
  1211.5 410.9 %reduce-scatter.23.cloned.1.call-start = ((), (), s32[]{:S(2)}) async-start(), calls=%async_computation.19 | async-start | bytes 2621440 | tf_op jit(solution)/shard_map/reduce_scatter | solution.py:149
  1239.2 257.8 %copy-start.37 = (f32[4096]{0:T(1024)S(1)}, f32[4096]{0:T(1024)}, u32[]{:S(2)}) copy-start(f32[4096]{0:T(1024)} %copy-done.36) | copy-start | bytes 49156
  1239.2 257.8 %copy-start.68 = (f32[128]{0:T(128)S(1)}, f32[128]{0:T(128)}, u32[]{:S(2)}) copy-start(f32[128]{0:T(128)} %copy-done.67) | copy-start | bytes 1540
  1241.7 258.6 %copy-start.62 = (f32[64]{0:T(128)S(1)}, f32[64]{0:T(128)}, u32[]{:S(2)}) copy-start(f32[64]{0:T(128)} %param.32) | copy-start | bytes 772
  1537.9 84.5 %copy-start.1 = (bf16[1024,1024]{1,0:T(8,128)(2,1)S(1)}, bf16[1024,1024]{1,0:T(8,128)(2,1)}, u32[]{:S(2)}) copy-start(bf16[1024,1024]{1,0:T(8,128)(2,1)} %param.36) | copy-start | bytes 6291460
  (70 other events, 512.5 us)
Sparse Core Ops, SparseCore 0:
  405.1 97.9 reduce-scatter.12
  718.8 206.5 reduce-scatter.8
  929.7 281.7 reduce-scatter.16
  1215.1 281.7 reduce-scatter.20
  1500.0 21.0 reduce-scatter.14
  1524.1 28.4 reduce-scatter.10
  1555.8 32.0 reduce-scatter.18
  1591.0 31.3 reduce-scatter.22
where the time goes:
time: 1630 us
  waiting for transfers between devices  866 us (53%)
  matrix products  438 us (27%)
  blocking collectives  176 us (11%)
  local copies, waits for them, and re-layouts  68.8 us (4%)
  other arithmetic  52.3 us (3%)
    reduce_scatter x1, waiting for transfers between devices, reduce_matrices(): lax.psum_scatter(matrix_grads[2], 'seq', scatter_dimension=0, tiled=True)  286 us
    reduce_scatter x1, waiting for transfers between devices, reduce_matrices(): lax.psum_scatter(matrix_grads[3], 'seq', scatter_dimension=0, tiled=True)  255 us
    reduce_scatter x1, waiting for transfers between devices, reduce_matrices(): lax.psum_scatter(matrix_grads[0], 'seq', scatter_dimension=0, tiled=True)  177 us
    all_to_all x1, blocking collectives, on_device(): lax.all_to_all(grad_received.astype(jnp.bfloat16), 'seq', split_axis=2, c...  93.3 us
    all_to_all x1, waiting for transfers between devices, on_device(): lax.all_to_all(projected.astype(jnp.bfloat16), 'seq', split_axis=1, conca...  70.4 us
    dot_general x4, matrix products, forward_real(): jnp.einsum('ckn,nm->ckm', turned_re, sin_q, precision=HIGH)  41.6 us
    psum x1, blocking collectives, on_device(): lax.psum((grad_gain1, grad_shift1, grad_in_bias, grad_out_bias, grad_gain...  41.1 us
    dot_general x4, matrix products, forward_real(): jnp.einsum('kn,cnq->ckq', cos_p[:, :half_rows], blocked, precision=HIGH)  38.4 us
  transfers between devices with their start and end apart: 10, of which 7 were waited for; matrix products, arithmetic and copies ran while one was open for 18% of the time, Pallas kernels for 0%

commit v1 on v0

v1 whole, which is shorter than its diff:
```python
import functools
import math

import jax
import jax.numpy as jnp
import numpy as np
from jax import lax
from jax.experimental import pallas as pl
from jax.experimental.pallas import tpu as pltpu
from jax.sharding import PartitionSpec as P

EMB = 33
HIGH = lax.Precision.HIGHEST
EPSILON = 1e-05
BLOCK = 128
ROWS = 16
F32 = jnp.float32
BF16 = jnp.bfloat16


def times_root(re, im, num, den):
    num = num % den
    if num == 0:
        return re, im
    if 4 * num == den:
        return -im, re
    if 2 * num == den:
        return -re, -im
    if 4 * num == 3 * den:
        return im, -re
    angle = 2.0 * math.pi * num / den
    cos, sin = math.cos(angle), math.sin(angle)
    if abs(abs(cos) - abs(sin)) < 1e-12:
        sc, ss = (1.0 if cos > 0 else -1.0), (1.0 if sin > 0 else -1.0)
        root = abs(cos)
        return root * (sc * re - ss * im), root * (sc * im + ss * re)
    return re * cos - im * sin, im * cos + re * sin


def small_fft(re, im, sign):
    count = len(re)
    if count == 1:
        return re, im
    if count == 2:
        return [re[0] + re[1], re[0] - re[1]], [im[0] + im[1], im[0] - im[1]]
    even_re, even_im = small_fft(re[0::2], im[0::2], sign)
    odd_re, odd_im = small_fft(re[1::2], im[1::2], sign)
    low_re, low_im, top_re, top_im = [], [], [], []
    for k in range(count // 2):
        tr, ti = times_root(odd_re[k], odd_im[k], sign * k, count)
        low_re.append(even_re[k] + tr)
        low_im.append(even_im[k] + ti)
        top_re.append(even_re[k] - tr)
        top_im.append(even_im[k] - ti)
    return low_re + top_re, low_im + top_im


def blocks_forward(source, target, count):
    def body(step, carry):
        row = pl.multiple_of(step * ROWS, ROWS)
        re, im = [], []
        for a in range(count):
            value = source[a, pl.ds(row, ROWS), :].astype(F32)
            angle = 2.0 * math.pi * a / (4 * count)
            re.append(value * math.cos(angle))
            im.append(value * math.sin(angle))
        re, im = small_fft(re, im, -1)
        for k in range(count):
            target[k, pl.ds(row, ROWS), :] = re[k].astype(BF16)
            target[k, pl.ds(BLOCK + row, ROWS), :] = im[k].astype(BF16)
        return carry

    lax.fori_loop(0, BLOCK // ROWS, body, 0)


def blocks_inverse(source, emit, count):
    def body(step, carry):
        row = pl.multiple_of(step * ROWS, ROWS)
        re = [source[k, pl.ds(row, ROWS), :] for k in range(count)]
        im = [source[k, pl.ds(BLOCK + row, ROWS), :] for k in range(count)]
        re, im = small_fft(re, im, 1)
        for a in range(count):
            angle = 2.0 * math.pi * a / (4 * count)
            emit(a, row, re[a] * math.cos(angle) + im[a] * math.sin(angle))
        return carry

    lax.fori_loop(0, BLOCK // ROWS, body, 0)


def mxu(left, right):
    return jnp.dot(left, right, preferred_element_type=F32)


def table_kernel(alpha_cos, alpha_sin, beta_cos, beta_sin, forward, inverse, *, scale):
    ca, sa = alpha_cos[0], alpha_sin[0]
    cb, sb = beta_cos[...], beta_sin[...]
    cos = ca * cb - sa * sb
    sin = sa * cb + ca * sb
    forward[0, :BLOCK, :BLOCK] = cos.astype(BF16)
    forward[0, :BLOCK, BLOCK:] = sin.astype(BF16)
    forward[0, BLOCK:, :BLOCK] = (-sin).astype(BF16)
    forward[0, BLOCK:, BLOCK:] = cos.astype(BF16)
    cos, sin = cos.T * scale, sin.T * scale
    inverse[0, :BLOCK, :BLOCK] = cos.astype(BF16)
    inverse[0, :BLOCK, BLOCK:] = (-sin).astype(BF16)
    inverse[0, BLOCK:, :BLOCK] = sin.astype(BF16)
    inverse[0, BLOCK:, BLOCK:] = cos.astype(BF16)


def make_tables(length):
    count = length // BLOCK
    alpha = 2.0 * np.pi * np.arange(BLOCK)[None, :] * (np.arange(count)[:, None] - 0.25) / length
    beta = 2.0 * np.pi * ((np.arange(BLOCK)[:, None] * np.arange(BLOCK)[None, :]) % BLOCK) / BLOCK
    alpha = alpha[:, None, :]
    const = lambda v: jnp.asarray(v, F32)
    row = pl.BlockSpec((1, 1, BLOCK), lambda i: (i, 0, 0))
    flat = pl.BlockSpec((BLOCK, BLOCK), lambda i: (0, 0))
    out = pl.BlockSpec((1, 2 * BLOCK, 2 * BLOCK), lambda i: (i, 0, 0))
    shape = jax.ShapeDtypeStruct((count, 2 * BLOCK, 2 * BLOCK), BF16)
    return pl.pallas_call(
        functools.partial(table_kernel, scale=1.0 / length),
        grid=(count,),
        in_specs=[row, row, flat, flat],
        out_specs=[out, out],
        out_shape=[shape, shape],
        name="tables",
    )(const(np.cos(alpha)), const(np.sin(alpha)), const(np.cos(beta)), const(np.sin(beta)))


def split_spec(value):
    return value[:BLOCK], value[BLOCK:]


def spectrum_kernel(signal, forward, spectrum, mid):
    count = signal.shape[0]
    blocks_forward(signal, mid, count)

    def body(k, carry):
        spectrum[k] = mxu(forward[k], mid[k]).astype(BF16)
        return carry

    lax.fori_loop(0, count, body, 0, unroll=4)


def conv_kernel(signal, kernel_spec, bias, forward, inverse, result, spectrum, mid, back, *, conjugate):
    count = signal.shape[0]
    blocks_forward(signal, mid, count)

    def body(k, carry):
        spec = mxu(forward[k], mid[k])
        spectrum[k] = spec.astype(BF16)
        a_re, a_im = split_spec(spec)
        b_re, b_im = split_spec(kernel_spec[k].astype(F32))
        if conjugate:
            b_im = -b_im
        product = jnp.concatenate([a_re * b_re - a_im * b_im, a_re * b_im + a_im * b_re], axis=0)
        back[k] = mxu(inverse[k], product.astype(BF16))
        return carry

    lax.fori_loop(0, count, body, 0, unroll=4)
    gain = bias[...]

    def emit(a, row, value):
        direct = signal[a, pl.ds(row, ROWS), :].astype(F32) * gain
        result[a, pl.ds(row, ROWS), :] = (value + direct).astype(result.dtype)

    blocks_inverse(back, emit, count)


def kernel_grad_kernel(grad_spec, signal_spec, grad, signal, inverse, result, bias_grad, back):
    count = grad_spec.shape[0]

    def body(k, carry):
        a_re, a_im = split_spec(grad_spec[k].astype(F32))
        b_re, b_im = split_spec(signal_spec[k].astype(F32))
        product = jnp.concatenate([a_re * b_re + a_im * b_im, a_im * b_re - a_re * b_im], axis=0)
        back[k] = mxu(inverse[k], product.astype(BF16))
        return carry

    lax.fori_loop(0, count, body, 0, unroll=4)

    def emit(a, row, value):
        result[a, pl.ds(row, ROWS), :] = value

    blocks_inverse(back, emit, count)

    def total(a, acc):
        prod = grad[a].astype(F32) * signal[a].astype(F32)
        return acc + jnp.sum(prod.reshape(BLOCK // 8, 8, prod.shape[-1]), axis=0)

    acc = lax.fori_loop(0, count, total, jnp.zeros((8, grad.shape[-1]), F32))
    bias_grad[...] = jnp.sum(acc, axis=0, keepdims=True)


VMEM_SPEC = pl.BlockSpec(memory_space=pltpu.VMEM)
BIG = pltpu.CompilerParams(vmem_limit_bytes=48 << 20)


def vmem_call(kernel, outs, scratch, args, name):
    return pl.pallas_call(
        kernel,
        in_specs=[VMEM_SPEC] * len(args),
        out_specs=[VMEM_SPEC] * len(outs),
        out_shape=outs,
        scratch_shapes=scratch,
        compiler_params=BIG,
        name=name,
    )(*args)


class FastMixer:
    def __init__(self, length, channels):
        self.count = length // BLOCK
        self.channels = channels
        self.forward, self.inverse = make_tables(length)
        self.mid = pltpu.VMEM((self.count, 2 * BLOCK, channels), BF16)
        self.back = pltpu.VMEM((self.count, 2 * BLOCK, channels), F32)
        self.spec = jax.ShapeDtypeStruct((self.count, 2 * BLOCK, channels), BF16)

    def blocked(self, value):
        return value.reshape(self.count, BLOCK, self.channels)

    def spectrum(self, signal):
        return vmem_call(
            spectrum_kernel, [self.spec], [self.mid], (self.blocked(signal), self.forward), "spectrum"
        )[0]

    def convolve(self, signal, kernel_spec, bias, conjugate):
        out = jax.ShapeDtypeStruct((self.count, BLOCK, self.channels), BF16)
        result, spectrum = vmem_call(
            functools.partial(conv_kernel, conjugate=conjugate),
            [out, self.spec],
            [self.mid, self.back],
            (self.blocked(signal), kernel_spec, bias[None, :], self.forward, self.inverse),
            "correlate" if conjugate else "convolve",
        )
        return result.reshape(signal.shape), spectrum

    def kernel_grad(self, grad_spec, signal_spec, grad, signal):
        outs = [
            jax.ShapeDtypeStruct((self.count, BLOCK, self.channels), F32),
            jax.ShapeDtypeStruct((1, self.channels), F32),
        ]
        result, bias_grad = vmem_call(
            kernel_grad_kernel,
            outs,
            [self.back],
            (grad_spec, signal_spec, self.blocked(grad), self.blocked(signal), self.inverse),
            "kernel_grad",
        )
        return result.reshape(grad.shape), bias_grad[0]


class PlainMixer:
    def __init__(self, length, channels):
        self.length = length
        self.channels = channels
        full = 2 * length
        p = 2
        while p * p * 2 <= full and full % (p * 2) == 0:
            p = p * 2
        q = full // p
        self.p, self.q = p, q
        ip, iq = jnp.arange(p, dtype=jnp.int32), jnp.arange(q, dtype=jnp.int32)
        tp = 2.0 * math.pi * (ip[:, None] * ip[None, :] % p).astype(F32) / p
        tq = 2.0 * math.pi * (iq[:, None] * iq[None, :] % q).astype(F32) / q
        tt = 2.0 * math.pi * (ip[:, None] * iq[None, :] % full).astype(F32) / full
        self.cp, self.sp, self.cq, self.sq = jnp.cos(tp), jnp.sin(tp), jnp.cos(tq), jnp.sin(tq)
        self.ct, self.st = jnp.cos(tt), jnp.sin(tt)

    def spectrum(self, signal):
        half = self.p // 2
        x = signal.astype(F32).T.reshape(self.channels, half, self.q)
        ein = functools.partial(jnp.einsum, precision=HIGH)
        re = ein("kn,cnq->ckq", self.cp[:, :half], x)
        im = -ein("kn,cnq->ckq", self.sp[:, :half], x)
        re, im = re * self.ct + im * self.st, im * self.ct - re * self.st
        return (
            ein("ckn,nm->ckm", re, self.cq) + ein("ckn,nm->ckm", im, self.sq),
            ein("ckn,nm->ckm", im, self.cq) - ein("ckn,nm->ckm", re, self.sq),
        )

    def back(self, re, im):
        half = self.p // 2
        ein = functools.partial(jnp.einsum, precision=HIGH)
        br = ein("ckm,nm->ckn", re, self.cq) - ein("ckm,nm->ckn", im, self.sq)
        bi = ein("ckm,nm->ckn", im, self.cq) + ein("ckm,nm->ckn", re, self.sq)
        br, bi = br * self.ct - bi * self.st, bi * self.ct + br * self.st
        out = ein("nk,ckq->cnq", self.cp[:half], br) - ein("nk,ckq->cnq", self.sp[:half], bi)
        return (out.reshape(self.channels, self.length) / (2 * self.length)).T

    def convolve(self, signal, kernel_spec, bias, conjugate):
        a_re, a_im = self.spectrum(signal)
        b_re, b_im = kernel_spec
        if conjugate:
            b_im = -b_im
        out = self.back(a_re * b_re - a_im * b_im, a_re * b_im + a_im * b_re)
        out = out + signal.astype(F32) * bias[None, :]
        return out.astype(BF16), (a_re, a_im)

    def kernel_grad(self, grad_spec, signal_spec, grad, signal):
        a_re, a_im = grad_spec
        b_re, b_im = signal_spec
        out = self.back(a_re * b_re + a_im * b_im, a_im * b_re - a_re * b_im)
        return out, jnp.sum(grad.astype(F32) * signal.astype(F32), axis=0)


def position_features(length):
    steps = jnp.arange(length, dtype=F32)
    scaled = steps / (length - 1)
    angles = 2.0 * math.pi * steps / length
    bands = (EMB - 1) // 2
    freqs = 0.0001 + jnp.arange(bands, dtype=F32) * (bands - 1 - 0.0001) / (bands - 1)
    phase = freqs[:, None] * angles[None, :]
    return jnp.concatenate([scaled[None, :], jnp.cos(phase), -jnp.sin(phase)], axis=0)


def swap(value, axis, bit):
    size = lax.axis_size(axis)
    return lax.ppermute(value, axis, [(i, i ^ bit) for i in range(size)])


def pick(value, index, axis):
    return lax.dynamic_index_in_dim(value, index, axis, keepdims=False)


def add(left, right):
    return left.astype(F32) + right.astype(F32)


def seq_stages(block, first_bit):
    seq = lax.axis_size("seq")
    me = lax.axis_index("seq")
    bit = first_bit
    while bit < seq:
        count, rows, cols = block.shape
        pairs = block.reshape(count // 2, 2, rows, cols)
        mine = (me // bit) % 2
        got = swap(pick(pairs, 1 - mine, 1).astype(BF16), "seq", bit)
        block = add(pick(pairs, mine, 1), got)
        bit *= 2
    return block[0]


def scatter_start(left, right, start, width, stride, y_first):
    seq = lax.axis_size("seq")
    dp_me = lax.axis_index("dp")
    mine = lax.axis_index("seq") % 2
    height = left.shape[1] // seq

    def columns(which):
        offset = start + jnp.bitwise_xor(dp_me, which) * stride
        return lax.dynamic_slice_in_dim(right, offset, width, 1)

    def partial(which):
        part = jnp.concatenate([columns(w) for w in which], axis=1)
        return matmul("ta,tb->ab", left, part)

    got = swap(partial((3, 1)).astype(BF16), "dp", 1)
    if y_first:
        both = (partial((2, 0)) + got.astype(F32)).astype(BF16)
        pairs = both.reshape(seq // 2, 2, height, 2 * width)
        return pick(pairs, 1 - mine, 1), pick(pairs, mine, 1)
    send = (partial((2,)) + got[:, :width].astype(F32)).astype(BF16)
    own = (partial((0,)) + got[:, width:].astype(F32)).astype(BF16)
    return send.reshape(seq, height, width), own.reshape(seq, height, width)


def scatter_middle(send, kept, y_first):
    if y_first:
        width = kept.shape[-1] // 2
        got = swap(send, "seq", 1)
        far = add(kept[..., :width], got[..., :width]).astype(BF16)
        return far, add(kept[..., width:], got[..., width:]).astype(BF16)
    got = swap(send, "dp", 2)
    count, height, width = kept.shape
    mine = lax.axis_index("seq") % 2
    kept, got = (v.reshape(count // 2, 2, height, width) for v in (kept, got))
    out = add(pick(kept, 1 - mine, 1), pick(got, 1 - mine, 1)).astype(BF16)
    return out, add(pick(kept, mine, 1), pick(got, mine, 1)).astype(BF16)


def scatter_finish(send, kept, y_first):
    got = swap(send, "dp", 2) if y_first else swap(send, "seq", 1)
    return seq_stages(add(kept, got), 2)


def pack(parts):
    flat = jnp.concatenate([p.reshape(-1) for p in parts])
    short = -flat.shape[0] % 1024
    return jnp.pad(flat, (0, short)).reshape(-1, 128)


def unpack(packed, like):
    flat = packed.reshape(-1)
    out, place = [], 0
    for p in like:
        out.append(flat[place : place + p.size].reshape(p.shape))
        place += p.size
    return out


def sum_all(value, axis):
    bit = 1
    while bit < lax.axis_size(axis):
        value = value + swap(value, axis, bit)
        bit *= 2
    return value


def matmul(spec, left, right):
    return jnp.einsum(spec, left, right, preferred_element_type=F32)


def normalise(value):
    centred = value - jnp.mean(value, axis=-1, keepdims=True)
    scale = lax.rsqrt(jnp.mean(centred * centred, axis=-1, keepdims=True) + EPSILON)
    return centred * scale, scale


def norm_back(grad, normal, scale, gain):
    e = grad * gain
    mean_e = jnp.mean(e, axis=-1, keepdims=True)
    mean_en = jnp.mean(e * normal, axis=-1, keepdims=True)
    return (e - mean_e - normal * mean_en) * scale


def on_device(
    tokens,
    cotangent,
    norm1_gain,
    norm1_bias,
    in_weight,
    in_bias,
    short_weight,
    short_bias,
    filter_in,
    filter_in_bias,
    sine_freq,
    filter_out,
    decay_rates,
    filter_bias,
    out_weight,
    out_bias,
    norm2_gain,
    norm2_bias,
    up_weight,
    up_bias,
    down_weight,
    down_bias,
):
    width = in_weight.shape[0]
    ff = up_weight.shape[1]
    rows = tokens.shape[1]
    seq = lax.axis_size("seq")
    me = lax.axis_index("seq")
    length = rows * seq
    chans = width // seq
    halo = 8
    up_shift = [(i, i + 1) for i in range(seq - 1)]
    down_shift = [(i + 1, i) for i in range(seq - 1)]

    mine = jnp.concatenate([short_weight.reshape(9, chans), short_bias], axis=0)
    all_taps = lax.all_to_all(
        jnp.broadcast_to(mine[None], (seq, 12, chans)), "seq", split_axis=0, concat_axis=0, tiled=True
    )
    all_taps = all_taps.reshape(seq, 12, chans).transpose(1, 0, 2).reshape(12, width)
    taps, tap_shift = all_taps[:9].reshape(3, 3, width), all_taps[9:]

    mixer = (FastMixer if length // BLOCK <= 64 else PlainMixer)(length, chans)
    features = position_features(length)
    hidden_pre = jnp.dot(filter_in.T, features, precision=HIGH) + filter_in_bias[:, None]
    phase = sine_freq[:, None] * hidden_pre
    hidden = jnp.sin(phase)
    window = jnp.exp(-features[0][:, None] * decay_rates[None, :])
    kernel = jnp.einsum("hn,hc->nc", hidden, filter_out, precision=HIGH) * window
    kernel_spec = mixer.spectrum(kernel)

    x = tokens[0]
    before = lax.ppermute(x[rows - halo :], "seq", up_shift)
    x32 = x.astype(F32)
    ext = jnp.concatenate([before.astype(F32), x32], axis=0)
    normal1_ext, scale1_ext = normalise(ext)
    normed_ext = (normal1_ext * norm1_gain + norm1_bias).astype(BF16)
    normal1, scale1 = normal1_ext[halo:], scale1_ext[halo:]
    normed = normed_ext[halo:]
    proj = (matmul("td,dn->tn", normed_ext, in_weight) + in_bias).astype(BF16)
    live = (me > 0) | (jnp.arange(rows + halo)[:, None] >= halo)
    proj = jnp.where(live, proj, 0).astype(F32)

    def lagged(k, j):
        part = proj[:, k * width : (k + 1) * width]
        return part[halo - 2 + j : halo - 2 + j + rows]

    short = [
        tap_shift[k] + sum(taps[j, k] * lagged(k, j) for j in range(3)) for k in range(3)
    ]
    gate_out, gate_in, values = short
    inner = (values * gate_in).astype(BF16)

    def to_channels(value):
        blocks = value.reshape(rows, seq, chans).transpose(1, 0, 2)
        got = lax.all_to_all(blocks, "seq", split_axis=0, concat_axis=0, tiled=True)
        return got.reshape(length, chans)

    def to_tokens(value):
        blocks = value.reshape(seq, rows, chans)
        got = lax.all_to_all(blocks, "seq", split_axis=0, concat_axis=0, tiled=True)
        return got.transpose(1, 0, 2).reshape(rows, width)

    inner_chan = to_channels(inner)
    conv_chan, inner_spec = mixer.convolve(inner_chan, kernel_spec, filter_bias, False)
    conv = to_tokens(conv_chan).astype(F32)

    mixed = (conv * gate_out).astype(BF16)
    resid = x32 + matmul("tc,ce->te", mixed, out_weight) + out_bias
    normal2, scale2 = normalise(resid)
    normed2 = (normal2 * norm2_gain + norm2_bias).astype(BF16)
    up_pre = matmul("td,df->tf", normed2, up_weight) + up_bias
    activated, gelu_pull = jax.vjp(jax.nn.gelu, up_pre)
    activated = activated.astype(BF16)
    block_out = resid + matmul("tf,fd->td", activated, down_weight) + down_bias
    dy = cotangent[0]
    dy32 = dy.astype(F32)
    grad_activated = matmul("td,fd->tf", dy, down_weight)
    grad_up_pre = gelu_pull(grad_activated)[0].astype(BF16)
    down_start = scatter_start(activated, dy, 0, width // 4, width // 4, False)
    d2 = matmul("tf,df->td", grad_up_pre, up_weight)
    up_start = scatter_start(normed2, grad_up_pre, 0, ff // 4, ff // 4, True)
    grad_resid = dy32 + norm_back(d2, normal2, scale2, norm2_gain)
    grad_attn = grad_resid.astype(BF16)
    out_start = scatter_start(mixed, grad_attn, 0, width // 4, width // 4, False)
    grad_mixed = matmul("te,ce->tc", grad_attn, out_weight)
    grad_conv = (grad_mixed * gate_out).astype(BF16)
    grad_gate_out = grad_mixed * conv

    grad_chan = to_channels(grad_conv)
    grad_chan, down_start, up_start, out_start = lax.optimization_barrier(
        (grad_chan, down_start, up_start, out_start)
    )
    down_mid = scatter_middle(*down_start, False)
    up_mid = scatter_middle(*up_start, True)
    out_mid = scatter_middle(*out_start, False)
    grad_inner_chan, grad_spec = mixer.convolve(grad_chan, kernel_spec, filter_bias, True)
    grad_inner = to_tokens(grad_inner_chan)
    grad_inner, down_mid, up_mid, out_mid = lax.optimization_barrier(
        (grad_inner, down_mid, up_mid, out_mid)
    )
    grad_inner = grad_inner.astype(F32)
    grad_down = scatter_finish(*down_mid, False)
    grad_up = scatter_finish(*up_mid, True)
    grad_out_weight = scatter_finish(*out_mid, False)

    grad_kernel, grad_filter_bias = mixer.kernel_grad(grad_spec, inner_spec, grad_chan, inner_chan)
    grad_raw = grad_kernel * window
    grad_filter_out = jnp.einsum("hn,nc->hc", hidden, grad_raw, precision=HIGH)
    grad_phase = jnp.einsum("nc,hc->hn", grad_raw, filter_out, precision=HIGH) * jnp.cos(phase)
    grad_freq = jnp.sum(grad_phase * hidden_pre, axis=1)
    grad_hidden_pre = grad_phase * sine_freq[:, None]
    grad_filter_in = jnp.einsum("en,hn->eh", features, grad_hidden_pre, precision=HIGH)
    grad_filter_in_bias = jnp.sum(grad_hidden_pre, axis=1)

    grad_short = [grad_gate_out, grad_inner * values, grad_inner * gate_in]
    edge = jnp.stack([g[:halo] for g in grad_short]).astype(BF16)
    after = lax.ppermute(edge, "seq", down_shift).astype(F32)
    grad_proj = []
    grad_taps = []
    for k in range(3):
        longer = jnp.concatenate([grad_short[k], after[k]], axis=0)
        grad_proj.append(sum(taps[j, k] * longer[2 - j : 2 - j + rows] for j in range(3)))
        grad_taps.append(jnp.stack([jnp.sum(grad_short[k] * lagged(k, j), axis=0) for j in range(3)]))
    grad_proj = jnp.concatenate(grad_proj, axis=1).astype(BF16)
    grad_taps = jnp.stack(grad_taps, axis=1)
    grad_tap_shift = jnp.stack([jnp.sum(g, axis=0) for g in grad_short])
    part, half = 3 * width // 4, 3 * width // 8
    in_start = [scatter_start(normed, grad_proj, i * half, half, part, bool(i)) for i in range(2)]
    grad_in_bias = jnp.sum(grad_proj.astype(F32), axis=0)
    d1 = matmul("tn,dn->td", grad_proj, in_weight)
    grad_tokens = grad_resid + norm_back(d1, normal1, scale1, norm1_gain)

    shared = (
        jnp.sum(d1 * normal1, axis=0),
        jnp.sum(d1, axis=0),
        grad_in_bias,
        jnp.sum(grad_attn.astype(F32), axis=0),
        jnp.sum(d2 * normal2, axis=0),
        jnp.sum(d2, axis=0),
        jnp.sum(grad_up_pre.astype(F32), axis=0),
        jnp.sum(dy32, axis=0),
        grad_filter_in,
        grad_filter_in_bias,
        grad_freq,
        grad_taps,
        grad_tap_shift,
    )
    channel = (grad_filter_out, grad_filter_bias)
    packed = pack(shared)
    rows_shared = packed.shape[0]
    packed, in_start = lax.optimization_barrier((packed, in_start))
    in_mid = [scatter_middle(*in_start[i], bool(i)) for i in range(2)]
    grad_in = jnp.concatenate([scatter_finish(*in_mid[i], bool(i)) for i in range(2)], axis=1)
    packed = sum_all(jnp.concatenate([packed, pack(channel)], axis=0), "dp")
    channel = unpack(packed[rows_shared:], channel)
    shared = unpack(sum_all(packed[:rows_shared], "seq"), shared)
    own_taps = lax.dynamic_slice_in_dim(shared[11], me * chans, chans, 2)
    own_shift = lax.dynamic_slice_in_dim(shared[12], me * chans, chans, 1)
    return (
        block_out.astype(BF16)[None],
        grad_tokens[None],
        shared[0],
        shared[1],
        grad_in,
        shared[2],
        own_taps,
        own_shift,
        shared[8],
        shared[9],
        shared[10],
        channel[0],
        channel[1],
        grad_out_weight,
        shared[3],
        shared[4],
        shared[5],
        grad_up,
        shared[6],
        grad_down,
        shared[7],
    )


def solution(mesh):
    everywhere, by_token, by_rows = P(), P("dp", "seq", None), P("seq", "dp")
    taps, shift, chan = P(None, None, "seq"), P(None, "seq"), P("seq")
    in_specs = (by_token,) * 2 + (everywhere,) * 4 + (taps, shift) + (everywhere,) * 3
    in_specs += (shift, chan, chan) + (everywhere,) * 8
    out_specs = (by_token, by_token, everywhere, everywhere, by_rows, everywhere, taps, shift)
    out_specs += (everywhere,) * 3 + (shift, chan, by_rows) + (everywhere,) * 3
    out_specs += (by_rows, everywhere, by_rows, everywhere)
    return jax.shard_map(
        on_device, mesh=mesh, in_specs=in_specs, out_specs=out_specs, check_vma=False
    )
```

time: 1630 us -> 461 us (0.28)
  waiting for transfers between devices: 866 us -> 113 us
  matrix products: 438 us -> 121 us
  blocking collectives: 176 us -> 0 us
  Pallas kernels: 0 us -> 57.1 us
  starting transfers between devices: 13 us -> 60.1 us
  local copies, waits for them, and re-layouts: 68.8 us -> 36.4 us
    reduce_scatter x8 -> x0, waiting for transfers between devices: 759 us -> none  [the longest x1 286 us: reduce_matrices(): lax.psum_scatter(matrix_grads[2], 'seq', scatter_dimension=0, tiled=True)]
    dot_general x53 -> x26, matrix products: 438 us -> 121 us  [the longest x21 97.1 us: matmul(): return jnp.einsum(spec, left, right, preferred_element_type=F32)]
    all_to_all x2 -> x0, blocking collectives: 123 us -> none  [the longest x1 93.3 us: on_device(): lax.all_to_all(grad_received.astype(jnp.bfloat16), 'seq', split_axis=2, c...]
    ppermute x0 -> x32, waiting for transfers between devices: none -> 72.9 us  [the longest x30 52.5 us: swap(): return lax.ppermute(value, axis, [(i, i ^ bit) for i in range(size)])]
    all_to_all x2 -> x5, waiting for transfers between devices: 106 us -> 39.7 us  [the longest x2 31.6 us: to_tokens(): got = lax.all_to_all(blocks, 'seq', split_axis=0, concat_axis=0, tiled=True)]
    pallas_call x0 -> x5, Pallas kernels: none -> 57.1 us  [the longest x4 40.9 us: vmem_call(): pl.pallas_call(kernel, in_specs=[VMEM_SPEC] * len(args), out_specs=[VMEM_...]
    psum x2 -> x0, blocking collectives: 53.8 us -> none  [the longest x1 41.1 us: on_device(): lax.psum((grad_gain1, grad_shift1, grad_in_bias, grad_out_bias, grad_gain...]
    ppermute x0 -> x32, starting transfers between devices: none -> 35.7 us  [the longest x30 29.6 us: swap(): return lax.ppermute(value, axis, [(i, i ^ bit) for i in range(size)])]
  transfers between devices with their start and end apart: 10 -> 37, of which waited for: 7 -> 17; matrix products, arithmetic and copies ran while one was open for 18% -> 32% of each run, Pallas kernels for 0% -> 10%
where the time goes in v1:
time: 461 us; the launch traced here: 455 us
  matrix products  121 us (26%)
  waiting for transfers between devices  113 us (25%)
  other arithmetic  65 us (14%)
  starting transfers between devices  60.1 us (13%)
  Pallas kernels  57.1 us (12%)
  local copies, waits for them, and re-layouts  36.4 us (8%)
    dot_general x21, matrix products, matmul(): return jnp.einsum(spec, left, right, preferred_element_type=F32)  97.1 us
    ppermute x30, waiting for transfers between devices, swap(): return lax.ppermute(value, axis, [(i, i ^ bit) for i in range(size)])  52.5 us
    pallas_call x4, Pallas kernels, vmem_call(): pl.pallas_call(kernel, in_specs=[VMEM_SPEC] * len(args), out_specs=[VMEM_...  40.9 us
    all_to_all x2, waiting for transfers between devices, to_tokens(): got = lax.all_to_all(blocks, 'seq', split_axis=0, concat_axis=0, tiled=True)  31.6 us
    ppermute x30, starting transfers between devices, swap(): return lax.ppermute(value, axis, [(i, i ^ bit) for i in range(size)])  29.6 us
    ppermute x1, waiting for transfers between devices, on_device(): after = lax.ppermute(edge, 'seq', down_shift).astype(F32)  20.4 us
    pallas_call x1, Pallas kernels, make_tables(): pl.pallas_call(functools.partial(table_kernel, scale=1.0 / length), grid=...  16.2 us
    unnamed x174, local copies, waits for them, and re-layouts  15.2 us
  transfers between devices with their start and end apart: 37, of which 17 were waited for; matrix products, arithmetic and copies ran while one was open for 32% of the time, Pallas kernels for 10%

profile of v1, /device:TPU:0, one launch (start us, length us, event | category | flops | bytes accessed | tf_op | source)
XLA Modules:
  0.0 454.8 jit_solution(7705292914443026767)
XLA Ops:
  1.5 4.9 %collective-permute-start = (bf16[8,1024]{1,0:T(8,128)(2,1)S(1)}, bf16[8,1024]{1,0:T(8,128)(2,1)S(1)}, u32[]{:S(2)}, u32[]{:S(2)}) collective-permute-start(bf16[8,1024]{1,0:T(8,128)(2,1)S(1)} %slice_bitcast_fusion.4), channel_id=1, source_target_pairs={{0,1},{1,2},{2,3},{3,4},{4,5},{5,6},{6,7},{8,9},{9,10},{10,11},{11... | collective-permute-start | bytes 49160 | tf_op jit(solution)/shard_map/ppermute | solution.py:480
  8.4 4.9 %all-to-all-start = ((f32[8,12,128]{2,1,0:T(8,128)}), f32[8,12,128]{2,1,0:T(8,128)S(1)}, u32[]{:S(2)}, u32[]{:S(2)}) async-start(f32[8,12,128]{2,1,0:T(8,128)} %broadcast_in_dim.16), calls=%async_computation | async-start | bytes 131072 | tf_op jit(solution)/shard_map/all_to_all | solution.py:464
  16.2 16.2 %tables.1 = (bf16[32,256,256]{2,1,0:T(8,128)(2,1)}, bf16[32,256,256]{2,1,0:T(8,128)(2,1)}) custom-call(f32[32,1,128]{2,1,0:T(1,128)} %constant.273.clone.alpha_cos, f32[32,1,128]{2,1,0:T(1,128)} %constant.274.clone.alpha_sin, f32[128,128]{1,0:T(8,128)} %constant.275.clone.beta_cos, f32[128,128]{1,0:T(8,128)} %constant.276.clone.beta_sin), custom_call_target="tpu_custom_call" | custom-call | tf_op jit(solution)/shard_map/tables/pallas_call | solution.py:120
  38.6 5.4 %fusion.10 = f32[520,3072]{1,0:T(8,128)} fusion(bf16[520,1024]{1,0:T(8,128)(2,1)S(1)} %get-tuple-element.116, bf16[1024,3072]{1,0:T(8,128)(2,1)S(1)} %copy-done.73, f32[3072]{0:T(1024)S(1)} %copy-done.75, pred[520]{0:T(1024)(128)(4,1)S(1)} %fusion.123), kind=kOutput, calls=%fused_computation.24 | convolution fusion | flops 3277946880 | bytes 13758984 | tf_op jit(solution)/shard_map/td,dn->tn/dot_general | solution.py:412
  44.2 8.9 %fusion.41 = (bf16[64,8,8,128]{3,2,1,0:T(8,128)(2,1)S(1)}, f32[512,1024]{1,0:T(8,128)}, f32[512,1024]{1,0:T(8,128)}) fusion(f32[520,3072]{1,0:T(8,128)} %fusion.10, f32[1024]{0:T(1024)S(1)} %bitcast.308, f32[1024]{0:T(1024)S(1)} %bitcast.310, f32[1024]{0:T(1024)S(1)} %bitcast.312, f32[1024]{0:T(1024)S(1)} %bitcast.327, f32[1024]{0:T(1024)S(1)} %bitcast.302, ...), kind=kLoop, calls=%fused_computation.118 | loop fusion | flops 7340032 | bytes 17858560
  54.3 6.6 %all-to-all-start.1 = ((bf16[8,512,128]{2,1,0:T(8,128)(2,1)}), bf16[8,512,128]{2,1,0:T(8,128)(2,1)S(1)}, u32[]{:S(2)}, u32[]{:S(2)}) async-start(bf16[8,512,128]{2,1,0:T(8,128)(2,1)} %bitcast.275), calls=%async_computation.1 | async-start | bytes 2097152 | tf_op jit(solution)/shard_map/all_to_all | solution.py:503
  63.1 7.1 %convolution_multiply_fusion = f32[4096,128]{1,0:T(8,128)S(1)} fusion(f32[64,128]{1,0:T(8,128)S(1)} %copy-done.45, f32[128]{0:T(128)S(1)} %copy-done.71, f32[4096]{0:T(1024)S(1)} %multiply_negate_fusion, f32[64,4096]{1,0:T(8,128)S(1)} %fusion.7, f32[64]{0:T(128)S(1)} %copy-done.67), kind=kOutput, calls=%fused_computation.15 | convolution fusion | flops 403963904 | bytes 3195648 | tf_op jit(solution)/shard_map/hn,hc->nc/dot_general | solution.py:476
  70.3 6.4 %spectrum.1.kernel_spec = bf16[32,256,128]{2,1,0:T(8,128)(2,1)S(1)} custom-call(f32[32,128,128]{2,1,0:T(8,128)S(1)} %bitcast.263, bf16[32,256,256]{2,1,0:T(8,128)(2,1)} %get-tuple-element.48.forward), custom_call_target="tpu_custom_call" | custom-call | tf_op jit(solution)/shard_map/spectrum/pallas_call | solution.py:200
  77.9 8.1 %all-to-all-done.1 = bf16[8,512,128]{2,1,0:T(8,128)(2,1)S(1)} async-done(((bf16[8,512,128]{2,1,0:T(8,128)(2,1)}), bf16[8,512,128]{2,1,0:T(8,128)(2,1)S(1)}, u32[]{:S(2)}, u32[]{:S(2)}) %all-to-all-start.1) | async-done | bytes 1048608 | tf_op jit(solution)/shard_map/all_to_all | solution.py:503
  86.1 12.5 %convolve.1 = (bf16[32,128,128]{2,1,0:T(8,128)(2,1)S(1)}, bf16[32,256,128]{2,1,0:T(8,128)(2,1)S(1)}) custom-call(bf16[32,128,128]{2,1,0:T(8,128)(2,1)S(1)} %bitcast.259, bf16[32,256,128]{2,1,0:T(8,128)(2,1)} %copy-done.2, f32[1,128]{1,0:T(1,128)S(1)} %bitcast.265, bf16[32,256,256]{2,1,0:T(8,128)(2,1)} %get-tuple-element.48.forward, ...), custom_call_target="tpu_custom_call" | custom-call | tf_op jit(solution)/shard_map/convolve/pallas_call | solution.py:200
  108.1 22.7 %all-to-all-done.2 = bf16[8,512,128]{2,1,0:T(8,128)(2,1)} async-done(((bf16[8,512,128]{2,1,0:T(8,128)(2,1)}), bf16[8,512,128]{2,1,0:T(8,128)(2,1)}, u32[]{:S(2)}, u32[]{:S(2)}) %all-to-all-start.2) | async-done | bytes 1048608 | tf_op jit(solution)/shard_map/all_to_all | solution.py:508
  138.1 9.8 %multiply_convert_fusion = (bf16[512,4096]{1,0:T(8,128)(2,1)}, f32[512,4096]{1,0:T(8,128)}) fusion(f32[4096]{0:T(1024)S(1)} %copy-done.74, bf16[1024,4096]{1,0:T(8,128)(2,1)S(1)} %bitcast.330, f32[512,1024]{1,0:T(8,128)S(1)} %get-tuple-element.165, f32[1024]{0:T(1024)S(1)} %copy-done.78, f32[1024]{0:T(1024)S(1)} %copy-done.69, f32[512]{0:T(512)S(1)} %add_rsqrt_fusion.1, ...), kind=kOutput, calls=%fused_computation.11 | convolution fusion | flops 4318560256 | bytes 23097344 | tf_op jit(solution)/shard_map/td,df->tf/dot_general | solution.py:412
  147.9 13.7 %convert_reduce_fusion = (f32[4096]{0:T(1024)}, bf16[512,4096]{1,0:T(8,128)(2,1)S(1)}) fusion(f32[512,4096]{1,0:T(8,128)} %get-tuple-element.167, f32[4096]{0:T(1024)S(1)} %copy-done.74, bf16[4096,1024]{1,0:T(8,128)(2,1)} %param.46, bf16[1,512,1024]{2,1,0:T(8,128)(2,1)S(1)} %copy-done.26), kind=kOutput, calls=%fused_computation.9 | convolution fusion | flops 4343197696 | bytes 22052864 | tf_op jit(solution)/shard_map/td,fd->tf/dot_general | solution.py:412
  161.6 8.5 %multiply_reduce_fusion.10 = (f32[1024]{0:T(1024)}, f32[512]{0:T(512)S(1)}, f32[512]{0:T(512)S(1)}, f32[1024]{0:T(1024)}, f32[512,1024]{1,0:T(8,128)S(1)}) fusion(f32[512,1024]{1,0:T(8,128)S(1)} %get-tuple-element.165, f32[512]{0:T(512)S(1)} %add_rsqrt_fusion.1, f32[512]{0:T(512)S(1)} %broadcast_multiply_fusion.5, f32[1024]{0:T(1024)S(1)} %copy-done.69, ...), kind=kOutput, calls=%fused_computation.84 | convolution fusion | flops 4299682816 | bytes 16797696 | tf_op jit(solution)/shard_map/tf,df->td/dot_general | solution.py:412
  193.8 10.8 %fusion.40 = bf16[1,512,1024]{2,1,0:T(8,128)(2,1)} fusion(f32[512,1024]{1,0:T(8,128)} %copy-done.20, bf16[512,4096]{1,0:T(8,128)(2,1)} %get-tuple-element.166, bf16[4096,1024]{1,0:T(8,128)(2,1)} %param.46, f32[1024]{0:T(1024)S(1)} %copy-done.77), kind=kOutput, calls=%fused_computation.116 | convolution fusion | flops 4296540160 | bytes 15732736 | tf_op jit(solution)/shard_map/tf,fd->td/dot_general | solution.py:412
  209.6 4.9 %add_convert_fusion = bf16[1024,2048]{1,0:T(8,128)(2,1)S(1)} fusion(bf16[1024,2048]{1,0:T(8,128)(2,1)} %collective-permute-done.2, bf16[512,1024]{1,0:T(8,128)(2,1)S(1)} %copy-done.38, bf16[512,1024]{1,0:T(8,128)(2,1)S(1)} %copy-done.37, f32[512,1024]{1,0:T(8,128)S(1)} %copy-done.21, f32[1024]{0:T(1024)S(1)} %copy-done.78, f32[1024]{0:T(1024)S(1)} %copy-done.69, ...), kind=kOutput, calls=%fused_computation.10 | convolution fusion | flops 2160590848 | bytes 12595200 | tf_op jit(solution)/shard_map/ta,tb->ab/dot_general | solution.py:412
  231.1 13.5 %correlate.1 = (bf16[32,128,128]{2,1,0:T(8,128)(2,1)}, bf16[32,256,128]{2,1,0:T(8,128)(2,1)S(1)}) custom-call(bf16[32,128,128]{2,1,0:T(8,128)(2,1)S(1)} %bitcast.261, bf16[32,256,128]{2,1,0:T(8,128)(2,1)} %copy-done.2, f32[1,128]{1,0:T(1,128)S(1)} %bitcast.266, bf16[32,256,256]{2,1,0:T(8,128)(2,1)} %get-tuple-element.48.forward, ...), custom_call_target="tpu_custom_call" | custom-call | tf_op jit(solution)/shard_map/correlate/pallas_call | solution.py:200
  250.5 8.5 %kernel_grad.1 = (f32[32,128,128]{2,1,0:T(8,128)S(1)}, f32[1,128]{1,0:T(1,128)S(1)}) custom-call(bf16[32,256,128]{2,1,0:T(8,128)(2,1)} %copy-done.4, bf16[32,256,128]{2,1,0:T(8,128)(2,1)} %copy-done.3, bf16[32,128,128]{2,1,0:T(8,128)(2,1)S(1)} %bitcast.262, bf16[32,128,128]{2,1,0:T(8,128)(2,1)S(1)} %bitcast.260, bf16[32,256,256]{2,1,0:T(8,128)(2,1)} %get-tuple-element.49.inverse), custom_call_target="tpu_custom_call" | custom-call | tf_op jit(solution)/shard_map/kernel_grad/pallas_call | solution.py:200
  260.3 8.4 %multiply_reduce_fusion.17 = (f32[64]{0:T(128)}, f32[64]{0:T(128)}, f32[64,4096]{1,0:T(8,128)S(1)}) fusion(f32[64,4096]{1,0:T(8,128)S(1)} %copy-done.10, f32[64]{0:T(128)S(1)} %copy-done.67, f32[4096,128]{1,0:T(8,128)S(1)} %bitcast_multiply_fusion.2, f32[64,128]{1,0:T(8,128)S(1)} %copy-done.45), kind=kOutput, calls=%fused_computation.132 | convolution fusion | flops 404225920 | bytes 4227840 | tf_op jit(solution)/shard_map/nc,hc->hn/dot_general | solution.py:557
  269.8 6.4 %convolution_bitcast_fusion.1 = f32[8192]{0:T(1024)S(1)} fusion(f32[4096,128]{1,0:T(8,128)} %copy-done.8, f32[64,4096]{1,0:T(8,128)S(1)} %copy-done.10, f32[64]{0:T(128)S(1)} %copy-done.67), kind=kOutput, calls=%fused_computation.117 | convolution fusion | flops 402915328 | bytes 3178752 | tf_op jit(solution)/shard_map/hn,nc->hc/dot_general | solution.py:556
  279.0 8.9 %all-to-all-done.4 = bf16[8,512,128]{2,1,0:T(8,128)(2,1)} async-done(((bf16[8,512,128]{2,1,0:T(8,128)(2,1)}), bf16[8,512,128]{2,1,0:T(8,128)(2,1)}, u32[]{:S(2)}, u32[]{:S(2)}) %all-to-all-start.4) | async-done | bytes 1048608 | tf_op jit(solution)/shard_map/all_to_all | solution.py:508
  309.4 20.4 %collective-permute-done.7 = bf16[3,8,1024]{2,1,0:T(8,128)(2,1)} collective-permute-done((bf16[3,8,1024]{2,1,0:T(8,128)(2,1)}, bf16[3,8,1024]{2,1,0:T(8,128)(2,1)}, u32[]{:S(2)}, u32[]{:S(2)}) %collective-permute-start.7) | collective-permute-done | bytes 49184 | tf_op jit(solution)/shard_map/ppermute | solution.py:565
  382.2 10.6 %collective-permute-done.27 = bf16[2,128,1024]{2,1,0:T(8,128)(2,1)S(1)} collective-permute-done((bf16[2,128,1024]{2,1,0:T(8,128)(2,1)S(1)}, bf16[2,128,1024]{2,1,0:T(8,128)(2,1)S(1)}, u32[]{:S(2)}, u32[]{:S(2)}) %collective-permute-start.27) | collective-permute-done | bytes 524320 | tf_op jit(solution)/shard_map/ppermute | solution.py:320
  397.9 14.7 %collective-permute-done.12 = f32[224,128]{1,0:T(8,128)S(1)} collective-permute-done((f32[224,128]{1,0:T(8,128)S(1)}, f32[224,128]{1,0:T(8,128)S(1)}, u32[]{:S(2)}, u32[]{:S(2)}) %collective-permute-start.12) | collective-permute-done | bytes 114720 | tf_op jit(solution)/shard_map/ppermute | solution.py:320
  (379 shorter events, 209.5 us)
Async XLA Ops:
  1.5 30.9 %collective-permute-start = (bf16[8,1024]{1,0:T(8,128)(2,1)S(1)}, bf16[8,1024]{1,0:T(8,128)(2,1)S(1)}, u32[]{:S(2)}, u32[]{:S(2)}) collective-permute-start(bf16[8,1024]{1,0:T(8,128)(2,1)S(1)} %slice_bitcast_fusion.4), channel_id=1, source_target_pairs={{0,1},{1,2},{2,3},{3,4},{4,5},{5,6},{6,7},{8,9},{9,10},{10,11},{11... | collective-permute-start | bytes 49160 | tf_op jit(solution)/shard_map/ppermute | solution.py:480
  8.4 35.6 %all-to-all-start = ((f32[8,12,128]{2,1,0:T(8,128)}), f32[8,12,128]{2,1,0:T(8,128)S(1)}, u32[]{:S(2)}, u32[]{:S(2)}) async-start(f32[8,12,128]{2,1,0:T(8,128)} %broadcast_in_dim.16), calls=%async_computation | async-start | bytes 131072 | tf_op jit(solution)/shard_map/all_to_all | solution.py:464
  54.3 31.7 %all-to-all-start.1 = ((bf16[8,512,128]{2,1,0:T(8,128)(2,1)}), bf16[8,512,128]{2,1,0:T(8,128)(2,1)S(1)}, u32[]{:S(2)}, u32[]{:S(2)}) async-start(bf16[8,512,128]{2,1,0:T(8,128)(2,1)} %bitcast.275), calls=%async_computation.1 | async-start | bytes 2097152 | tf_op jit(solution)/shard_map/all_to_all | solution.py:503
  100.9 29.8 %all-to-all-start.2 = ((bf16[8,512,128]{2,1,0:T(8,128)(2,1)}), bf16[8,512,128]{2,1,0:T(8,128)(2,1)}, u32[]{:S(2)}, u32[]{:S(2)}) async-start(bf16[8,512,128]{2,1,0:T(8,128)(2,1)} %bitcast.264), calls=%async_computation.2 | async-start | bytes 2097152 | tf_op jit(solution)/shard_map/all_to_all | solution.py:508
  176.5 33.2 %collective-permute-start.2 = (bf16[1024,2048]{1,0:T(8,128)(2,1)}, bf16[1024,2048]{1,0:T(8,128)(2,1)}, u32[]{:S(2)}, u32[]{:S(2)}) collective-permute-start(bf16[1024,2048]{1,0:T(8,128)(2,1)} %convolution_convert_fusion.1), channel_id=1, source_target_pairs={{0,8},{8,0},{16,24},{24,16},{1,9},{9,1},{17,25},{25,17},{2,10},{10... | collective-permute-start | bytes 12582920 | tf_op jit(solution)/shard_map/ppermute | solution.py:320
  181.0 36.2 %collective-permute-start.1 = (bf16[4096,512]{1,0:T(8,128)(2,1)}, bf16[4096,512]{1,0:T(8,128)(2,1)}, u32[]{:S(2)}, u32[]{:S(2)}) collective-permute-start(bf16[4096,512]{1,0:T(8,128)(2,1)} %convolution_convert_fusion), channel_id=1, source_target_pairs={{0,8},{8,0},{16,24},{24,16},{1,9},{9,1},{17,25},{25,17},{2,10},{10... | collective-permute-start | bytes 12582920 | tf_op jit(solution)/shard_map/ppermute | solution.py:320
  186.1 18.5 %collective-permute-start.3 = (bf16[1024,512]{1,0:T(8,128)(2,1)}, bf16[1024,512]{1,0:T(8,128)(2,1)}, u32[]{:S(2)}, u32[]{:S(2)}) collective-permute-start(bf16[1024,512]{1,0:T(8,128)(2,1)} %convolution_convert_fusion.4), channel_id=1, source_target_pairs={{0,8},{8,0},{16,24},{24,16},{1,9},{9,1},{17,25},{25,17},{2,10},{10... | collective-permute-start | bytes 3145736 | tf_op jit(solution)/shard_map/ppermute | solution.py:320
  189.9 37.2 %all-to-all-start.3 = ((bf16[8,512,128]{2,1,0:T(8,128)(2,1)}), bf16[8,512,128]{2,1,0:T(8,128)(2,1)S(1)}, u32[]{:S(2)}, u32[]{:S(2)}) async-start(bf16[8,512,128]{2,1,0:T(8,128)(2,1)} %bitcast_bitcast_fusion), calls=%async_computation.3 | async-start | bytes 2097152 | tf_op jit(solution)/shard_map/all_to_all | solution.py:503
  227.1 49.1 %collective-permute-start.6 = (bf16[8,128,256]{2,1,0:T(8,128)(2,1)}, bf16[8,128,256]{2,1,0:T(8,128)(2,1)}, u32[]{:S(2)}, u32[]{:S(2)}) collective-permute-start(bf16[8,128,256]{2,1,0:T(8,128)(2,1)} %bitcast.334), channel_id=1, source_target_pairs={{0,16},{8,24},{16,0},{24,8},{1,17},{9,25},{17,1},{25,9},{2,18},{10... | collective-permute-start | bytes 1572872 | tf_op jit(solution)/shard_map/ppermute | solution.py:320
  228.6 65.8 %collective-permute-start.5 = (bf16[4,128,2048]{2,1,0:T(8,128)(2,1)}, bf16[4,128,2048]{2,1,0:T(8,128)(2,1)}, u32[]{:S(2)}, u32[]{:S(2)}) collective-permute-start(bf16[4,128,2048]{2,1,0:T(8,128)(2,1)} %get-tuple-element.56), channel_id=1, source_target_pairs={{0,1},{1,0},{2,3},{3,2},{4,5},{5,4},{6,7},{7,6},{8,9},{9,8},{10,11... | collective-permute-start | bytes 6291464 | tf_op jit(solution)/shard_map/ppermute | solution.py:320
  230.6 58.9 %collective-permute-start.4 = (bf16[8,512,256]{2,1,0:T(8,128)(2,1)}, bf16[8,512,256]{2,1,0:T(8,128)(2,1)}, u32[]{:S(2)}, u32[]{:S(2)}) collective-permute-start(bf16[8,512,256]{2,1,0:T(8,128)(2,1)} %bitcast.333), channel_id=1, source_target_pairs={{0,16},{8,24},{16,0},{24,8},{1,17},{9,25},{17,1},{25,9},{2,18},{10... | collective-permute-start | bytes 6291464 | tf_op jit(solution)/shard_map/ppermute | solution.py:320
  245.9 42.0 %all-to-all-start.4 = ((bf16[8,512,128]{2,1,0:T(8,128)(2,1)}), bf16[8,512,128]{2,1,0:T(8,128)(2,1)}, u32[]{:S(2)}, u32[]{:S(2)}) async-start(bf16[8,512,128]{2,1,0:T(8,128)(2,1)} %bitcast.40), calls=%async_computation.4 | async-start | bytes 2097152 | tf_op jit(solution)/shard_map/all_to_all | solution.py:508
  298.4 64.1 %collective-permute-start.29 = (bf16[4,512,256]{2,1,0:T(8,128)(2,1)}, bf16[4,512,256]{2,1,0:T(8,128)(2,1)}, u32[]{:S(2)}, u32[]{:S(2)}) collective-permute-start(bf16[4,512,256]{2,1,0:T(8,128)(2,1)} %fusion.43), channel_id=1, source_target_pairs={{0,1},{1,0},{2,3},{3,2},{4,5},{5,4},{6,7},{7,6},{8,9},{9,8},{10,11... | collective-permute-start | bytes 3145736 | tf_op jit(solution)/shard_map/ppermute | solution.py:320
  300.1 65.4 %collective-permute-start.26 = (bf16[4,128,1024]{2,1,0:T(8,128)(2,1)}, bf16[4,128,1024]{2,1,0:T(8,128)(2,1)}, u32[]{:S(2)}, u32[]{:S(2)}) collective-permute-start(bf16[4,128,1024]{2,1,0:T(8,128)(2,1)} %get-tuple-element.72), channel_id=1, source_target_pairs={{0,16},{8,24},{16,0},{24,8},{1,17},{9,25},{17,1},{25,9},{2,18},{10... | collective-permute-start | bytes 3145736 | tf_op jit(solution)/shard_map/ppermute | solution.py:320
  300.6 48.4 %collective-permute-start.23 = (bf16[4,128,256]{2,1,0:T(8,128)(2,1)}, bf16[4,128,256]{2,1,0:T(8,128)(2,1)}, u32[]{:S(2)}, u32[]{:S(2)}) collective-permute-start(bf16[4,128,256]{2,1,0:T(8,128)(2,1)} %fusion.90), channel_id=1, source_target_pairs={{0,1},{1,0},{2,3},{3,2},{4,5},{5,4},{6,7},{7,6},{8,9},{9,8},{10,11... | collective-permute-start | bytes 786440 | tf_op jit(solution)/shard_map/ppermute | solution.py:320
  307.9 22.0 %collective-permute-start.7 = (bf16[3,8,1024]{2,1,0:T(8,128)(2,1)}, bf16[3,8,1024]{2,1,0:T(8,128)(2,1)}, u32[]{:S(2)}, u32[]{:S(2)}) collective-permute-start(bf16[3,8,1024]{2,1,0:T(8,128)(2,1)} %pad_maximum_fusion.10), channel_id=1, source_target_pairs={{1,0},{2,1},{3,2},{4,3},{5,4},{6,5},{7,6},{9,8},{10,9},{11,10},{12... | collective-permute-start | bytes 147464 | tf_op jit(solution)/shard_map/ppermute | solution.py:565
  341.9 29.0 %collective-permute-start.9 = (bf16[1024,768]{1,0:T(8,128)(2,1)}, bf16[1024,768]{1,0:T(8,128)(2,1)}, u32[]{:S(2)}, u32[]{:S(2)}) collective-permute-start(bf16[1024,768]{1,0:T(8,128)(2,1)} %convolution_convert_fusion.2), channel_id=1, source_target_pairs={{0,8},{8,0},{16,24},{24,16},{1,9},{9,1},{17,25},{25,17},{2,10},{10... | collective-permute-start | bytes 4718600 | tf_op jit(solution)/shard_map/ppermute | solution.py:320
  344.1 23.9 %collective-permute-start.8 = (bf16[1024,768]{1,0:T(8,128)(2,1)}, bf16[1024,768]{1,0:T(8,128)(2,1)}, u32[]{:S(2)}, u32[]{:S(2)}) collective-permute-start(bf16[1024,768]{1,0:T(8,128)(2,1)} %convolution_convert_fusion.3), channel_id=1, source_target_pairs={{0,8},{8,0},{16,24},{24,16},{1,9},{9,1},{17,25},{25,17},{2,10},{10... | collective-permute-start | bytes 4718600 | tf_op jit(solution)/shard_map/ppermute | solution.py:320
  367.2 25.6 %collective-permute-start.27 = (bf16[2,128,1024]{2,1,0:T(8,128)(2,1)S(1)}, bf16[2,128,1024]{2,1,0:T(8,128)(2,1)S(1)}, u32[]{:S(2)}, u32[]{:S(2)}) collective-permute-start(bf16[2,128,1024]{2,1,0:T(8,128)(2,1)S(1)} %fusion.74), channel_id=1, source_target_pairs={{0,2},{1,3},{2,0},{3,1},{4,6},{5,7},{6,4},{7,5},{8,10},{9,11},{10,... | collective-permute-start | bytes 1572872 | tf_op jit(solution)/shard_map/ppermute | solution.py:320
  379.1 17.9 %collective-permute-start.31 = (bf16[1,512,256]{2,1,0:T(8,128)(2,1)S(1)}, bf16[1,512,256]{2,1,0:T(8,128)(2,1)S(1)}, u32[]{:S(2)}, u32[]{:S(2)}) collective-permute-start(bf16[1,512,256]{2,1,0:T(8,128)(2,1)S(1)} %dynamic-slice_convert_fusion.2), channel_id=1, source_target_pairs={{0,4},{1,5},{2,6},{3,7},{4,0},{5,1},{6,2},{7,3},{8,12},{9,13},{10,... | collective-permute-start | bytes 786440 | tf_op jit(solution)/shard_map/ppermute | solution.py:320
  393.0 22.6 %collective-permute-start.28 = (bf16[1,128,1024]{2,1,0:T(8,128)(2,1)S(1)}, bf16[1,128,1024]{2,1,0:T(8,128)(2,1)S(1)}, u32[]{:S(2)}, u32[]{:S(2)}) collective-permute-start(bf16[1,128,1024]{2,1,0:T(8,128)(2,1)S(1)} %dynamic-slice_convert_fusion.3), channel_id=1, source_target_pairs={{0,4},{1,5},{2,6},{3,7},{4,0},{5,1},{6,2},{7,3},{8,12},{9,13},{10,... | collective-permute-start | bytes 786440 | tf_op jit(solution)/shard_map/ppermute | solution.py:320
  394.4 33.9 %collective-permute-start.15 = (bf16[8,128,384]{2,1,0:T(8,128)(2,1)}, bf16[8,128,384]{2,1,0:T(8,128)(2,1)S(1)}, u32[]{:S(2)}, u32[]{:S(2)}) collective-permute-start(bf16[8,128,384]{2,1,0:T(8,128)(2,1)} %bitcast.71), channel_id=1, source_target_pairs={{0,16},{8,24},{16,0},{24,8},{1,17},{9,25},{17,1},{25,9},{2,18},{10... | collective-permute-start | bytes 2359304 | tf_op jit(solution)/shard_map/ppermute | solution.py:320
  394.9 35.4 %collective-permute-start.19 = (bf16[4,128,768]{2,1,0:T(8,128)(2,1)}, bf16[4,128,768]{2,1,0:T(8,128)(2,1)}, u32[]{:S(2)}, u32[]{:S(2)}) collective-permute-start(bf16[4,128,768]{2,1,0:T(8,128)(2,1)} %get-tuple-element.68), channel_id=1, source_target_pairs={{0,1},{1,0},{2,3},{3,2},{4,5},{5,4},{6,7},{7,6},{8,9},{9,8},{10,11... | collective-permute-start | bytes 2359304 | tf_op jit(solution)/shard_map/ppermute | solution.py:320
  395.0 17.7 %collective-permute-start.12 = (f32[224,128]{1,0:T(8,128)S(1)}, f32[224,128]{1,0:T(8,128)S(1)}, u32[]{:S(2)}, u32[]{:S(2)}) collective-permute-start(f32[224,128]{1,0:T(8,128)S(1)} %slice.422), channel_id=1, source_target_pairs={{0,1},{1,0},{2,3},{3,2},{4,5},{5,4},{6,7},{7,6},{8,9},{9,8},{10,11... | collective-permute-start | bytes 344072 | tf_op jit(solution)/shard_map/ppermute | solution.py:320
  (100 other events, 1115.4 us)

commit v2 on v1

v2 whole, which is shorter than its diff:
```python
import functools
import math

import jax
import jax.numpy as jnp
import numpy as np
from jax import lax
from jax.experimental import pallas as pl
from jax.experimental.pallas import tpu as pltpu
from jax.sharding import PartitionSpec as P

EMB = 33
HIGH = lax.Precision.HIGHEST
EPSILON = 1e-05
BLOCK = 128
LANES = 128
ROWS = 16
CHUNK = 64
GRANT = 60 << 20
COST = 8
F32 = jnp.float32
BF16 = jnp.bfloat16


def times_root(re, im, num, den):
    num = num % den
    if num == 0:
        return re, im
    if 4 * num == den:
        return -im, re
    if 2 * num == den:
        return -re, -im
    if 4 * num == 3 * den:
        return im, -re
    angle = 2.0 * math.pi * num / den
    cos, sin = math.cos(angle), math.sin(angle)
    if abs(abs(cos) - abs(sin)) < 1e-12:
        sc, ss = (1.0 if cos > 0 else -1.0), (1.0 if sin > 0 else -1.0)
        root = abs(cos)
        return root * (sc * re - ss * im), root * (sc * im + ss * re)
    return re * cos - im * sin, im * cos + re * sin


def small_fft(re, im, sign):
    count = len(re)
    if count == 1:
        return re, im
    if count == 2:
        return [re[0] + re[1], re[0] - re[1]], [im[0] + im[1], im[0] - im[1]]
    even_re, even_im = small_fft(re[0::2], im[0::2], sign)
    odd_re, odd_im = small_fft(re[1::2], im[1::2], sign)
    low_re, low_im, top_re, top_im = [], [], [], []
    for k in range(count // 2):
        tr, ti = times_root(odd_re[k], odd_im[k], sign * k, count)
        low_re.append(even_re[k] + tr)
        low_im.append(even_im[k] + ti)
        top_re.append(even_re[k] - tr)
        top_im.append(even_im[k] - ti)
    return low_re + top_re, low_im + top_im


def blocks_forward(source, target, count):
    def body(step, carry):
        row = pl.multiple_of(step * ROWS, ROWS)
        re, im = [], []
        for a in range(count):
            value = source[a, pl.ds(row, ROWS), :].astype(F32)
            angle = 2.0 * math.pi * a / (4 * count)
            re.append(value * math.cos(angle))
            im.append(value * math.sin(angle))
        re, im = small_fft(re, im, -1)
        for k in range(count):
            target[k, pl.ds(row, ROWS), :] = re[k].astype(BF16)
            target[k, pl.ds(BLOCK + row, ROWS), :] = im[k].astype(BF16)
        return carry

    lax.fori_loop(0, BLOCK // ROWS, body, 0)


def blocks_inverse(source, emit, count):
    def body(step, carry):
        row = pl.multiple_of(step * ROWS, ROWS)
        re = [source[k, pl.ds(row, ROWS), :] for k in range(count)]
        im = [source[k, pl.ds(BLOCK + row, ROWS), :] for k in range(count)]
        re, im = small_fft(re, im, 1)
        for a in range(count):
            angle = 2.0 * math.pi * a / (4 * count)
            emit(a, row, re[a] * math.cos(angle) + im[a] * math.sin(angle))
        return carry

    lax.fori_loop(0, BLOCK // ROWS, body, 0)


def cost(flops, bytes_accessed):
    return pl.CostEstimate(flops=flops // COST, bytes_accessed=bytes_accessed // COST, transcendentals=0)


def mxu(left, right):
    return jnp.dot(left, right, preferred_element_type=F32)

def mxu_nt(left, right):
    return lax.dot_general(left, right, (((1,), (1,)), ((), ())), preferred_element_type=F32)

def mxu_tn(left, right):
    return lax.dot_general(left, right, (((0,), (0,)), ((), ())), preferred_element_type=F32)

def rows_loop(total, chunk, body, unroll=1):
    def step(i, carry):
        return body(pl.ds(pl.multiple_of(i * chunk, chunk), chunk), carry)
    return lambda init: lax.fori_loop(0, total // chunk, step, init, unroll=unroll)

def fold8(v):
    return jnp.sum(v.reshape(v.shape[0] // 8, 8, v.shape[1]), axis=0)


def table_kernel(alpha_cos, alpha_sin, beta_cos, beta_sin, forward, inverse, *, scale):
    cb, sb = beta_cos[...], beta_sin[...]
    for i in range(forward.shape[0]):
        ca, sa = alpha_cos[i], alpha_sin[i]
        cos = ca * cb - sa * sb
        sin = sa * cb + ca * sb
        low_cos, low_sin = cos.astype(BF16), sin.astype(BF16)
        forward[i, :BLOCK, :BLOCK] = low_cos
        forward[i, :BLOCK, BLOCK:] = low_sin
        forward[i, BLOCK:, :BLOCK] = -low_sin
        forward[i, BLOCK:, BLOCK:] = low_cos
        low_cos, low_sin = (cos.T * scale).astype(BF16), (sin.T * scale).astype(BF16)
        inverse[i, :BLOCK, :BLOCK] = low_cos
        inverse[i, :BLOCK, BLOCK:] = -low_sin
        inverse[i, BLOCK:, :BLOCK] = low_sin
        inverse[i, BLOCK:, BLOCK:] = low_cos


def make_tables(length):
    count = length // BLOCK
    alpha = 2.0 * np.pi * np.arange(BLOCK)[None, :] * (np.arange(count)[:, None] - 0.25) / length
    beta = 2.0 * np.pi * ((np.arange(BLOCK)[:, None] * np.arange(BLOCK)[None, :]) % BLOCK) / BLOCK
    alpha = alpha[:, None, :]
    consts = [jnp.asarray(f(v), F32) for v in (alpha, beta) for f in (np.cos, np.sin)]
    each = math.gcd(count, 4)
    row = pl.BlockSpec((each, 1, BLOCK), lambda i: (i, 0, 0))
    flat = pl.BlockSpec((BLOCK, BLOCK), lambda i: (0, 0))
    out = pl.BlockSpec((each, 2 * BLOCK, 2 * BLOCK), lambda i: (i, 0, 0))
    shape = jax.ShapeDtypeStruct((count, 2 * BLOCK, 2 * BLOCK), BF16)
    return pl.pallas_call(
        functools.partial(table_kernel, scale=1.0 / length),
        grid=(count // each,),
        in_specs=[row, row, flat, flat],
        out_specs=[out, out],
        out_shape=[shape, shape],
        cost_estimate=cost(16 * count * BLOCK * BLOCK, 8 << 20),
        name="tables",
    )(*consts)


def split_spec(value):
    return value[:BLOCK], value[BLOCK:]


def turn_back(prod, inverse, back):
    def body(k, carry):
        back[k] = mxu(inverse[k], prod[k])
        return carry

    lax.fori_loop(0, prod.shape[0], body, 0, unroll=8)


def spectrum_kernel(signal, forward, spectrum, mid):
    (signal, have_signal), (forward, have_forward) = signal, forward
    count = signal.shape[0]
    have_signal()
    blocks_forward(signal, mid, count)
    have_forward()

    def body(k, carry):
        spectrum[k] = mxu(forward[k], mid[k]).astype(BF16)
        return carry

    lax.fori_loop(0, count, body, 0, unroll=8)


def conv_kernel(signal, kernel_spec, bias, forward, inverse, result, spectrum, mid, prod, back, *, conjugate):
    (signal, have_signal), (kernel_spec, have_spec), (bias, have_bias) = signal, kernel_spec, bias
    (forward, have_forward), (inverse, have_inverse) = forward, inverse
    count = signal.shape[0]
    have_signal()
    blocks_forward(signal, mid, count)
    have_spec()
    have_bias()
    have_forward()

    def body(k, carry):
        spec = mxu(forward[k], mid[k])
        spectrum[k] = spec.astype(BF16)
        a_re, a_im = split_spec(spec)
        b_re, b_im = split_spec(kernel_spec[k].astype(F32))
        if conjugate:
            b_im = -b_im
        prod[k, :BLOCK, :] = (a_re * b_re - a_im * b_im).astype(BF16)
        prod[k, BLOCK:, :] = (a_re * b_im + a_im * b_re).astype(BF16)
        return carry

    lax.fori_loop(0, count, body, 0, unroll=8)
    have_inverse()
    turn_back(prod, inverse, back)
    gain = bias[...]
    devices, rows, _ = result.shape
    per = count // devices
    size = per * BLOCK

    def emit(a, row, value):
        direct = signal[a, pl.ds(row, ROWS), :].astype(F32) * gain
        result[a // per, pl.ds((a % per) * BLOCK + row, ROWS), :] = (value + direct).astype(result.dtype)

    blocks_inverse(back, emit, count)
    if rows > size:
        for j in range(devices - 1):
            result[j, size:, :] = result[j + 1, : rows - size, :]
        result[devices - 1, size:, :] = jnp.zeros((rows - size, result.shape[2]), result.dtype)


def filter_grad_kernel(
    grad_spec, signal_spec, grad, signal, inverse, window, hidden, slope, hidden_pre, features, filter_out,
    out_grad, in_grad, sums, bias_grad, prod, back, raw,
):
    (grad_spec, have_grad_spec), (signal_spec, have_signal_spec) = grad_spec, signal_spec
    count = grad_spec.shape[0]
    have_grad_spec()
    have_signal_spec()

    def body(k, carry):
        a_re, a_im = split_spec(grad_spec[k].astype(F32))
        b_re, b_im = split_spec(signal_spec[k].astype(F32))
        prod[k, :BLOCK, :] = (a_re * b_re + a_im * b_im).astype(BF16)
        prod[k, BLOCK:, :] = (a_im * b_re - a_re * b_im).astype(BF16)
        return carry

    lax.fori_loop(0, count, body, 0, unroll=2)
    for _, wait in (grad, signal, inverse, window, hidden, slope, hidden_pre, features, filter_out):
        wait()
    grad, signal, inverse, window, hidden, slope, hidden_pre, features, filter_out = (
        v[0] for v in (grad, signal, inverse, window, hidden, slope, hidden_pre, features, filter_out)
    )
    turn_back(prod, inverse, back)

    def emit(a, row, value):
        at = pl.ds(a * BLOCK + row, ROWS)
        raw[at, :] = (value * window[at, :]).astype(BF16)

    blocks_inverse(back, emit, count)

    def total(a, acc):
        return acc + fold8(grad[a].astype(F32) * signal[a].astype(F32))

    acc = lax.fori_loop(0, count, total, jnp.zeros((8, grad.shape[-1]), F32))
    bias_grad[...] = jnp.sum(acc, axis=0, keepdims=True)
    out_grad[...] = mxu(hidden[...], raw[...])
    turned = mxu_nt(filter_out[...], raw[...]) * slope[...]
    sums[...] = jnp.concatenate(
        [jnp.sum(turned * hidden_pre[...], axis=1, keepdims=True), jnp.sum(turned, axis=1, keepdims=True)], axis=1
    )
    in_grad[...] = mxu_nt(features[...], turned.astype(BF16))


def vmem_call(kernel, outs, scratch, args, name):
    count = len(args)

    def body(*refs):
        ins, rest = refs[:count], refs[count:]
        results, local = rest[: len(outs)], rest[len(outs) : len(outs) + len(scratch)]
        bufs, sems = rest[len(outs) + len(scratch) : -1], rest[-1]
        copies = [pltpu.make_async_copy(src, dst, sems.at[i]) for i, (src, dst) in enumerate(zip(ins, bufs))]
        for copy in copies:
            copy.start()
        kernel(*[(buf, copy.wait) for buf, copy in zip(bufs, copies)], *results, *local)

    scratch = list(scratch)
    held = [pltpu.VMEM(a.shape, a.dtype) for a in args]
    return pl.pallas_call(
        body,
        in_specs=[pl.BlockSpec(memory_space=pl.ANY)] * count,
        out_specs=[pl.BlockSpec(o.shape, lambda n=len(o.shape): (0,) * n) for o in outs],
        out_shape=outs,
        scratch_shapes=scratch + held + [pltpu.SemaphoreType.DMA((count,))],
        cost_estimate=cost(4 << 30, 16 << 20),
        compiler_params=pltpu.CompilerParams(vmem_limit_bytes=GRANT),
        name=name,
    )(*args)


class FastMixer:
    def __init__(self, length, channels, devices, tables):
        self.count = length // BLOCK
        self.channels = channels
        self.devices = devices
        self.forward, self.inverse = tables
        self.mid = pltpu.VMEM((self.count, 2 * BLOCK, channels), BF16)
        self.back = pltpu.VMEM((self.count, 2 * BLOCK, channels), F32)
        self.spec = jax.ShapeDtypeStruct((self.count, 2 * BLOCK, channels), BF16)

    def blocked(self, value):
        return value.reshape(self.count, BLOCK, self.channels)

    def spectrum(self, signal):
        args = (self.blocked(signal), self.forward)
        return vmem_call(spectrum_kernel, [self.spec], [self.mid], args, "spectrum")[0]

    def convolve(self, signal, kernel_spec, bias, conjugate, extra):
        rows = self.count * BLOCK // self.devices + extra
        out = jax.ShapeDtypeStruct((self.devices, rows, self.channels), BF16)
        return vmem_call(
            functools.partial(conv_kernel, conjugate=conjugate),
            [out, self.spec],
            [self.mid, self.mid, self.back],
            (self.blocked(signal), kernel_spec, bias[None, :], self.forward, self.inverse),
            "correlate" if conjugate else "convolve",
        )

    def filter_grad(self, grad_spec, signal_spec, grad, signal, filt):
        features, hidden_pre, phase, hidden, window, filter_out = filt
        units = hidden.shape[0]
        outs = [
            jax.ShapeDtypeStruct((units, self.channels), F32),
            jax.ShapeDtypeStruct((48, units), F32),
            jax.ShapeDtypeStruct((units, 2), F32),
            jax.ShapeDtypeStruct((1, self.channels), F32),
        ]
        padded = jnp.pad(features.astype(BF16), ((0, 48 - EMB), (0, 0)))
        raw = pltpu.VMEM((self.count * BLOCK, self.channels), BF16)
        out_grad, in_grad, sums, bias_grad = vmem_call(
            filter_grad_kernel,
            outs,
            [self.mid, self.back, raw],
            (grad_spec, signal_spec, self.blocked(grad), self.blocked(signal), self.inverse, window)
            + (hidden.astype(BF16), jnp.cos(phase), hidden_pre, padded, filter_out.astype(BF16)),
            "filter_grad",
        )
        return out_grad, in_grad[:EMB], sums.T, bias_grad[0]


class PlainMixer:
    def __init__(self, length, channels, devices, tables):
        self.length = length
        self.devices = devices
        self.channels = channels
        full = 2 * length
        p = 2
        while p * p * 2 <= full and full % (p * 2) == 0:
            p = p * 2
        q = full // p
        self.p, self.q = p, q
        ip, iq = jnp.arange(p, dtype=jnp.int32), jnp.arange(q, dtype=jnp.int32)
        tp = 2.0 * math.pi * (ip[:, None] * ip[None, :] % p).astype(F32) / p
        tq = 2.0 * math.pi * (iq[:, None] * iq[None, :] % q).astype(F32) / q
        tt = 2.0 * math.pi * (ip[:, None] * iq[None, :] % full).astype(F32) / full
        self.cp, self.sp, self.cq, self.sq = jnp.cos(tp), jnp.sin(tp), jnp.cos(tq), jnp.sin(tq)
        self.ct, self.st = jnp.cos(tt), jnp.sin(tt)

    def spectrum(self, signal):
        half = self.p // 2
        x = signal.astype(F32).T.reshape(self.channels, half, self.q)
        ein = functools.partial(jnp.einsum, precision=HIGH)
        re = ein("kn,cnq->ckq", self.cp[:, :half], x)
        im = -ein("kn,cnq->ckq", self.sp[:, :half], x)
        re, im = re * self.ct + im * self.st, im * self.ct - re * self.st
        return (
            ein("ckn,nm->ckm", re, self.cq) + ein("ckn,nm->ckm", im, self.sq),
            ein("ckn,nm->ckm", im, self.cq) - ein("ckn,nm->ckm", re, self.sq),
        )

    def back(self, re, im):
        half = self.p // 2
        ein = functools.partial(jnp.einsum, precision=HIGH)
        br = ein("ckm,nm->ckn", re, self.cq) - ein("ckm,nm->ckn", im, self.sq)
        bi = ein("ckm,nm->ckn", im, self.cq) + ein("ckm,nm->ckn", re, self.sq)
        br, bi = br * self.ct - bi * self.st, bi * self.ct + br * self.st
        out = ein("nk,ckq->cnq", self.cp[:half], br) - ein("nk,ckq->cnq", self.sp[:half], bi)
        return (out.reshape(self.channels, self.length) / (2 * self.length)).T

    def convolve(self, signal, kernel_spec, bias, conjugate, extra):
        a_re, a_im = self.spectrum(signal)
        b_re, b_im = kernel_spec
        if conjugate:
            b_im = -b_im
        out = self.back(a_re * b_re - a_im * b_im, a_re * b_im + a_im * b_re)
        out = out + signal.astype(F32) * bias[None, :]
        out = jnp.pad(out.astype(BF16), ((0, extra), (0, 0)))
        rows = self.length // self.devices
        parts = [out[j * rows : (j + 1) * rows + extra] for j in range(self.devices)]
        return jnp.stack(parts), (a_re, a_im)

    def filter_grad(self, grad_spec, signal_spec, grad, signal, filt):
        features, hidden_pre, phase, hidden, window, filter_out = filt
        a_re, a_im = grad_spec
        b_re, b_im = signal_spec
        raw = self.back(a_re * b_re + a_im * b_im, a_im * b_re - a_re * b_im) * window
        out_grad = jnp.einsum("hn,nc->hc", hidden, raw, precision=HIGH)
        turned = jnp.einsum("nc,hc->hn", raw, filter_out, precision=HIGH) * jnp.cos(phase)
        in_grad = jnp.einsum("en,hn->eh", features, turned, precision=HIGH)
        sums = jnp.stack([jnp.sum(turned * hidden_pre, axis=1), jnp.sum(turned, axis=1)])
        return out_grad, in_grad, sums, jnp.sum(grad.astype(F32) * signal.astype(F32), axis=0)


def position_features(length):
    steps = jnp.arange(length, dtype=F32)
    scaled = steps / (length - 1)
    angles = 2.0 * math.pi * steps / length
    bands = (EMB - 1) // 2
    freqs = 0.0001 + jnp.arange(bands, dtype=F32) * (bands - 1 - 0.0001) / (bands - 1)
    phase = freqs[:, None] * angles[None, :]
    return jnp.concatenate([scaled[None, :], jnp.cos(phase), -jnp.sin(phase)], axis=0)


def swap(value, axis, bit):
    size = lax.axis_size(axis)
    return lax.ppermute(value, axis, [(i, i ^ bit) for i in range(size)])


def pick(value, index, axis):
    return lax.dynamic_index_in_dim(value, index, axis, keepdims=False)


def add(left, right):
    return (left.astype(F32) + right.astype(F32)).astype(BF16)


def seq_bits():
    bit, bits = 1, []
    while bit < lax.axis_size("seq"):
        bits.append(bit)
        bit *= 2
    return bits


def block_order(bits):
    order = [0]
    for bit in reversed(bits):
        order = [r ^ bit for r in order] + order
    return jnp.bitwise_xor(lax.axis_index("seq"), jnp.array(order, jnp.int32))


def chip_units(right, unit, which):
    per = right.shape[0] * right.shape[2] // (4 * unit)
    me = lax.axis_index("dp")
    return jnp.concatenate([jnp.bitwise_xor(me, w) * per + jnp.arange(per, dtype=jnp.int32) for w in which])


def halve(kept, got):
    half = kept.shape[0] // 2
    return add(kept[:half], got[:half]), add(kept[half:], got[half:])


def last(kept, got):
    return (kept.astype(F32) + got.astype(F32))[0]


def tie(*values):
    return lax.optimization_barrier(values)


def pack(parts):
    flat = jnp.concatenate([p.reshape(-1) for p in parts])
    short = -flat.shape[0] % 1024
    return jnp.pad(flat, (0, short)).reshape(-1, 128)


def unpack(packed, like):
    flat = packed.reshape(-1)
    out, place = [], 0
    for p in like:
        out.append(flat[place : place + p.size].reshape(p.shape))
        place += p.size
    return out


def back_act_kernel(dy, down, out, dy_sum):
    out[...] = mxu_nt(dy[...], down[...]).astype(BF16)
    @pl.when(pl.program_id(0) == 0)
    def _():
        acc = rows_loop(dy.shape[0], 16, lambda r, c: c + fold8(dy[r, :].astype(F32)))(jnp.zeros((8, dy.shape[1]), F32))
        dy_sum[...] = jnp.sum(acc, axis=0, keepdims=True)

def back_act(dy, down, block=512):
    rows, width = dy.shape
    ff = down.shape[0]
    return pl.pallas_call(
        back_act_kernel, grid=(ff // block,),
        in_specs=[pl.BlockSpec((rows, width), lambda f: (0, 0)), pl.BlockSpec((block, width), lambda f: (f, 0))],
        out_specs=[pl.BlockSpec((rows, block), lambda f: (0, f)), pl.BlockSpec((1, width), lambda f: (0, 0))],
        out_shape=[jax.ShapeDtypeStruct((rows, ff), BF16), jax.ShapeDtypeStruct((1, width), F32)],
        cost_estimate=cost(2 * rows * width * ff, 13 << 20),
        compiler_params=pltpu.CompilerParams(vmem_limit_bytes=GRANT), name="back_act")(dy, down)

def block_out_kernel(act, down, resid, bias, out, acc):
    f = pl.program_id(0)
    part = mxu(act[...], down[...])
    @pl.when(f == 0)
    def _():
        acc[...] = part + bias[...]
    @pl.when((f > 0) & (f < pl.num_programs(0) - 1))
    def _():
        acc[...] += part
    @pl.when(f == pl.num_programs(0) - 1)
    def _():
        out[...] = (acc[...] + part + resid[...].astype(F32)).astype(BF16)

def block_out(act, down, resid, bias, block=1024):
    rows, ff = act.shape
    width = down.shape[1]
    return pl.pallas_call(
        block_out_kernel, grid=(ff // block,),
        in_specs=[pl.BlockSpec((rows, block), lambda f: (0, f)), pl.BlockSpec((block, width), lambda f: (f, 0)),
                  pl.BlockSpec((rows, width), lambda f: (0, 0)), pl.BlockSpec((1, width), lambda f: (0, 0))],
        out_specs=pl.BlockSpec((rows, width), lambda f: (0, 0)),
        out_shape=jax.ShapeDtypeStruct((rows, width), BF16),
        scratch_shapes=[pltpu.VMEM((rows, width), F32)],
        cost_estimate=cost(2 * rows * width * ff, 15 << 20),
        compiler_params=pltpu.CompilerParams(vmem_limit_bytes=GRANT), name="block_out")(act, down, resid, bias)

C0 = math.sqrt(2.0 / math.pi)
C1 = C0 * 0.044715

def middle_kernel(conv, gate, x, dy, ga, wout, bout, gain, bias, up, up_bias,
                  act, gup, gup_sum, resid, normed, mixed, gattn, gconv, ggate, sums,
                  d2, normal, scale):
    f = pl.program_id(0)
    last = pl.num_programs(0) - 1
    rows, width = x.shape
    nb = width // LANES

    @pl.when((f == 0))
    def _():
        def mix(r, c):
            for j in range(nb):
                lanes = slice(j * LANES, (j + 1) * LANES)
                mixed[r, lanes] = (conv[j, r, :].astype(F32) * gate[r, lanes].astype(F32)).astype(BF16)
            return c
        rows_loop(rows, CHUNK, mix)(0)
        for h in range(2):
            half = slice(h * rows // 2, (h + 1) * rows // 2)
            d2[half, :] = mxu(mixed[half, :], wout[...])

        def norm(r, c):
            v = x[r, :].astype(F32) + d2[r, :] + bout[...]
            resid[r, :] = v.astype(BF16)
            mean = jnp.mean(v, axis=-1, keepdims=True)
            v = v - mean
            s = lax.rsqrt(jnp.mean(v * v, axis=-1, keepdims=True) + EPSILON)
            n = v * s
            scale[r, :] = s
            normal[r, :] = n
            normed[r, :] = (n * gain[...] + bias[...]).astype(BF16)
            return c
        rows_loop(rows, CHUNK, norm)(0)

    total = jnp.zeros((8, up.shape[1]), F32)
    pieces = 1
    for h in range(pieces):
        part = slice(h * rows // pieces, (h + 1) * rows // pieces)
        v = mxu(normed[part, :], up[...]) + up_bias[...]
        v2 = v * v
        t = jnp.tanh(v * (C0 + C1 * v2))
        half = 0.5 + 0.5 * t
        act[part, :] = (v * half).astype(BF16)
        slope = half + (0.5 * v) * (1.0 - t * t) * (C0 + (3.0 * C1) * v2)
        g = (ga[part, :].astype(F32) * slope).astype(BF16)
        gup[part, :] = g
        total += fold8(g.astype(F32))
        back = mxu_nt(g, up[...])
        @pl.when(f == 0)
        def _():
            d2[part, :] = back
        @pl.when(f > 0)
        def _():
            d2[part, :] += back
    gup_sum[...] = jnp.sum(total, axis=0, keepdims=True)

    @pl.when((f == last))
    def _():
        def norm_back(r, carry):
            a, b, o = carry
            d, n = d2[r, :], normal[r, :]
            a += fold8(d * n)
            b += fold8(d)
            e = d * gain[...]
            m1 = jnp.mean(e, axis=-1, keepdims=True)
            m2 = jnp.mean(e * n, axis=-1, keepdims=True)
            g = dy[r, :].astype(F32) + (e - m1 - n * m2) * scale[r, :]
            low = g.astype(BF16)
            gattn[r, :] = low
            o += fold8(low.astype(F32))
            return a, b, o
        zero = jnp.zeros((8, width), F32)
        a, b, o = rows_loop(rows, CHUNK, norm_back)((zero, zero, zero))
        sums[0:1, :] = jnp.sum(a, axis=0, keepdims=True)
        sums[1:2, :] = jnp.sum(b, axis=0, keepdims=True)
        sums[2:3, :] = jnp.sum(o, axis=0, keepdims=True)
        for h in range(2):
            half = slice(h * rows // 2, (h + 1) * rows // 2)
            d2[half, :] = mxu_nt(gattn[half, :], wout[...])
        def out(r, c):
            for j in range(nb):
                lanes = slice(j * LANES, (j + 1) * LANES)
                g = d2[r, lanes]
                gconv[j, r, :] = (g * gate[r, lanes].astype(F32)).astype(BF16)
                ggate[r, lanes] = (g * conv[j, r, :].astype(F32)).astype(BF16)
            return c
        rows_loop(rows, CHUNK, out)(0)

def middle(conv, gate, x, dy, ga, wout, bout, gain, bias, up, up_bias, block=512):
    rows, width = x.shape
    ff = up.shape[1]
    nb = width // LANES
    whole = lambda *s: pl.BlockSpec(s, lambda f: (0,) * len(s))
    flat = whole(rows, width)
    row = whole(1, width)
    cols = pl.BlockSpec((rows, block), lambda f: (0, f))
    bar = pl.BlockSpec((1, block), lambda f: (0, f))
    sd = jax.ShapeDtypeStruct
    return pl.pallas_call(
        middle_kernel, grid=(ff // block,),
        in_specs=[whole(nb, rows, LANES), flat, flat, flat, cols, whole(width, width), row, row, row,
                  pl.BlockSpec((width, block), lambda f: (0, f)), bar],
        out_specs=[cols, cols, bar, flat, flat, flat, flat, whole(nb, rows, LANES), flat, whole(3, width)],
        out_shape=[sd((rows, ff), BF16), sd((rows, ff), BF16), sd((1, ff), F32), sd((rows, width), BF16),
                   sd((rows, width), BF16), sd((rows, width), BF16), sd((rows, width), BF16),
                   sd((nb, rows, LANES), BF16), sd((rows, width), BF16), sd((3, width), F32)],
        scratch_shapes=[pltpu.VMEM((rows, width), F32), pltpu.VMEM((rows, width), F32), pltpu.VMEM((rows, 1), F32)],
        cost_estimate=cost(4 * rows * width * (ff + width), 34 << 20),
        compiler_params=pltpu.CompilerParams(vmem_limit_bytes=GRANT), name="middle")(
            conv, gate, x, dy, ga, wout, bout, gain, bias, up, up_bias)

PRE = 16

def enter_kernel(first, x, before, gain, bias, w0, w1, w2, b0, b1, b2, taps, inner, gate, proj, normed_out, normed, shifted):
    rows, width = x.shape
    def norm(src, base):
        def body(r, c):
            v = src[r, :].astype(F32)
            v = v - jnp.mean(v, axis=-1, keepdims=True)
            s = lax.rsqrt(jnp.mean(v * v, axis=-1, keepdims=True) + EPSILON)
            normed[pl.ds(r.start + base, r.size), :] = (v * s * gain[...] + bias[...]).astype(BF16)
            return c
        return body
    @pl.when(pl.program_id(0) == 0)
    def _():
        rows_loop(PRE, 16, norm(before, 0))(0)
        rows_loop(rows, CHUNK, norm(x, PRE))(0)
        normed_out[...] = normed[PRE:, :]
    cb = w0.shape[1]
    short = []
    keep = jnp.where(first[0] == 0, 0.0, 1.0)
    for k, (w, b) in enumerate(((w0, b0), (w1, b1), (w2, b2))):
        p = (mxu(normed[...], w[...]) + b[...]).astype(BF16)
        proj[k, PRE:, :] = p[PRE:]
        proj[k, :PRE, :] = (p[:PRE].astype(F32) * keep).astype(BF16)
        shifted[k, PRE:, :] = p[PRE:].astype(F32)
        shifted[k, :PRE, :] = p[:PRE].astype(F32) * keep
    def gates(r, c):
        s = []
        for k in range(3):
            p = shifted[k, pl.ds(r.start + (PRE - 8), r.size + 8), :]
            v = taps[9 + k : 10 + k, :] + sum(
                taps[3 * j + k : 3 * j + k + 1, :] * p[6 + j : 6 + j + r.size] for j in range(3))
            s.append(v)
        gate[r, :] = s[0].astype(BF16)
        v = (s[1] * s[2]).astype(BF16)
        for j in range(cb // LANES):
            inner[j, r, :] = v[:, j * LANES : (j + 1) * LANES]
        return c
    rows_loop(rows, CHUNK, gates)(0)

def enter(first, x, before, gain, bias, weight, in_bias, taps, block=256):
    rows, width = x.shape
    nb = width // LANES
    steps = width // block
    whole = lambda *s: pl.BlockSpec(s, lambda c: (0,) * len(s))
    wspec = lambda k: pl.BlockSpec((width, block), lambda c, k=k: (0, k * steps + c))
    bspec = lambda k: pl.BlockSpec((1, block), lambda c, k=k: (0, k * steps + c))
    sd = jax.ShapeDtypeStruct
    return pl.pallas_call(
        enter_kernel, grid=(steps,),
        in_specs=[pl.BlockSpec(memory_space=pltpu.SMEM), whole(rows, width), whole(PRE, width), whole(1, width), whole(1, width),
                  wspec(0), wspec(1), wspec(2), bspec(0), bspec(1), bspec(2), pl.BlockSpec((12, block), lambda c: (0, c))],
        out_specs=[pl.BlockSpec((block // LANES, rows, LANES), lambda c: (c, 0, 0)), pl.BlockSpec((rows, block), lambda c: (0, c)),
                   pl.BlockSpec((3, PRE + rows, block), lambda c: (0, 0, c)), whole(rows, width)],
        out_shape=[sd((nb, rows, LANES), BF16), sd((rows, width), BF16), sd((3, PRE + rows, width), BF16), sd((rows, width), BF16)],
        scratch_shapes=[pltpu.VMEM((PRE + rows, width), BF16), pltpu.VMEM((3, PRE + rows, block), F32)],
        cost_estimate=cost(6 * rows * width * width, 14 << 20),
        compiler_params=pltpu.CompilerParams(vmem_limit_bytes=GRANT), name="enter")(
            first, x, before, gain, bias, weight, weight, weight, in_bias, in_bias, in_bias, taps)

POST = 16

def leave_kernel(ginner, ggate, ggate_after, proj, proj_after, taps, gproj, sums, pbuf, gbuf):
    rows = ggate.shape[0]
    cb = ggate.shape[1]
    for k in range(3):
        pbuf[k, : PRE + rows, :] = proj[k].astype(F32)
        pbuf[k, PRE + rows :, :] = proj_after[k].astype(F32)
    tap = lambda j, k: taps[3 * j + k : 3 * j + k + 1, :]

    def lags(k, start, size):
        p = pbuf[k, pl.ds(start + (PRE - 8), size + 8), :]
        return [p[6 + j : 6 + j + size] for j in range(3)]

    def grads(start, size, g0):
        gi = jnp.concatenate([ginner[j, pl.ds(start, size), :] for j in range(cb // LANES)], axis=1).astype(F32)
        p1 = lags(1, start, size)
        p2 = lags(2, start, size)
        s1 = taps[10:11, :] + sum(tap(j, 1) * p1[j] for j in range(3))
        s2 = taps[11:12, :] + sum(tap(j, 2) * p2[j] for j in range(3))
        return (g0, gi * s2, gi * s1), p1, p2

    def first(r, carry):
        g, p1, p2 = grads(r.start, r.size, ggate[r, :].astype(F32))
        p0 = lags(0, r.start, r.size)
        out = []
        for k in range(3):
            gbuf[k, r, :] = g[k]
        for j in range(3):
            for k, p in enumerate((p0, p1, p2)):
                out.append(carry[3 * j + k] + fold8(g[k] * p[j]))
        for k in range(3):
            out.append(carry[9 + k] + fold8(g[k]))
        return tuple(out)

    acc = rows_loop(rows, CHUNK, first)(tuple(jnp.zeros((8, cb), F32) for _ in range(12)))
    for i in range(12):
        sums[i : i + 1, :] = jnp.sum(acc[i], axis=0, keepdims=True)
    g, _, _ = grads(rows, POST, ggate_after[...].astype(F32))
    for k in range(3):
        gbuf[k, rows:, :] = g[k]

    def second(r, carry):
        out = []
        for k in range(3):
            g = gbuf[k, pl.ds(r.start, r.size + 8), :]
            v = sum(tap(j, k) * g[2 - j : 2 - j + r.size] for j in range(3)).astype(BF16)
            gproj[k, r, :] = v
            out.append(carry[k] + fold8(v.astype(F32)))
        return tuple(out)

    acc = rows_loop(rows, CHUNK, second)(tuple(jnp.zeros((8, cb), F32) for _ in range(3)))
    for i in range(3):
        sums[12 + i : 13 + i, :] = jnp.sum(acc[i], axis=0, keepdims=True)
    sums[15:16, :] = jnp.zeros((1, cb), F32)

def leave(ginner, ggate, ggate_after, proj, proj_after, taps, block=256):
    rows, width = ggate.shape
    steps = width // block
    sd = jax.ShapeDtypeStruct
    return pl.pallas_call(
        leave_kernel, grid=(steps,),
        in_specs=[pl.BlockSpec((block // LANES, rows + POST, LANES), lambda c: (c, 0, 0)),
                  pl.BlockSpec((rows, block), lambda c: (0, c)), pl.BlockSpec((POST, block), lambda c: (0, c)),
                  pl.BlockSpec((3, PRE + rows, block), lambda c: (0, 0, c)), pl.BlockSpec((3, POST, block), lambda c: (0, 0, c)),
                  pl.BlockSpec((12, block), lambda c: (0, c))],
        out_specs=[pl.BlockSpec((3, rows, block), lambda c: (0, 0, c)), pl.BlockSpec((16, block), lambda c: (0, c))],
        out_shape=[sd((3, rows, width), BF16), sd((16, width), F32)],
        scratch_shapes=[pltpu.VMEM((3, PRE + rows + POST, block), F32), pltpu.VMEM((3, rows + POST, block), F32)],
        cost_estimate=cost(60 * rows * width, 9 << 20),
        compiler_params=pltpu.CompilerParams(vmem_limit_bytes=GRANT), name="leave")(ginner, ggate, ggate_after, proj, proj_after, taps)

def tokens_kernel(gproj, weight, x, gres, gain, out, sums, acc):
    k = pl.program_id(0)
    rows, width = x.shape
    part = mxu_nt(gproj[0], weight[...])
    @pl.when(k == 0)
    def _():
        acc[...] = part
    @pl.when(k > 0)
    def _():
        acc[...] += part
    @pl.when(k == pl.num_programs(0) - 1)
    def _():
        def body(r, carry):
            a, b = carry
            v = x[r, :].astype(F32)
            v = v - jnp.mean(v, axis=-1, keepdims=True)
            s = lax.rsqrt(jnp.mean(v * v, axis=-1, keepdims=True) + EPSILON)
            n = v * s
            d = acc[r, :]
            a += fold8(d * n)
            b += fold8(d)
            e = d * gain[...]
            m1 = jnp.mean(e, axis=-1, keepdims=True)
            m2 = jnp.mean(e * n, axis=-1, keepdims=True)
            out[r, :] = gres[r, :].astype(F32) + (e - m1 - n * m2) * s
            return a, b
        zero = jnp.zeros((8, width), F32)
        a, b = rows_loop(rows, CHUNK, body)((zero, zero))
        sums[0:1, :] = jnp.sum(a, axis=0, keepdims=True)
        sums[1:2, :] = jnp.sum(b, axis=0, keepdims=True)

def tokens_back(gproj, weight, x, gres, gain):
    rows, width = x.shape
    whole = lambda *s: pl.BlockSpec(s, lambda k: (0,) * len(s))
    sd = jax.ShapeDtypeStruct
    return pl.pallas_call(
        tokens_kernel, grid=(3,),
        in_specs=[pl.BlockSpec((1, rows, width), lambda k: (k, 0, 0)), pl.BlockSpec((width, width), lambda k: (0, k)),
                  whole(rows, width), whole(rows, width), whole(1, width)],
        out_specs=[whole(rows, width), whole(2, width)],
        out_shape=[sd((rows, width), F32), sd((2, width), F32)],
        scratch_shapes=[pltpu.VMEM((rows, width), F32)],
        cost_estimate=cost(6 * rows * width * width, 14 << 20),
        compiler_params=pltpu.CompilerParams(vmem_limit_bytes=GRANT), name="tokens_back")(gproj, weight, x, gres, gain)


def wgrad_kernel(row_order, units, *refs, lefts, rights, held, mode):
    acc = None
    for side in range(2):
        refs_left, refs = refs[:lefts], refs[lefts:]
        left = jnp.concatenate([r[...] for r in refs_left], axis=1)
        refs_right, refs = refs[:rights], refs[rights:]
        right = jnp.concatenate([r[0] for r in refs_right], axis=1)
        part = mxu_tn(left, right)
        acc = part if acc is None else acc + part
    outs = refs[held:]
    count, height, _ = outs[0].shape
    width = acc.shape[1] // 2
    value = acc.reshape(count, height, acc.shape[1]).astype(BF16)
    if mode == "x":
        outs[0][...] = value[..., :width]
        outs[1][...] = value[..., width:]
    if mode == "xy":
        cut = width // 2
        outs[0][...] = value[..., :cut]
        outs[1][...] = value[..., width : width + cut]
        value = jnp.concatenate([value[..., cut:width], value[..., width + cut :]], axis=2)
        outs = outs[2:]
    if mode in ("y", "xy"):
        early = pl.program_id(0) < pl.num_programs(0) // 2

        @pl.when(early)
        def _():
            outs[0][...] = value

        @pl.when(jnp.logical_not(early))
        def _():
            outs[1][...] = value


def wgrad(left, right, row_order, units, unit, mode, each, held=(), tall=None, start=0):
    rows, m = left[0].shape
    blocks, count = row_order.shape[0], units.shape[0]
    height = m // blocks
    tall = tall or height
    at = start // height
    per = right[0].shape[2] // unit
    wide = count * unit
    half = wide // 2
    if height % LANES:
        left = [v.reshape(rows, blocks, height)[:, row_order].reshape(rows, m) for v in left]
        each = max(each, LANES // height)
        left_specs = [pl.BlockSpec((rows, each * height), lambda i, r, u: (0, i))]
    else:
        left_specs = [pl.BlockSpec((rows, height), lambda i, r, u, q=q: (0, r[i * each + q])) for q in range(each)]
    lefts, steps = len(left_specs), blocks // each
    right_specs = [
        pl.BlockSpec((1, rows, unit), lambda i, r, u, j=j: (u[j] // per, 0, u[j] % per)) for j in range(count)
    ]
    in_specs, args = [], []
    for side in range(2):
        in_specs += left_specs + right_specs
        args += [left[side]] * lefts + [right[side]] * count
    aliases = {2 + len(args) + i: i for i in range(len(held))}
    in_specs += [pl.BlockSpec(memory_space=pl.ANY)] * len(held)
    args += list(held)
    full = lambda w: ((blocks, tall, w), pl.BlockSpec((each, height, w), lambda i, r, u: (i, at, 0)))
    first = ((blocks // 2, tall, wide), lambda i: jnp.minimum(i, steps // 2 - 1))
    second = ((blocks // 2, tall, wide), lambda i: jnp.maximum(i - steps // 2, 0))
    part = lambda s, w: ((s[0][0], tall, w), pl.BlockSpec((each, height, w), lambda i, r, u: (s[1](i), at, 0)))
    outs = {
        "x": [full(half)] * 2,
        "y": [part(first, wide), part(second, wide)],
        "xy": [full(half // 2)] * 2 + [part(first, half), part(second, half)],
    }[mode]
    return pl.pallas_call(
        functools.partial(wgrad_kernel, lefts=lefts, rights=count, held=len(held), mode=mode),
        grid_spec=pltpu.PrefetchScalarGridSpec(
            num_scalar_prefetch=2, grid=(steps,), in_specs=in_specs, out_specs=[o[1] for o in outs]
        ),
        out_shape=[jax.ShapeDtypeStruct(o[0], BF16) for o in outs],
        input_output_aliases=aliases,
        cost_estimate=cost(4 * rows * m * wide, 4 * (rows * m + rows * wide + m * wide)),
        compiler_params=pltpu.CompilerParams(vmem_limit_bytes=GRANT),
        name="wgrad",
    )(row_order, units, *args)


def on_device(
    tokens,
    cotangent,
    norm1_gain,
    norm1_bias,
    in_weight,
    in_bias,
    short_weight,
    short_bias,
    filter_in,
    filter_in_bias,
    sine_freq,
    filter_out,
    decay_rates,
    filter_bias,
    out_weight,
    out_bias,
    norm2_gain,
    norm2_bias,
    up_weight,
    up_bias,
    down_weight,
    down_bias,
):
    width = in_weight.shape[0]
    ff = up_weight.shape[1]
    rows = tokens.shape[1]
    seq = lax.axis_size("seq")
    me = lax.axis_index("seq")
    length = rows * seq
    chans = width // seq
    down_shift = [(i + 1, i) for i in range(seq - 1)]

    x, dy = tokens[0], cotangent[0]
    mine = jnp.concatenate([short_weight.reshape(9 * chans), short_bias.reshape(3 * chans), x[rows - 2 :].reshape(-1).astype(F32)])
    used = mine.size
    mine = jnp.pad(mine, (0, -used % (8 * LANES)))
    got = lax.all_to_all(
        jnp.broadcast_to(mine.reshape(1, -1, LANES), (seq, mine.size // LANES, LANES)),
        "seq", split_axis=0, concat_axis=0, tiled=True,
    ).reshape(seq, -1)
    all_taps = got[:, : 12 * chans].reshape(seq, 12, chans).transpose(1, 0, 2).reshape(12, width)
    before = pick(got, jnp.maximum(me - 1, 0), 0)[12 * chans : used].reshape(2, width)
    before = jnp.concatenate([jnp.zeros((PRE - 2, width), BF16), before.astype(BF16)], axis=0)

    row = lambda v: v[None, :]
    first = me.reshape(1).astype(jnp.int32)
    fast = length // BLOCK <= 64
    tables = make_tables(length) if fast else None
    before, all_taps, tables = lax.optimization_barrier((before, all_taps, tables))
    inner, gate, proj, normed = enter(
        first, x, before, row(norm1_gain), row(norm1_bias), in_weight, row(in_bias), all_taps
    )
    proj_after = lax.ppermute(proj[:, PRE : PRE + POST], "seq", down_shift)

    def to_channels(value):
        if chans != LANES:
            value = value.transpose(1, 0, 2).reshape(rows, seq, chans).transpose(1, 0, 2)
        got = lax.all_to_all(value, "seq", split_axis=0, concat_axis=0, tiled=True)
        return got.reshape(length, chans)

    def to_tokens(value):
        got = lax.all_to_all(value, "seq", split_axis=0, concat_axis=0, tiled=True)
        if chans != LANES:
            got = got.transpose(1, 0, 2).reshape(got.shape[1], width // LANES, LANES).transpose(1, 0, 2)
        return got

    inner_chan = to_channels(inner)

    mixer = (FastMixer if fast else PlainMixer)(length, chans, seq, tables)
    features = position_features(length)
    hidden_pre = jnp.dot(filter_in.T, features, precision=HIGH) + filter_in_bias[:, None]
    phase = sine_freq[:, None] * hidden_pre
    hidden = jnp.sin(phase)
    window = jnp.exp(-features[0][:, None] * decay_rates[None, :])
    kernel = jnp.einsum("hn,hc->nc", hidden, filter_out, precision=HIGH) * window
    kernel_spec = mixer.spectrum(kernel)

    conv_chan, inner_spec = mixer.convolve(inner_chan, kernel_spec, filter_bias, False, 0)
    conv_chan, proj_after = tie(conv_chan, proj_after)
    conv = to_tokens(conv_chan)
    dy_other, normed_other = swap(dy, "dp", 1), swap(normed, "dp", 1)
    grad_act, dy_sum = back_act(dy, down_weight)
    conv, dy_other, normed_other = tie(conv, dy_other, normed_other)
    act, gup, gup_sum, resid, normed2, mixed, grad_attn, grad_conv, grad_gate, mid_sums = middle(
        conv, gate, x, dy, grad_act, out_weight, row(out_bias), row(norm2_gain), row(norm2_bias), up_weight, row(up_bias)
    )
    grad_chan = to_channels(grad_conv)
    gate_after = lax.ppermute(grad_gate[:POST], "seq", down_shift)

    bits = seq_bits()
    order = block_order(bits)
    up_bits = [bits[1], bits[0]] + bits[2:]
    up_order = block_order(up_bits)
    unit = width // 4
    tall = (ff + width) // seq
    wide = ff // seq

    pair = lambda value: (value, swap(value, "dp", 1))
    near_units, near_up = chip_units(dy[None], unit, (2, 0)), chip_units(gup[None], ff // 4, (2, 0))
    dy_pair, act_pair = (dy[None], dy_other[None]), pair(act)
    mixed_pair, attn_pair = pair(mixed), pair(grad_attn[None])
    gup_pair, normed2_pair = pair(gup[None]), pair(normed2)
    block_output = block_out(act, down_weight, resid, row(down_bias))
    block_output, act_pair = tie(block_output, act_pair)
    parts = wgrad(act_pair, dy_pair, order, near_units, unit, "x", 2, tall=tall)
    each = 8 if seq == 8 else 4
    tall_send, tall_kept = wgrad(
        mixed_pair, attn_pair, order, near_units, unit, "x", each, held=parts, tall=tall, start=wide
    )
    tall_got = swap(tall_send, "dp", 2)
    grad_chan, tall_kept = tie(grad_chan, tall_kept)
    grad_inner_chan, grad_spec = mixer.convolve(grad_chan, kernel_spec, filter_bias, True, POST)
    gup_pair, normed2_pair, grad_inner_chan, gate_after = tie(gup_pair, normed2_pair, grad_inner_chan, gate_after)
    grad_inner = to_tokens(grad_inner_chan)
    up_send, up_kept = wgrad(normed2_pair, gup_pair, up_order, near_up, ff // 4, "y", 4)

    grad_filter_out, grad_filter_in, filter_sums, grad_filter_bias = mixer.filter_grad(
        grad_spec, inner_spec, grad_chan, inner_chan, (features, hidden_pre, phase, hidden, window, filter_out)
    )
    grad_freq = filter_sums[0]
    grad_filter_in_bias = filter_sums[1] * sine_freq
    grad_filter_in = grad_filter_in * sine_freq[None, :]

    grad_inner, grad_filter_out, up_send = tie(grad_inner, grad_filter_out, up_send)
    up_got = swap(up_send, "seq", up_bits[0])
    grad_proj, leave_sums = leave(grad_inner, grad_gate, gate_after, proj, proj_after, all_taps)
    grad_proj, tall_got = tie(grad_proj, tall_got)
    tall_send, tall_kept = halve(tall_kept, tall_got)
    tall_got = swap(tall_send, "seq", bits[0])

    in_units = chip_units(grad_proj, unit, (2, 0))
    proj_pair = pair(grad_proj)
    in_parts = wgrad((normed, normed_other), proj_pair, order, in_units, unit, "xy", 4)
    grad_proj, in_a_send, in_b_send = tie(grad_proj, in_parts[0], in_parts[2])
    in_a_got = swap(in_a_send, "dp", 2)
    in_b_got = swap(in_b_send, "seq", bits[0])

    grad_tokens, token_sums = tokens_back(grad_proj, in_weight, x, grad_attn, row(norm1_gain))
    shared = (token_sums, leave_sums, mid_sums, gup_sum, dy_sum, grad_filter_in, grad_filter_in_bias, grad_freq)
    channel = (grad_filter_out, grad_filter_bias)
    packed, extra = pack(shared), pack(channel)
    rows_shared = packed.shape[0]
    packed = jnp.concatenate([packed, extra], axis=0)
    packed = packed + swap(packed, "dp", 1)
    packed, up_got, tall_got, in_a_got = tie(packed, up_got, tall_got, in_a_got)
    packed, extra = packed[:rows_shared], packed[rows_shared:]
    small = swap(packed, "seq", bits[0])
    cut = ff // 4
    up_send, up_kept = add(up_kept[..., :cut], up_got[..., :cut]), add(up_kept[..., cut:], up_got[..., cut:])
    up_got = swap(up_send, "dp", 2)
    tall_send, tall_kept = halve(tall_kept, tall_got)
    tall_got = swap(tall_send, "seq", bits[1])
    a_send, a_kept = halve(in_parts[1], in_a_got)
    a_got = swap(a_send, "seq", bits[0])

    in_b_got, tall_got, small = tie(in_b_got, tall_got, small)
    packed = packed + small
    small = swap(packed, "seq", bits[1])
    cut = in_b_got.shape[2] // 2
    b_send, b_kept = add(in_parts[3][..., :cut], in_b_got[..., :cut]), add(in_parts[3][..., cut:], in_b_got[..., cut:])
    b_got = swap(b_send, "dp", 2)
    tall_send, tall_kept = halve(tall_kept, tall_got)
    tall_got = swap(tall_send, "seq", bits[2])

    up_got, a_got, small = tie(up_got, a_got, small)
    both = jnp.concatenate([packed + small, extra], axis=0)
    small = swap(both, "dp", 2)
    up_send, up_kept = halve(up_kept, up_got)
    up_got = swap(up_send, "seq", up_bits[1])

    b_got, small = tie(b_got, small)
    both = both + small
    packed, extra = both[:rows_shared], both[rows_shared:]
    small = swap(packed, "seq", bits[2])
    kept, got = jnp.concatenate([a_kept, b_kept], axis=2), jnp.concatenate([a_got, b_got], axis=2)
    send, kept = halve(kept, got)
    got = swap(send, "seq", bits[1])

    for i in range(2, len(bits)):
        got, up_got, small, tall_got = tie(got, up_got, small, tall_got)
        packed = packed + small
        send, kept = halve(kept, got)
        got = swap(send, "seq", bits[i])
        up_send, up_kept = halve(up_kept, up_got)
        up_got = swap(up_send, "seq", bits[i])
        if i + 1 < len(bits):
            small = swap(packed, "seq", bits[i + 1])
            tall_send, tall_kept = halve(tall_kept, tall_got)
            tall_got = swap(tall_send, "seq", bits[i + 1])
    grad_in, grad_up, both = last(kept, got), last(up_kept, up_got), last(tall_kept, tall_got)
    grad_down, grad_out_weight = both[:wide], both[wide:]
    channel = unpack(extra, channel)
    shared = unpack(packed, shared)
    token_sums, leave_sums, mid_sums, gup_sum, dy_sum = shared[:5]
    own = lax.dynamic_slice_in_dim(leave_sums[:12], me * chans, chans, 1)
    return (
        block_output[None],
        grad_tokens[None],
        token_sums[0],
        token_sums[1],
        grad_in,
        leave_sums[12:15].reshape(-1),
        own[:9].reshape(3, 3, chans),
        own[9:],
        shared[5],
        shared[6],
        shared[7],
        channel[0],
        channel[1],
        grad_out_weight,
        mid_sums[2],
        mid_sums[0],
        mid_sums[1],
        grad_up,
        gup_sum[0],
        grad_down,
        dy_sum[0],
    )


def solution(mesh):
    everywhere, by_token, by_rows = P(), P("dp", "seq", None), P("seq", "dp")
    taps, shift, chan = P(None, None, "seq"), P(None, "seq"), P("seq")
    in_specs = (by_token,) * 2 + (everywhere,) * 4 + (taps, shift) + (everywhere,) * 3
    in_specs += (shift, chan, chan) + (everywhere,) * 8
    out_specs = (by_token, by_token, everywhere, everywhere, by_rows, everywhere, taps, shift)
    out_specs += (everywhere,) * 3 + (shift, chan, by_rows) + (everywhere,) * 3
    out_specs += (by_rows, everywhere, by_rows, everywhere)
    return jax.shard_map(
        on_device, mesh=mesh, in_specs=in_specs, out_specs=out_specs, check_vma=False
    )
```

time: 461 us -> 362 us (0.79)
  Pallas kernels: 57.1 us -> 165 us
  matrix products: 121 us -> 14.1 us
  other arithmetic: 65 us -> 26.3 us
  waiting for transfers between devices: 113 us -> 74.8 us
  local copies, waits for them, and re-layouts: 36.4 us -> 19.3 us
    pallas_call x4 -> x14, Pallas kernels: 40.9 us -> 159 us  [the longest x4 37.6 us: vmem_call(): pl.pallas_call(body, in_specs=[pl.BlockSpec(memory_space=pl.ANY)] * count...]
    dot_general x24 -> x0, matrix products: 113 us -> none  [the longest x21 97.1 us: matmul(): return jnp.einsum(spec, left, right, preferred_element_type=F32)]
    all_to_all x5, waiting for transfers between devices: 39.7 us -> 16.6 us  [the longest x2 13.8 us: to_tokens(): got = lax.all_to_all(value, 'seq', split_axis=0, concat_axis=0, tiled=True)]
    ppermute x2, waiting for transfers between devices: 20.4 us -> 0.01 us  [the longest x1 0.01 us: on_device(): gate_after = lax.ppermute(grad_gate[:POST], 'seq', down_shift)]
    reduce_sum x6 -> x0, other arithmetic: 10.6 us -> none  [the longest x1 4.27 us: on_device(): jnp.sum(grad_short[k] * lagged(k, j), axis=0)]
    pallas_call x1, Pallas kernels: 16.2 us -> 6.12 us  [make_tables(): pl.pallas_call(functools.partial(table_kernel, scale=1.0 / length), grid=...]
    unnamed x4 -> x1, other arithmetic: 8.89 us -> 0.73 us
    unnamed x174 -> x77, local copies, waits for them, and re-layouts: 15.2 us -> 7.27 us
  transfers between devices with their start and end apart: 37 -> 34, of which waited for: 17 -> 16; matrix products, arithmetic and copies ran while one was open for 32% -> 12% of each run, Pallas kernels for 10% -> 34%
where the time goes in v2:
time: 362 us; the launch traced here: 360 us
  Pallas kernels  165 us (46%)
  waiting for transfers between devices  74.8 us (21%)
  starting transfers between devices  58.8 us (16%)
  other arithmetic  26.3 us (7%)
  local copies, waits for them, and re-layouts  19.3 us (5%)
  matrix products  14.1 us (4%)
    ppermute x27, waiting for transfers between devices, swap(): return lax.ppermute(value, axis, [(i, i ^ bit) for i in range(size)])  58.1 us
    pallas_call x4, Pallas kernels, vmem_call(): pl.pallas_call(body, in_specs=[pl.BlockSpec(memory_space=pl.ANY)] * count...  37.6 us
    pallas_call x4, Pallas kernels, wgrad(): pl.pallas_call(functools.partial(wgrad_kernel, lefts=lefts, rights=count,...  34.5 us
    pallas_call x1, Pallas kernels, middle(): pl.pallas_call(middle_kernel, grid=(ff // block,), in_specs=[whole(nb, ro...  30.5 us
    ppermute x27, starting transfers between devices, swap(): return lax.ppermute(value, axis, [(i, i ^ bit) for i in range(size)])  26.9 us
    convert_element_type x10, other arithmetic, add(): return (left.astype(F32) + right.astype(F32)).astype(BF16)  16.4 us
    all_to_all x2, waiting for transfers between devices, to_tokens(): got = lax.all_to_all(value, 'seq', split_axis=0, concat_axis=0, tiled=True)  13.8 us
    pallas_call x1, Pallas kernels, enter(): pl.pallas_call(enter_kernel, grid=(steps,), in_specs=[pl.BlockSpec(memory...  12.9 us
  transfers between devices with their start and end apart: 34, of which 16 were waited for; matrix products, arithmetic and copies ran while one was open for 12% of the time, Pallas kernels for 34%

profile of v2, /device:TPU:0, one launch (start us, length us, event | category | flops | bytes accessed | tf_op | source)
XLA Modules:
  0.0 360.2 jit_solution(14018358033638012378)
XLA Ops:
  3.5 7.3 %all-to-all-start = ((f32[8,32,128]{2,1,0:T(8,128)}), f32[8,32,128]{2,1,0:T(8,128)S(1)}, u32[]{:S(2)}, u32[]{:S(2)}) async-start(f32[8,32,128]{2,1,0:T(8,128)} %broadcast_in_dim.60), calls=%async_computation | async-start | bytes 262144 | tf_op jit(solution)/shard_map/all_to_all | solution.py:930
  10.7 6.1 %tables.1 = (bf16[32,256,256]{2,1,0:T(8,128)(2,1)}, bf16[32,256,256]{2,1,0:T(8,128)(2,1)}) custom-call(f32[32,1,128]{2,1,0:T(1,128)} %constant.58.clone.alpha_cos, f32[32,1,128]{2,1,0:T(1,128)} %constant.59.clone.alpha_sin, f32[128,128]{1,0:T(8,128)} %constant.60.clone.beta_cos, f32[128,128]{1,0:T(8,128)} %constant.61.clone.beta_sin), custom_call_target="tpu_custom_call" | custom-call | flops 1048576 | bytes 1048576 | tf_op jit(solution)/shard_map/tables/pallas_call | solution.py:145
  19.6 12.9 %enter.1 = (bf16[8,512,128]{2,1,0:T(8,128)(2,1)}, bf16[512,1024]{1,0:T(8,128)(2,1)}, bf16[3,528,1024]{2,1,0:T(8,128)(2,1)}, bf16[512,1024]{1,0:T(8,128)(2,1)}) custom-call(s32[1]{0:T(128)} %bitcast.first, bf16[512,1024]{1,0:T(8,128)(2,1)} %bitcast.94, bf16[16,1024]{1,0:T(8,128)(2,1)} %concatenate.35.before, f32[1,1024]{1,0:T(1,128)} %bitcast.120, ...), custom_call_target="tpu_custom_call" | custom-call | flops 402653184 | bytes 1835008 | tf_op jit(solution)/shard_map/enter/pallas_call | solution.py:681
  38.4 5.8 %multiply_cosine_fusion = (f32[64,4096]{1,0:T(8,128)}, bf16[64,4096]{1,0:T(8,128)(2,1)}, f32[64,4096]{1,0:T(8,128)S(1)}) fusion(f32[64]{0:T(128)S(1)} %copy-done.28, f32[64]{0:T(128)S(1)} %copy-done.31, f32[33,64]{1,0:T(8,128)S(1)} %copy-done, f32[16,4096]{1,0:T(8,128)S(1)} %get-tuple-element.216, f32[16,4096]{1,0:T(8,128)S(1)} %get-tuple-element.215, ...), kind=kOutput, calls=%fused_computation.12 | convolution fusion | flops 104865792 | bytes 3171072 | tf_op jit(solution)/shard_map/dot_general | solution.py:964
  45.3 8.3 %convolution_multiply_fusion = f32[4096,128]{1,0:T(8,128)} fusion(f32[64,128]{1,0:T(8,128)S(1)} %copy-done.19, f32[64,4096]{1,0:T(8,128)S(1)} %get-tuple-element.217.refs_8_, f32[128]{0:T(128)S(1)} %copy-done.30, f32[4096]{0:T(1024)S(1)} %multiply_negate_fusion, f32[64]{0:T(128)S(1)} %copy-done.28), kind=kOutput, calls=%fused_computation | convolution fusion | flops 403963904 | bytes 3195648 | tf_op jit(solution)/shard_map/hn,hc->nc/dot_general | solution.py:968
  55.8 6.4 %spectrum.1.refs_1_ = bf16[32,256,128]{2,1,0:T(8,128)(2,1)} custom-call(f32[32,128,128]{2,1,0:T(8,128)} %bitcast.102, bf16[32,256,256]{2,1,0:T(8,128)(2,1)} %get-tuple-element.110.refs_1_.refs_3_), custom_call_target="tpu_custom_call" | custom-call | flops 536870912 | bytes 2097152 | tf_op jit(solution)/shard_map/spectrum/pallas_call | solution.py:279
  64.8 10.0 %convolve.1 = (bf16[8,512,128]{2,1,0:T(8,128)(2,1)}, bf16[32,256,128]{2,1,0:T(8,128)(2,1)}) custom-call(bf16[32,128,128]{2,1,0:T(8,128)(2,1)} %bitcast.97, bf16[32,256,128]{2,1,0:T(8,128)(2,1)} %spectrum.1.refs_1_, f32[1,128]{1,0:T(1,128)} %bitcast.131, bf16[32,256,256]{2,1,0:T(8,128)(2,1)} %get-tuple-element.110.refs_1_.refs_3_, ...), custom_call_target="tpu_custom_call" | custom-call | flops 536870912 | bytes 2097152 | tf_op jit(solution)/shard_map/convolve/pallas_call | solution.py:279
  74.8 5.6 %all-to-all-start.2 = ((bf16[8,512,128]{2,1,0:T(8,128)(2,1)}), bf16[8,512,128]{2,1,0:T(8,128)(2,1)}, u32[]{:S(2)}, u32[]{:S(2)}) async-start(bf16[8,512,128]{2,1,0:T(8,128)(2,1)} %get-tuple-element.114), calls=%async_computation.2 | async-start | bytes 2097152 | tf_op jit(solution)/shard_map/all_to_all | solution.py:955
  81.1 11.0 %back_act.1 = (bf16[512,4096]{1,0:T(8,128)(2,1)}, f32[1,1024]{1,0:T(1,128)}) custom-call(bf16[512,1024]{1,0:T(8,128)(2,1)} %bitcast.91, bf16[4096,1024]{1,0:T(8,128)(2,1)} %down.3), custom_call_target="tpu_custom_call" | custom-call | flops 536870912 | bytes 1703936 | tf_op jit(solution)/shard_map/back_act/pallas_call | solution.py:486
  92.0 13.1 %all-to-all-done.2.conv = bf16[8,512,128]{2,1,0:T(8,128)(2,1)} async-done(((bf16[8,512,128]{2,1,0:T(8,128)(2,1)}), bf16[8,512,128]{2,1,0:T(8,128)(2,1)}, u32[]{:S(2)}, u32[]{:S(2)}) %all-to-all-start.2) | async-done | bytes 1048608 | tf_op jit(solution)/shard_map/all_to_all | solution.py:955
  105.2 30.5 %middle.1 = (bf16[512,4096]{1,0:T(8,128)(2,1)}, bf16[512,4096]{1,0:T(8,128)(2,1)}, f32[1,4096]{1,0:T(1,128)}, bf16[512,1024]{1,0:T(8,128)(2,1)}, bf16[512,1024]{...) custom-call(bf16[8,512,128]{2,1,0:T(8,128)(2,1)} %all-to-all-done.2., ...), custom_call_target="tpu_custom_call" | custom-call | flops 1342177280 | bytes 4456448 | tf_op jit(solution)/shard_map/middle/pallas_call | solution.py:620
  142.4 9.9 %block_out.1 = bf16[512,1024]{1,0:T(8,128)(2,1)} custom-call(bf16[512,4096]{1,0:T(8,128)(2,1)} %get-tuple-element.127.act.refs_0_.refs_1_, bf16[4096,1024]{1,0:T(8,128)(2,1)} %down.3, bf16[512,1024]{1,0:T(8,128)(2,1)} %get-tuple-element.120.resid, f32[1,1024]{1,0:T(1,128)} %bitcast.130), custom_call_target="tpu_custom_call" | custom-call | flops 536870912 | bytes 1966080 | tf_op jit(solution)/shard_map/block_out/pallas_call | solution.py:510
  152.3 9.8 %wgrad.4 = (bf16[8,640,256]{2,1,0:T(8,128)(2,1)}, bf16[8,640,256]{2,1,0:T(8,128)(2,1)}) custom-call(s32[8]{0:T(128)} %broadcast_xor_fusion.1.row_order, s32[2]{0:T(128)} %pad_add_fusion.units, bf16[512,4096]{1,0:T(8,128)(2,1)} %get-tuple-element.127.act.refs_0_.refs_1_, bf16[512,4096]{1,0:T(8,128)(2,1)} %get-tuple-element.127.act.refs_0_.refs_1_, ...), custom_call_target="tpu_custom_call" | custom-call | flops 536870912 | bytes 2228224 | tf_op jit(solution)/shard_map/wgrad/pallas_call | solution.py:880
  171.5 10.1 %correlate.1 = (bf16[8,528,128]{2,1,0:T(8,128)(2,1)}, bf16[32,256,128]{2,1,0:T(8,128)(2,1)}) custom-call(bf16[32,128,128]{2,1,0:T(8,128)(2,1)} %bitcast.26.refs_0_.refs_2_, bf16[32,256,128]{2,1,0:T(8,128)(2,1)} %spectrum.1.refs_1_, f32[1,128]{1,0:T(1,128)} %bitcast.132, bf16[32,256,256]{2,1,0:T(8,128)(2,1)} %get-tuple-element.110.refs_1_.refs_3_, ...), custom_call_target="tpu_custom_call" | custom-call | flops 536870912 | bytes 2097152 | tf_op jit(solution)/shard_map/correlate/pallas_call | solution.py:279
  181.6 7.2 %all-to-all-start.4 = ((bf16[8,528,128]{2,1,0:T(8,128)(2,1)}), bf16[8,528,128]{2,1,0:T(8,128)(2,1)S(1)}, u32[]{:S(2)}, u32[]{:S(2)}) async-start(bf16[8,528,128]{2,1,0:T(8,128)(2,1)} %get-tuple-element.136), calls=%async_computation.4 | async-start | bytes 2162688 | tf_op jit(solution)/shard_map/all_to_all | solution.py:955
  192.4 11.0 %wgrad.6 = (bf16[4,128,2048]{2,1,0:T(8,128)(2,1)}, bf16[4,128,2048]{2,1,0:T(8,128)(2,1)}) custom-call(s32[8]{0:T(128)} %broadcast_xor_fusion.row_order, s32[2]{0:T(128)} %pad_add_fusion.units, bf16[512,1024]{1,0:T(8,128)(2,1)} %get-tuple-element.140.refs_0_.refs_1_.refs_2_.refs_3_, bf16[512,1024]{1,0:T(8,128)(2,1)} %get-tuple-element.140.refs_0_.refs_1_.refs_2_.refs_3_, ...), custom_call_target="tpu_custom_call" | custom-call | flops 536870912 | bytes 1835008 | tf_op jit(solution)/shard_map/wgrad/pallas_call | solution.py:880
  203.5 11.2 %filter_grad.1 = (f32[64,128]{1,0:T(8,128)}, f32[48,64]{1,0:T(8,128)}, f32[64,2]{1,0:T(8,128)}, f32[1,128]{1,0:T(1,128)}) custom-call(bf16[32,256,128]{2,1,0:T(8,128)(2,1)} %get-tuple-element.137.refs_0_, bf16[32,256,128]{2,1,0:T(8,128)(2,1)} %get-tuple-element.138.refs_1_, bf16[32,128,128]{2,1,0:T(8,128)(2,1)} %bitcast.26.refs_0_.refs_2_, ...), custom_call_target="tpu_custom_call" | custom-call | flops 536870912 | bytes 2097152 | tf_op jit(solution)/shard_map/filter_grad/pallas_call | solution.py:279
  216.3 11.8 %leave.1 = (bf16[3,512,1024]{2,1,0:T(8,128)(2,1)}, f32[16,1024]{1,0:T(8,128)}) custom-call(bf16[8,528,128]{2,1,0:T(8,128)(2,1)} %copy-done.12, bf16[512,1024]{1,0:T(8,128)(2,1)} %get-tuple-element.135.ggate, bf16[16,1024]{1,0:T(8,128)(2,1)} %copy-done.23, bf16[3,528,1024]{2,1,0:T(8,128)(2,1)} %get-tuple-element.113.proj, bf16[3,16,1024]{2,1,0:T(8,128)(2,1)} %copy-done.21, ...), custom_call_target="tpu_custom_call" | custom-call | flops 3932160 | bytes 1179648 | tf_op jit(solution)/shard_map/leave/pallas_call | solution.py:753
  238.1 8.8 %wgrad.7 = (bf16[8,128,384]{2,1,0:T(8,128)(2,1)}, bf16[8,128,384]{2,1,0:T(8,128)(2,1)}, bf16[4,128,768]{2,1,0:T(8,128)(2,1)}, bf16[4,128,768]{2,1,0:T(8,128)(2,1)}) custom-call(s32[8]{0:T(128)} %broadcast_xor_fusion.1.row_order, s32[6]{0:T(128)} %pad_add_fusion.1.units, bf16[512,1024]{1,0:T(8,128)(2,1)} %get-tuple-element.115.refs_0_.refs_1_.refs_2_.refs_3_, ...), custom_call_target="tpu_custom_call" | custom-call | flops 402653184 | bytes 1441792 | tf_op jit(solution)/shard_map/wgrad/pallas_call | solution.py:880
  248.4 11.4 %tokens_back.1 = (f32[512,1024]{1,0:T(8,128)}, f32[2,1024]{1,0:T(2,128)}) custom-call(bf16[3,512,1024]{2,1,0:T(8,128)(2,1)} %get-tuple-element.154.refs_4_.refs_5_.refs_6_.refs_7_.refs_8_.refs_9_.gproj, bf16[1024,3072]{1,0:T(8,128)(2,1)} %weight.1, bf16[512,1024]{1,0:T(8,128)(2,1)} %bitcast.96, bf16[512,1024]{1,0:T(8,128)(2,1)} %get-tuple-element.126.gres, ...), custom_call_target="tpu_custom_call" | custom-call | flops 402653184 | bytes 1835008 | tf_op jit(solution)/shard_map/tokens_back/pallas_call | solution.py:800
  266.2 10.3 %collective-permute-done.12 = bf16[4,128,2048]{2,1,0:T(8,128)(2,1)} collective-permute-done((bf16[4,128,2048]{2,1,0:T(8,128)(2,1)}, bf16[4,128,2048]{2,1,0:T(8,128)(2,1)}, u32[]{:S(2)}, u32[]{:S(2)}) %collective-permute-start.12) | collective-permute-done | bytes 2097184 | tf_op jit(solution)/shard_map/ppermute | solution.py:416
  290.3 5.7 %collective-permute-done.16 = bf16[2,640,256]{2,1,0:T(8,128)(2,1)} collective-permute-done((bf16[2,640,256]{2,1,0:T(8,128)(2,1)}, bf16[2,640,256]{2,1,0:T(8,128)(2,1)}, u32[]{:S(2)}, u32[]{:S(2)}) %collective-permute-start.16) | collective-permute-done | bytes 655392 | tf_op jit(solution)/shard_map/ppermute | solution.py:416
  324.8 6.1 %collective-permute-done.25 = f32[232,128]{1,0:T(8,128)S(1)} collective-permute-done((f32[232,128]{1,0:T(8,128)S(1)}, f32[232,128]{1,0:T(8,128)S(1)}, u32[]{:S(2)}, u32[]{:S(2)}) %collective-permute-start.25) | collective-permute-done | bytes 118816 | tf_op jit(solution)/shard_map/ppermute | solution.py:416
  342.9 15.6 %collective-permute-done.27 = bf16[1,128,768]{2,1,0:T(8,128)(2,1)S(1)} collective-permute-done((bf16[1,128,768]{2,1,0:T(8,128)(2,1)S(1)}, bf16[1,128,768]{2,1,0:T(8,128)(2,1)S(1)}, u32[]{:S(2)}, u32[]{:S(2)}) %collective-permute-start.27) | collective-permute-done | bytes 196640 | tf_op jit(solution)/shard_map/ppermute | solution.py:416
  (209 shorter events, 113.2 us)
Async XLA Ops:
  3.5 14.6 %all-to-all-start = ((f32[8,32,128]{2,1,0:T(8,128)}), f32[8,32,128]{2,1,0:T(8,128)S(1)}, u32[]{:S(2)}, u32[]{:S(2)}) async-start(f32[8,32,128]{2,1,0:T(8,128)} %broadcast_in_dim.60), calls=%async_computation | async-start | bytes 262144 | tf_op jit(solution)/shard_map/all_to_all | solution.py:930
  32.5 31.4 %all-to-all-start.1 = ((bf16[8,512,128]{2,1,0:T(8,128)(2,1)}), bf16[8,512,128]{2,1,0:T(8,128)(2,1)S(1)}, u32[]{:S(2)}, u32[]{:S(2)}) async-start(bf16[8,512,128]{2,1,0:T(8,128)(2,1)} %get-tuple-element.109), calls=%async_computation.1 | async-start | bytes 2097152 | tf_op jit(solution)/shard_map/all_to_all | solution.py:951
  54.5 20.3 %collective-permute-start = (bf16[3,16,1024]{2,1,0:T(8,128)(2,1)S(1)}, bf16[3,16,1024]{2,1,0:T(8,128)(2,1)S(1)}, u32[]{:S(2)}, u32[]{:S(2)}) collective-permute-start(bf16[3,16,1024]{2,1,0:T(8,128)(2,1)S(1)} %slice.257), channel_id=1, source_target_pairs={{1,0},{2,1},{3,2},{4,3},{5,4},{6,5},{7,6},{9,8},{10,9},{11,10},{12... | collective-permute-start | bytes 294920 | tf_op jit(solution)/shard_map/ppermute | solution.py:946
  74.8 30.3 %all-to-all-start.2 = ((bf16[8,512,128]{2,1,0:T(8,128)(2,1)}), bf16[8,512,128]{2,1,0:T(8,128)(2,1)}, u32[]{:S(2)}, u32[]{:S(2)}) async-start(bf16[8,512,128]{2,1,0:T(8,128)(2,1)} %get-tuple-element.114), calls=%async_computation.2 | async-start | bytes 2097152 | tf_op jit(solution)/shard_map/all_to_all | solution.py:955
  135.7 16.6 %collective-permute-start.3 = (bf16[512,4096]{1,0:T(8,128)(2,1)}, bf16[512,4096]{1,0:T(8,128)(2,1)}, u32[]{:S(2)}, u32[]{:S(2)}) collective-permute-start(bf16[512,4096]{1,0:T(8,128)(2,1)} %get-tuple-element.127.act.refs_0_.refs_1_), channel_id=1, source_target_pairs={{0,8},{8,0},{16,24},{24,16},{1,9},{9,1},{17,25},{25,17},{2,10},{10... | collective-permute-start | bytes 12582920 | tf_op jit(solution)/shard_map/ppermute | solution.py:416
  135.8 45.9 %collective-permute-start.4 = (bf16[1,512,4096]{2,1,0:T(8,128)(2,1)}, bf16[1,512,4096]{2,1,0:T(8,128)(2,1)}, u32[]{:S(2)}, u32[]{:S(2)}) collective-permute-start(bf16[1,512,4096]{2,1,0:T(8,128)(2,1)} %bitcast.88), channel_id=1, source_target_pairs={{0,8},{8,0},{16,24},{24,16},{1,9},{9,1},{17,25},{25,17},{2,10},{10... | collective-permute-start | bytes 12582920 | tf_op jit(solution)/shard_map/ppermute | solution.py:416
  136.3 35.2 %all-to-all-start.3 = ((bf16[8,512,128]{2,1,0:T(8,128)(2,1)}), bf16[8,512,128]{2,1,0:T(8,128)(2,1)}, u32[]{:S(2)}, u32[]{:S(2)}) async-start(bf16[8,512,128]{2,1,0:T(8,128)(2,1)} %get-tuple-element.124), calls=%async_computation.3 | async-start | bytes 2097152 | tf_op jit(solution)/shard_map/all_to_all | solution.py:951
  140.6 21.4 %collective-permute-start.7 = (bf16[1,512,1024]{2,1,0:T(8,128)(2,1)}, bf16[1,512,1024]{2,1,0:T(8,128)(2,1)}, u32[]{:S(2)}, u32[]{:S(2)}) collective-permute-start(bf16[1,512,1024]{2,1,0:T(8,128)(2,1)} %bitcast.99), channel_id=1, source_target_pairs={{0,8},{8,0},{16,24},{24,16},{1,9},{9,1},{17,25},{25,17},{2,10},{10... | collective-permute-start | bytes 3145736 | tf_op jit(solution)/shard_map/ppermute | solution.py:416
  140.7 21.3 %collective-permute-start.6 = (bf16[512,1024]{1,0:T(8,128)(2,1)S(1)}, bf16[512,1024]{1,0:T(8,128)(2,1)S(1)}, u32[]{:S(2)}, u32[]{:S(2)}) collective-permute-start(bf16[512,1024]{1,0:T(8,128)(2,1)S(1)} %copy-done.3), channel_id=1, source_target_pairs={{0,8},{8,0},{16,24},{24,16},{1,9},{9,1},{17,25},{25,17},{2,10},{10... | collective-permute-start | bytes 3145736 | tf_op jit(solution)/shard_map/ppermute | solution.py:416
  141.8 39.8 %collective-permute-start.5 = (bf16[512,1024]{1,0:T(8,128)(2,1)S(1)}, bf16[512,1024]{1,0:T(8,128)(2,1)}, u32[]{:S(2)}, u32[]{:S(2)}) collective-permute-start(bf16[512,1024]{1,0:T(8,128)(2,1)S(1)} %copy-done.7), channel_id=1, source_target_pairs={{0,8},{8,0},{16,24},{24,16},{1,9},{9,1},{17,25},{25,17},{2,10},{10... | collective-permute-start | bytes 3145736 | tf_op jit(solution)/shard_map/ppermute | solution.py:416
  167.9 60.2 %collective-permute-start.9 = (bf16[8,640,256]{2,1,0:T(8,128)(2,1)}, bf16[8,640,256]{2,1,0:T(8,128)(2,1)}, u32[]{:S(2)}, u32[]{:S(2)}) collective-permute-start(bf16[8,640,256]{2,1,0:T(8,128)(2,1)} %get-tuple-element.149), channel_id=1, source_target_pairs={{0,16},{8,24},{16,0},{24,8},{1,17},{9,25},{17,1},{25,9},{2,18},{10... | collective-permute-start | bytes 7864328 | tf_op jit(solution)/shard_map/ppermute | solution.py:416
  181.6 33.7 %all-to-all-start.4 = ((bf16[8,528,128]{2,1,0:T(8,128)(2,1)}), bf16[8,528,128]{2,1,0:T(8,128)(2,1)S(1)}, u32[]{:S(2)}, u32[]{:S(2)}) async-start(bf16[8,528,128]{2,1,0:T(8,128)(2,1)} %get-tuple-element.136), calls=%async_computation.4 | async-start | bytes 2162688 | tf_op jit(solution)/shard_map/all_to_all | solution.py:955
  228.2 48.4 %collective-permute-start.12 = (bf16[4,128,2048]{2,1,0:T(8,128)(2,1)}, bf16[4,128,2048]{2,1,0:T(8,128)(2,1)}, u32[]{:S(2)}, u32[]{:S(2)}) collective-permute-start(bf16[4,128,2048]{2,1,0:T(8,128)(2,1)} %get-tuple-element.165), channel_id=1, source_target_pairs={{0,2},{1,3},{2,0},{3,1},{4,6},{5,7},{6,4},{7,5},{8,10},{9,11},{10,... | collective-permute-start | bytes 6291464 | tf_op jit(solution)/shard_map/ppermute | solution.py:416
  234.3 31.9 %collective-permute-start.13 = (bf16[4,640,256]{2,1,0:T(8,128)(2,1)}, bf16[4,640,256]{2,1,0:T(8,128)(2,1)}, u32[]{:S(2)}, u32[]{:S(2)}) collective-permute-start(bf16[4,640,256]{2,1,0:T(8,128)(2,1)} %get-tuple-element.192), channel_id=1, source_target_pairs={{0,1},{1,0},{2,3},{3,2},{4,5},{5,4},{6,7},{7,6},{8,9},{9,8},{10,11... | collective-permute-start | bytes 3932168 | tf_op jit(solution)/shard_map/ppermute | solution.py:416
  246.9 29.7 %collective-permute-start.14 = (bf16[8,128,384]{2,1,0:T(8,128)(2,1)}, bf16[8,128,384]{2,1,0:T(8,128)(2,1)S(1)}, u32[]{:S(2)}, u32[]{:S(2)}) collective-permute-start(bf16[8,128,384]{2,1,0:T(8,128)(2,1)} %get-tuple-element.168), channel_id=1, source_target_pairs={{0,16},{8,24},{16,0},{24,8},{1,17},{9,25},{17,1},{25,9},{2,18},{10... | collective-permute-start | bytes 2359304 | tf_op jit(solution)/shard_map/ppermute | solution.py:416
  260.7 28.1 %collective-permute-start.15 = (bf16[4,128,768]{2,1,0:T(8,128)(2,1)}, bf16[4,128,768]{2,1,0:T(8,128)(2,1)}, u32[]{:S(2)}, u32[]{:S(2)}) collective-permute-start(bf16[4,128,768]{2,1,0:T(8,128)(2,1)} %get-tuple-element.170), channel_id=1, source_target_pairs={{0,1},{1,0},{2,3},{3,2},{4,5},{5,4},{6,7},{7,6},{8,9},{9,8},{10,11... | collective-permute-start | bytes 2359304 | tf_op jit(solution)/shard_map/ppermute | solution.py:416
  279.3 16.6 %collective-permute-start.16 = (bf16[2,640,256]{2,1,0:T(8,128)(2,1)}, bf16[2,640,256]{2,1,0:T(8,128)(2,1)}, u32[]{:S(2)}, u32[]{:S(2)}) collective-permute-start(bf16[2,640,256]{2,1,0:T(8,128)(2,1)} %get-tuple-element.196), channel_id=1, source_target_pairs={{0,2},{1,3},{2,0},{3,1},{4,6},{5,7},{6,4},{7,5},{8,10},{9,11},{10,... | collective-permute-start | bytes 1966088 | tf_op jit(solution)/shard_map/ppermute | solution.py:416
  283.9 26.3 %collective-permute-start.18 = (bf16[4,128,1024]{2,1,0:T(8,128)(2,1)}, bf16[4,128,1024]{2,1,0:T(8,128)(2,1)S(1)}, u32[]{:S(2)}, u32[]{:S(2)}) collective-permute-start(bf16[4,128,1024]{2,1,0:T(8,128)(2,1)} %get-tuple-element.194), channel_id=1, source_target_pairs={{0,16},{8,24},{16,0},{24,8},{1,17},{9,25},{17,1},{25,9},{2,18},{10... | collective-permute-start | bytes 3145736 | tf_op jit(solution)/shard_map/ppermute | solution.py:416
  288.2 15.4 %collective-permute-start.19 = (bf16[4,128,384]{2,1,0:T(8,128)(2,1)S(1)}, bf16[4,128,384]{2,1,0:T(8,128)(2,1)S(1)}, u32[]{:S(2)}, u32[]{:S(2)}) collective-permute-start(bf16[4,128,384]{2,1,0:T(8,128)(2,1)S(1)} %get-tuple-element.203), channel_id=1, source_target_pairs={{0,1},{1,0},{2,3},{3,2},{4,5},{5,4},{6,7},{7,6},{8,9},{9,8},{10,11... | collective-permute-start | bytes 1179656 | tf_op jit(solution)/shard_map/ppermute | solution.py:416
  297.0 27.7 %collective-permute-start.26 = (bf16[1,640,256]{2,1,0:T(8,128)(2,1)S(1)}, bf16[1,640,256]{2,1,0:T(8,128)(2,1)S(1)}, u32[]{:S(2)}, u32[]{:S(2)}) collective-permute-start(bf16[1,640,256]{2,1,0:T(8,128)(2,1)S(1)} %add_convert_fusion.15), channel_id=1, source_target_pairs={{0,4},{1,5},{2,6},{3,7},{4,0},{5,1},{6,2},{7,3},{8,12},{9,13},{10,... | collective-permute-start | bytes 983048 | tf_op jit(solution)/shard_map/ppermute | solution.py:416
  302.3 16.4 %collective-permute-start.21 = (bf16[4,128,384]{2,1,0:T(8,128)(2,1)S(1)}, bf16[4,128,384]{2,1,0:T(8,128)(2,1)S(1)}, u32[]{:S(2)}, u32[]{:S(2)}) collective-permute-start(bf16[4,128,384]{2,1,0:T(8,128)(2,1)S(1)} %get-tuple-element.201), channel_id=1, source_target_pairs={{0,16},{8,24},{16,0},{24,8},{1,17},{9,25},{17,1},{25,9},{2,18},{10... | collective-permute-start | bytes 1179656 | tf_op jit(solution)/shard_map/ppermute | solution.py:416
  313.1 17.7 %collective-permute-start.24 = (bf16[2,128,1024]{2,1,0:T(8,128)(2,1)S(1)}, bf16[2,128,1024]{2,1,0:T(8,128)(2,1)S(1)}, u32[]{:S(2)}, u32[]{:S(2)}) collective-permute-start(bf16[2,128,1024]{2,1,0:T(8,128)(2,1)S(1)} %get-tuple-element.198), channel_id=1, source_target_pairs={{0,1},{1,0},{2,3},{3,2},{4,5},{5,4},{6,7},{7,6},{8,9},{9,8},{10,11... | collective-permute-start | bytes 1572872 | tf_op jit(solution)/shard_map/ppermute | solution.py:416
  337.2 22.1 %collective-permute-start.28 = (bf16[1,128,1024]{2,1,0:T(8,128)(2,1)S(1)}, bf16[1,128,1024]{2,1,0:T(8,128)(2,1)S(1)}, u32[]{:S(2)}, u32[]{:S(2)}) collective-permute-start(bf16[1,128,1024]{2,1,0:T(8,128)(2,1)S(1)} %add_convert_fusion.16), channel_id=1, source_target_pairs={{0,4},{1,5},{2,6},{3,7},{4,0},{5,1},{6,2},{7,3},{8,12},{9,13},{10,... | collective-permute-start | bytes 786440 | tf_op jit(solution)/shard_map/ppermute | solution.py:416
  338.8 19.6 %collective-permute-start.27 = (bf16[1,128,768]{2,1,0:T(8,128)(2,1)S(1)}, bf16[1,128,768]{2,1,0:T(8,128)(2,1)S(1)}, u32[]{:S(2)}, u32[]{:S(2)}) collective-permute-start(bf16[1,128,768]{2,1,0:T(8,128)(2,1)S(1)} %add_convert_fusion.18), channel_id=1, source_target_pairs={{0,4},{1,5},{2,6},{3,7},{4,0},{5,1},{6,2},{7,3},{8,12},{9,13},{10,... | collective-permute-start | bytes 589832 | tf_op jit(solution)/shard_map/ppermute | solution.py:416
  (45 other events, 461.7 us)

commit v3 on v2

--- a/solution.py
+++ b/solution.py
@@ -737,7 +737,7 @@
         for k in range(3):
             g = gbuf[k, pl.ds(r.start, r.size + 8), :]
             v = sum(tap(j, k) * g[2 - j : 2 - j + r.size] for j in range(3)).astype(BF16)
-            gproj[k, r, :] = v
+            gproj[k, 0, r, :] = v
             out.append(carry[k] + fold8(v.astype(F32)))
         return tuple(out)
 
@@ -756,8 +756,8 @@
                   pl.BlockSpec((rows, block), lambda c: (0, c)), pl.BlockSpec((POST, block), lambda c: (0, c)),
                   pl.BlockSpec((3, PRE + rows, block), lambda c: (0, 0, c)), pl.BlockSpec((3, POST, block), lambda c: (0, 0, c)),
                   pl.BlockSpec((12, block), lambda c: (0, c))],
-        out_specs=[pl.BlockSpec((3, rows, block), lambda c: (0, 0, c)), pl.BlockSpec((16, block), lambda c: (0, c))],
-        out_shape=[sd((3, rows, width), BF16), sd((16, width), F32)],
+        out_specs=[pl.BlockSpec((3, 1, rows, block), lambda c: (0, c, 0, 0)), pl.BlockSpec((16, block), lambda c: (0, c))],
+        out_shape=[sd((3, steps, rows, block), BF16), sd((16, width), F32)],
         scratch_shapes=[pltpu.VMEM((3, PRE + rows + POST, block), F32), pltpu.VMEM((3, rows + POST, block), F32)],
         cost_estimate=cost(60 * rows * width, 9 << 20),
         compiler_params=pltpu.CompilerParams(vmem_limit_bytes=GRANT), name="leave")(ginner, ggate, ggate_after, proj, proj_after, taps)
@@ -765,7 +765,8 @@
 def tokens_kernel(gproj, weight, x, gres, gain, out, sums, acc):
     k = pl.program_id(0)
     rows, width = x.shape
-    part = mxu_nt(gproj[0], weight[...])
+    unit = gproj.shape[3]
+    part = sum(mxu_nt(gproj[0, j], weight[:, j * unit : (j + 1) * unit]) for j in range(gproj.shape[1]))
     @pl.when(k == 0)
     def _():
         acc[...] = part
@@ -799,7 +800,7 @@
     sd = jax.ShapeDtypeStruct
     return pl.pallas_call(
         tokens_kernel, grid=(3,),
-        in_specs=[pl.BlockSpec((1, rows, width), lambda k: (k, 0, 0)), pl.BlockSpec((width, width), lambda k: (0, k)),
+        in_specs=[pl.BlockSpec((1,) + gproj.shape[1:], lambda k: (k, 0, 0, 0)), pl.BlockSpec((width, width), lambda k: (0, k)),
                   whole(rows, width), whole(rows, width), whole(1, width)],
         out_specs=[whole(rows, width), whole(2, width)],
         out_shape=[sd((rows, width), F32), sd((2, width), F32)],
@@ -808,9 +809,9 @@
         compiler_params=pltpu.CompilerParams(vmem_limit_bytes=GRANT), name="tokens_back")(gproj, weight, x, gres, gain)
 
 
-def wgrad_kernel(row_order, units, *refs, lefts, rights, held, mode):
+def wgrad_kernel(row_order, units, *refs, sides, lefts, rights, held, mode):
     acc = None
-    for side in range(2):
+    for side in range(sides):
         refs_left, refs = refs[:lefts], refs[lefts:]
         left = jnp.concatenate([r[...] for r in refs_left], axis=1)
         refs_right, refs = refs[:rights], refs[rights:]
@@ -824,31 +825,27 @@
     if mode == "x":
         outs[0][...] = value[..., :width]
         outs[1][...] = value[..., width:]
-    if mode == "xy":
-        cut = width // 2
-        outs[0][...] = value[..., :cut]
-        outs[1][...] = value[..., width : width + cut]
-        value = jnp.concatenate([value[..., cut:width], value[..., width + cut :]], axis=2)
-        outs = outs[2:]
-    if mode in ("y", "xy"):
+    if mode == "y":
         early = pl.program_id(0) < pl.num_programs(0) // 2
 
         @pl.when(early)
         def _():
-            outs[0][...] = value
+            place = 0
+            for piece in outs[:-1]:
+                piece[...] = value[..., place : place + piece.shape[2]]
+                place += piece.shape[2]
 
         @pl.when(jnp.logical_not(early))
         def _():
-            outs[1][...] = value
-
-
-def wgrad(left, right, row_order, units, unit, mode, each, held=(), tall=None, start=0):
+            outs[-1][...] = value
+
+
+def wgrad(left, right, row_order, units, unit, mode, each, held=(), tall=None, start=0, pieces=(1,)):
     rows, m = left[0].shape
-    blocks, count = row_order.shape[0], units.shape[0]
+    sides, blocks, count = len(left), row_order.shape[0], units[0].shape[0]
     height = m // blocks
     tall = tall or height
     at = start // height
-    per = right[0].shape[2] // unit
     wide = count * unit
     half = wide // 2
     if height % LANES:
@@ -858,12 +855,13 @@
     else:
         left_specs = [pl.BlockSpec((rows, height), lambda i, r, u, q=q: (0, r[i * each + q])) for q in range(each)]
     lefts, steps = len(left_specs), blocks // each
-    right_specs = [
-        pl.BlockSpec((1, rows, unit), lambda i, r, u, j=j: (u[j] // per, 0, u[j] % per)) for j in range(count)
-    ]
     in_specs, args = [], []
-    for side in range(2):
-        in_specs += left_specs + right_specs
+    for side in range(sides):
+        per, base = right[side].shape[2] // unit, side * count
+        in_specs += left_specs + [
+            pl.BlockSpec((1, rows, unit), lambda i, r, u, j=base + j, per=per: (u[j] // per, 0, u[j] % per))
+            for j in range(count)
+        ]
         args += [left[side]] * lefts + [right[side]] * count
     aliases = {2 + len(args) + i: i for i in range(len(held))}
     in_specs += [pl.BlockSpec(memory_space=pl.ANY)] * len(held)
@@ -874,20 +872,19 @@
     part = lambda s, w: ((s[0][0], tall, w), pl.BlockSpec((each, height, w), lambda i, r, u: (s[1](i), at, 0)))
     outs = {
         "x": [full(half)] * 2,
-        "y": [part(first, wide), part(second, wide)],
-        "xy": [full(half // 2)] * 2 + [part(first, half), part(second, half)],
+        "y": [part(first, wide * p // sum(pieces)) for p in pieces] + [part(second, wide)],
     }[mode]
     return pl.pallas_call(
-        functools.partial(wgrad_kernel, lefts=lefts, rights=count, held=len(held), mode=mode),
+        functools.partial(wgrad_kernel, sides=sides, lefts=lefts, rights=count, held=len(held), mode=mode),
         grid_spec=pltpu.PrefetchScalarGridSpec(
             num_scalar_prefetch=2, grid=(steps,), in_specs=in_specs, out_specs=[o[1] for o in outs]
         ),
         out_shape=[jax.ShapeDtypeStruct(o[0], BF16) for o in outs],
         input_output_aliases=aliases,
-        cost_estimate=cost(4 * rows * m * wide, 4 * (rows * m + rows * wide + m * wide)),
+        cost_estimate=cost(2 * sides * rows * m * wide, 2 * sides * (rows * m + rows * wide) + 4 * m * wide),
         compiler_params=pltpu.CompilerParams(vmem_limit_bytes=GRANT),
         name="wgrad",
-    )(row_order, units, *args)
+    )(row_order, jnp.concatenate(units), *args)
 
 
 def on_device(
@@ -969,11 +966,13 @@
     kernel_spec = mixer.spectrum(kernel)
 
     conv_chan, inner_spec = mixer.convolve(inner_chan, kernel_spec, filter_bias, False, 0)
-    conv_chan, proj_after = tie(conv_chan, proj_after)
+    normed_x = swap(normed, "dp", 2)
+    conv_chan, proj_after, normed_x = tie(conv_chan, proj_after, normed_x)
+    normed_all = [normed, swap(normed, "dp", 1), normed_x, swap(normed_x, "dp", 1)]
     conv = to_tokens(conv_chan)
-    dy_other, normed_other = swap(dy, "dp", 1), swap(normed, "dp", 1)
+    dy_other = swap(dy, "dp", 1)
     grad_act, dy_sum = back_act(dy, down_weight)
-    conv, dy_other, normed_other = tie(conv, dy_other, normed_other)
+    conv, dy_other, normed_all = tie(conv, dy_other, normed_all)
     act, gup, gup_sum, resid, normed2, mixed, grad_attn, grad_conv, grad_gate, mid_sums = middle(
         conv, gate, x, dy, grad_act, out_weight, row(out_bias), row(norm2_gain), row(norm2_bias), up_weight, row(up_bias)
     )
@@ -993,19 +992,17 @@
     dy_pair, act_pair = (dy[None], dy_other[None]), pair(act)
     mixed_pair, attn_pair = pair(mixed), pair(grad_attn[None])
     gup_pair, normed2_pair = pair(gup[None]), pair(normed2)
-    block_output = block_out(act, down_weight, resid, row(down_bias))
-    block_output, act_pair = tie(block_output, act_pair)
-    parts = wgrad(act_pair, dy_pair, order, near_units, unit, "x", 2, tall=tall)
+    parts = wgrad(act_pair, dy_pair, order, [near_units] * 2, unit, "x", 2, tall=tall)
     each = 8 if seq == 8 else 4
     tall_send, tall_kept = wgrad(
-        mixed_pair, attn_pair, order, near_units, unit, "x", each, held=parts, tall=tall, start=wide
+        mixed_pair, attn_pair, order, [near_units] * 2, unit, "x", each, held=parts, tall=tall, start=wide
     )
     tall_got = swap(tall_send, "dp", 2)
     grad_chan, tall_kept = tie(grad_chan, tall_kept)
     grad_inner_chan, grad_spec = mixer.convolve(grad_chan, kernel_spec, filter_bias, True, POST)
     gup_pair, normed2_pair, grad_inner_chan, gate_after = tie(gup_pair, normed2_pair, grad_inner_chan, gate_after)
     grad_inner = to_tokens(grad_inner_chan)
-    up_send, up_kept = wgrad(normed2_pair, gup_pair, up_order, near_up, ff // 4, "y", 4)
+    *up_sends, up_kept = wgrad(normed2_pair, gup_pair, up_order, [near_up] * 2, ff // 4, "y", 4, pieces=(1, 2, 1))
 
     grad_filter_out, grad_filter_in, filter_sums, grad_filter_bias = mixer.filter_grad(
         grad_spec, inner_spec, grad_chan, inner_chan, (features, hidden_pre, phase, hidden, window, filter_out)
@@ -1014,73 +1011,75 @@
     grad_filter_in_bias = filter_sums[1] * sine_freq
     grad_filter_in = grad_filter_in * sine_freq[None, :]
 
-    grad_inner, grad_filter_out, up_send = tie(grad_inner, grad_filter_out, up_send)
-    up_got = swap(up_send, "seq", up_bits[0])
+    grad_inner, grad_filter_out, up_sends = tie(grad_inner, grad_filter_out, up_sends)
+    up_gots = [swap(up_sends[0], "seq", up_bits[0])]
     grad_proj, leave_sums = leave(grad_inner, grad_gate, gate_after, proj, proj_after, all_taps)
-    grad_proj, tall_got = tie(grad_proj, tall_got)
+    grad_proj, tall_got, up_gots[0] = tie(grad_proj, tall_got, up_gots[0])
     tall_send, tall_kept = halve(tall_kept, tall_got)
     tall_got = swap(tall_send, "seq", bits[0])
-
-    in_units = chip_units(grad_proj, unit, (2, 0))
-    proj_pair = pair(grad_proj)
-    in_parts = wgrad((normed, normed_other), proj_pair, order, in_units, unit, "xy", 4)
-    grad_proj, in_a_send, in_b_send = tie(grad_proj, in_parts[0], in_parts[2])
-    in_a_got = swap(in_a_send, "dp", 2)
-    in_b_got = swap(in_b_send, "seq", bits[0])
-
+    proj_units = grad_proj.reshape((-1,) + grad_proj.shape[2:])
+    proj_all = lax.all_to_all(proj_units, "dp", split_axis=0, concat_axis=0, tiled=True)
+    up_gots.append(swap(up_sends[1], "seq", up_bits[0]))
     grad_tokens, token_sums = tokens_back(grad_proj, in_weight, x, grad_attn, row(norm1_gain))
+
     shared = (token_sums, leave_sums, mid_sums, gup_sum, dy_sum, grad_filter_in, grad_filter_in_bias, grad_freq)
     channel = (grad_filter_out, grad_filter_bias)
     packed, extra = pack(shared), pack(channel)
     rows_shared = packed.shape[0]
     packed = jnp.concatenate([packed, extra], axis=0)
     packed = packed + swap(packed, "dp", 1)
-    packed, up_got, tall_got, in_a_got = tie(packed, up_got, tall_got, in_a_got)
+    packed, up_gots[1], proj_all = tie(packed, up_gots[1], proj_all)
     packed, extra = packed[:rows_shared], packed[rows_shared:]
+    up_gots.append(swap(up_sends[2], "seq", up_bits[0]))
     small = swap(packed, "seq", bits[0])
+    dp_me = lax.axis_index("dp")
+    share = proj_units.shape[0] // 4
+    ahead = jnp.arange(share, dtype=jnp.int32)
+    in_units = [jnp.bitwise_xor(dp_me, w) * share + ahead for w in range(4)]
+    in_send, in_kept = wgrad(normed_all, [proj_all] * 4, order, in_units, proj_units.shape[2], "y", 4)
+
+    in_send, small, tall_got, up_gots, act = tie(in_send, small, tall_got, up_gots, act)
+    in_got = swap(in_send, "seq", bits[0])
     cut = ff // 4
-    up_send, up_kept = add(up_kept[..., :cut], up_got[..., :cut]), add(up_kept[..., cut:], up_got[..., cut:])
+    part = up_gots[1].shape[2] // 2
+    up_send = add(up_kept[..., :cut], jnp.concatenate([up_gots[0], up_gots[1][..., :part]], axis=2))
     up_got = swap(up_send, "dp", 2)
     tall_send, tall_kept = halve(tall_kept, tall_got)
     tall_got = swap(tall_send, "seq", bits[1])
-    a_send, a_kept = halve(in_parts[1], in_a_got)
-    a_got = swap(a_send, "seq", bits[0])
-
-    in_b_got, tall_got, small = tie(in_b_got, tall_got, small)
-    packed = packed + small
-    small = swap(packed, "seq", bits[1])
-    cut = in_b_got.shape[2] // 2
-    b_send, b_kept = add(in_parts[3][..., :cut], in_b_got[..., :cut]), add(in_parts[3][..., cut:], in_b_got[..., cut:])
-    b_got = swap(b_send, "dp", 2)
+    both = jnp.concatenate([packed + small, extra], axis=0)
+    small = swap(both, "dp", 2)
+    block_output = block_out(act, down_weight, resid, row(down_bias))
+    up_kept = add(up_kept[..., cut:], jnp.concatenate([up_gots[1][..., part:], up_gots[2]], axis=2))
+
+    in_got, tall_got, block_output, up_kept = tie(in_got, tall_got, block_output, up_kept)
+    in_send, in_kept = halve(in_kept, in_got)
+    in_got = swap(in_send, "seq", bits[1])
     tall_send, tall_kept = halve(tall_kept, tall_got)
     tall_got = swap(tall_send, "seq", bits[2])
 
-    up_got, a_got, small = tie(up_got, a_got, small)
-    both = jnp.concatenate([packed + small, extra], axis=0)
-    small = swap(both, "dp", 2)
+    in_got, up_got, small = tie(in_got, up_got, small)
+    in_send, in_kept = halve(in_kept, in_got)
+    in_got = swap(in_send, "seq", bits[2])
     up_send, up_kept = halve(up_kept, up_got)
     up_got = swap(up_send, "seq", up_bits[1])
-
-    b_got, small = tie(b_got, small)
     both = both + small
     packed, extra = both[:rows_shared], both[rows_shared:]
-    small = swap(packed, "seq", bits[2])
-    kept, got = jnp.concatenate([a_kept, b_kept], axis=2), jnp.concatenate([a_got, b_got], axis=2)
-    send, kept = halve(kept, got)
-    got = swap(send, "seq", bits[1])
+    small = swap(packed, "seq", bits[1])
 
     for i in range(2, len(bits)):
-        got, up_got, small, tall_got = tie(got, up_got, small, tall_got)
+        up_got, small = tie(up_got, small)
+        if i > 2:
+            in_got, tall_got = tie(in_got, tall_got)
+            in_send, in_kept = halve(in_kept, in_got)
+            in_got = swap(in_send, "seq", bits[i])
+            tall_send, tall_kept = halve(tall_kept, tall_got)
+            tall_got = swap(tall_send, "seq", bits[i])
+        up_send, up_kept = halve(up_kept, up_got)
+        up_got = swap(up_send, "seq", up_bits[i])
         packed = packed + small
-        send, kept = halve(kept, got)
-        got = swap(send, "seq", bits[i])
-        up_send, up_kept = halve(up_kept, up_got)
-        up_got = swap(up_send, "seq", bits[i])
-        if i + 1 < len(bits):
-            small = swap(packed, "seq", bits[i + 1])
-            tall_send, tall_kept = halve(tall_kept, tall_got)
-            tall_got = swap(tall_send, "seq", bits[i + 1])
-    grad_in, grad_up, both = last(kept, got), last(up_kept, up_got), last(tall_kept, tall_got)
+        small = swap(packed, "seq", bits[i])
+    grad_up, packed = last(up_kept, up_got), packed + small
+    grad_in, both = last(in_kept, in_got), last(tall_kept, tall_got)
     grad_down, grad_out_weight = both[:wide], both[wide:]
     channel = unpack(extra, channel)
     shared = unpack(packed, shared)

time: 362 us -> 352 us (0.972)
  waiting for transfers between devices: 74.8 us -> 67.8 us
    ppermute x27, waiting for transfers between devices: 58.1 us -> 37.8 us  [swap(): return lax.ppermute(value, axis, [(i, i ^ bit) for i in range(size)])]
    all_to_all x0 -> x1, waiting for transfers between devices: none -> 10.2 us  [on_device(): lax.all_to_all(proj_units, 'dp', split_axis=0, concat_axis=0, tiled=True)]
    all_to_all x0 -> x1, starting transfers between devices: none -> 3.93 us  [on_device(): lax.all_to_all(proj_units, 'dp', split_axis=0, concat_axis=0, tiled=True)]
    unnamed x77 -> x70, local copies, waits for them, and re-layouts: 7.27 us -> 3.82 us
    convert_element_type x10 -> x8, other arithmetic: 16.4 us -> 13.6 us  [add(): return (left.astype(F32) + right.astype(F32)).astype(BF16)]
  transfers between devices with their start and end apart: 34 -> 35, of which waited for: 16 -> 15; matrix products, arithmetic and copies ran while one was open for 12% -> 14% of each run, Pallas kernels for 34% -> 35%
where the time goes in v3:
time: 352 us; the launch traced here: 350 us
  Pallas kernels  166 us (47%)
  waiting for transfers between devices  67.8 us (19%)
  starting transfers between devices  58.7 us (17%)
  other arithmetic  24.6 us (7%)
  local copies, waits for them, and re-layouts  17.7 us (5%)
  matrix products  14.1 us (4%)
    ppermute x27, waiting for transfers between devices, swap(): return lax.ppermute(value, axis, [(i, i ^ bit) for i in range(size)])  37.8 us
    pallas_call x4, Pallas kernels, vmem_call(): pl.pallas_call(body, in_specs=[pl.BlockSpec(memory_space=pl.ANY)] * count...  37.7 us
    pallas_call x4, Pallas kernels, wgrad(): pl.pallas_call(functools.partial(wgrad_kernel, sides=sides, lefts=lefts,...  34.6 us
    pallas_call x1, Pallas kernels, middle(): pl.pallas_call(middle_kernel, grid=(ff // block,), in_specs=[whole(nb, ro...  30.4 us
    ppermute x27, starting transfers between devices, swap(): return lax.ppermute(value, axis, [(i, i ^ bit) for i in range(size)])  24 us
    convert_element_type x8, other arithmetic, add(): return (left.astype(F32) + right.astype(F32)).astype(BF16)  13.6 us
    all_to_all x2, waiting for transfers between devices, to_tokens(): got = lax.all_to_all(value, 'seq', split_axis=0, concat_axis=0, tiled=True)  13.5 us
    pallas_call x1, Pallas kernels, enter(): pl.pallas_call(enter_kernel, grid=(steps,), in_specs=[pl.BlockSpec(memory...  12.9 us
  transfers between devices with their start and end apart: 35, of which 15 were waited for; matrix products, arithmetic and copies ran while one was open for 14% of the time, Pallas kernels for 35%

profile of v3, /device:TPU:0, one launch (start us, length us, event | category | flops | bytes accessed | tf_op | source)
XLA Modules:
  0.0 350.0 jit_solution(5666634680778059237)
XLA Ops:
  3.5 7.3 %all-to-all-start = ((f32[8,32,128]{2,1,0:T(8,128)}), f32[8,32,128]{2,1,0:T(8,128)S(1)}, u32[]{:S(2)}, u32[]{:S(2)}) async-start(f32[8,32,128]{2,1,0:T(8,128)} %broadcast_in_dim.60), calls=%async_computation | async-start | bytes 262144 | tf_op jit(solution)/shard_map/all_to_all | solution.py:927
  10.8 6.2 %tables.1 = (bf16[32,256,256]{2,1,0:T(8,128)(2,1)}, bf16[32,256,256]{2,1,0:T(8,128)(2,1)}) custom-call(f32[32,1,128]{2,1,0:T(1,128)} %constant.59.clone.alpha_cos, f32[32,1,128]{2,1,0:T(1,128)} %constant.60.clone.alpha_sin, f32[128,128]{1,0:T(8,128)} %constant.61.clone.beta_cos, f32[128,128]{1,0:T(8,128)} %constant.62.clone.beta_sin), custom_call_target="tpu_custom_call" | custom-call | flops 1048576 | bytes 1048576 | tf_op jit(solution)/shard_map/tables/pallas_call | solution.py:145
  19.6 12.9 %enter.1 = (bf16[8,512,128]{2,1,0:T(8,128)(2,1)}, bf16[512,1024]{1,0:T(8,128)(2,1)}, bf16[3,528,1024]{2,1,0:T(8,128)(2,1)}, bf16[512,1024]{1,0:T(8,128)(2,1)}) custom-call(s32[1]{0:T(128)} %bitcast.first, bf16[512,1024]{1,0:T(8,128)(2,1)} %bitcast.93, bf16[16,1024]{1,0:T(8,128)(2,1)} %concatenate.42.before, f32[1,1024]{1,0:T(1,128)} %bitcast.119, ...), custom_call_target="tpu_custom_call" | custom-call | flops 402653184 | bytes 1835008 | tf_op jit(solution)/shard_map/enter/pallas_call | solution.py:681
  40.2 5.8 %multiply_cosine_fusion = (f32[64,4096]{1,0:T(8,128)}, bf16[64,4096]{1,0:T(8,128)(2,1)}, f32[64,4096]{1,0:T(8,128)S(1)}) fusion(f32[64]{0:T(128)S(1)} %copy-done.24, f32[64]{0:T(128)S(1)} %copy-done.27, f32[33,64]{1,0:T(8,128)S(1)} %copy-done, f32[16,4096]{1,0:T(8,128)S(1)} %get-tuple-element.222, f32[16,4096]{1,0:T(8,128)S(1)} %get-tuple-element.221, ...), kind=kOutput, calls=%fused_computation.12 | convolution fusion | flops 104865792 | bytes 3171072 | tf_op jit(solution)/shard_map/dot_general | solution.py:961
  47.0 8.3 %convolution_multiply_fusion = f32[4096,128]{1,0:T(8,128)} fusion(f32[64,128]{1,0:T(8,128)S(1)} %copy-done.16, f32[64,4096]{1,0:T(8,128)S(1)} %get-tuple-element.223.refs_8_, f32[128]{0:T(128)S(1)} %copy-done.26, f32[4096]{0:T(1024)S(1)} %multiply_negate_fusion, f32[64]{0:T(128)S(1)} %copy-done.24), kind=kOutput, calls=%fused_computation | convolution fusion | flops 403963904 | bytes 3195648 | tf_op jit(solution)/shard_map/hn,hc->nc/dot_general | solution.py:965
  58.2 6.4 %spectrum.1.refs_1_ = bf16[32,256,128]{2,1,0:T(8,128)(2,1)} custom-call(f32[32,128,128]{2,1,0:T(8,128)} %bitcast.101, bf16[32,256,256]{2,1,0:T(8,128)(2,1)} %get-tuple-element.114.refs_1_.refs_3_), custom_call_target="tpu_custom_call" | custom-call | flops 536870912 | bytes 2097152 | tf_op jit(solution)/shard_map/spectrum/pallas_call | solution.py:279
  65.5 10.0 %convolve.1 = (bf16[8,512,128]{2,1,0:T(8,128)(2,1)}, bf16[32,256,128]{2,1,0:T(8,128)(2,1)}) custom-call(bf16[32,128,128]{2,1,0:T(8,128)(2,1)} %bitcast.96, bf16[32,256,128]{2,1,0:T(8,128)(2,1)} %spectrum.1.refs_1_, f32[1,128]{1,0:T(1,128)} %bitcast.130, bf16[32,256,256]{2,1,0:T(8,128)(2,1)} %get-tuple-element.114.refs_1_.refs_3_, ...), custom_call_target="tpu_custom_call" | custom-call | flops 536870912 | bytes 2097152 | tf_op jit(solution)/shard_map/convolve/pallas_call | solution.py:279
  75.6 7.8 %all-to-all-start.2 = ((bf16[8,512,128]{2,1,0:T(8,128)(2,1)}), bf16[8,512,128]{2,1,0:T(8,128)(2,1)}, u32[]{:S(2)}, u32[]{:S(2)}) async-start(bf16[8,512,128]{2,1,0:T(8,128)(2,1)} %get-tuple-element.119), calls=%async_computation.2 | async-start | bytes 2097152 | tf_op jit(solution)/shard_map/all_to_all | solution.py:952
  84.0 10.9 %back_act.1 = (bf16[512,4096]{1,0:T(8,128)(2,1)}, f32[1,1024]{1,0:T(1,128)}) custom-call(bf16[512,1024]{1,0:T(8,128)(2,1)} %bitcast.13.dy, bf16[4096,1024]{1,0:T(8,128)(2,1)} %down.3), custom_call_target="tpu_custom_call" | custom-call | flops 536870912 | bytes 1703936 | tf_op jit(solution)/shard_map/back_act/pallas_call | solution.py:486
  94.9 12.9 %all-to-all-done.2.conv = bf16[8,512,128]{2,1,0:T(8,128)(2,1)} async-done(((bf16[8,512,128]{2,1,0:T(8,128)(2,1)}), bf16[8,512,128]{2,1,0:T(8,128)(2,1)}, u32[]{:S(2)}, u32[]{:S(2)}) %all-to-all-start.2) | async-done | bytes 1048608 | tf_op jit(solution)/shard_map/all_to_all | solution.py:952
  107.8 30.4 %middle.1 = (bf16[512,4096]{1,0:T(8,128)(2,1)}, bf16[512,4096]{1,0:T(8,128)(2,1)}, f32[1,4096]{1,0:T(1,128)}, bf16[512,1024]{1,0:T(8,128)(2,1)}, bf16[512,1024]{...) custom-call(bf16[8,512,128]{2,1,0:T(8,128)(2,1)} %all-to-all-done.2., ...), custom_call_target="tpu_custom_call" | custom-call | flops 1342177280 | bytes 4456448 | tf_op jit(solution)/shard_map/middle/pallas_call | solution.py:620
  145.8 9.8 %wgrad.4 = (bf16[8,640,256]{2,1,0:T(8,128)(2,1)}, bf16[8,640,256]{2,1,0:T(8,128)(2,1)}) custom-call(s32[8]{0:T(128)} %broadcast_xor_fusion.1.row_order, s32[4]{0:T(128)} %pad_add_fusion.1.units, bf16[512,4096]{1,0:T(8,128)(2,1)} %get-tuple-element.179.refs_0_.refs_1_.act, bf16[512,4096]{1,0:T(8,128)(2,1)} %get-tuple-element.179.refs_0_.refs_1_.act, ...), custom_call_target="tpu_custom_call" | custom-call | flops 536870912 | bytes 2228224 | tf_op jit(solution)/shard_map/wgrad/pallas_call | solution.py:877
  164.4 5.1 %all-to-all-done.3 = bf16[8,512,128]{2,1,0:T(8,128)(2,1)} async-done(((bf16[8,512,128]{2,1,0:T(8,128)(2,1)}), bf16[8,512,128]{2,1,0:T(8,128)(2,1)}, u32[]{:S(2)}, u32[]{:S(2)}) %all-to-all-start.3) | async-done | bytes 1048608 | tf_op jit(solution)/shard_map/all_to_all | solution.py:948
  169.5 10.1 %correlate.1 = (bf16[8,528,128]{2,1,0:T(8,128)(2,1)}, bf16[32,256,128]{2,1,0:T(8,128)(2,1)}) custom-call(bf16[32,128,128]{2,1,0:T(8,128)(2,1)} %bitcast.24.refs_0_.refs_2_, bf16[32,256,128]{2,1,0:T(8,128)(2,1)} %spectrum.1.refs_1_, f32[1,128]{1,0:T(1,128)} %bitcast.131, bf16[32,256,256]{2,1,0:T(8,128)(2,1)} %get-tuple-element.114.refs_1_.refs_3_, ...), custom_call_target="tpu_custom_call" | custom-call | flops 536870912 | bytes 2097152 | tf_op jit(solution)/shard_map/correlate/pallas_call | solution.py:279
  187.2 11.0 %wgrad.6 = (bf16[4,128,512]{2,1,0:T(8,128)(2,1)}, bf16[4,128,1024]{2,1,0:T(8,128)(2,1)}, bf16[4,128,512]{2,1,0:T(8,128)(2,1)}, bf16[4,128,2048]{2,1,0:T(8,128)(2,1)}) custom-call(s32[8]{0:T(128)} %broadcast_xor_fusion.row_order, s32[4]{0:T(128)} %pad_add_fusion.1.units, bf16[512,1024]{1,0:T(8,128)(2,1)} %get-tuple-element.142.refs_0_.refs_1_.refs_2_.refs_3_, ...), custom_call_target="tpu_custom_call" | custom-call | flops 536870912 | bytes 1835008 | tf_op jit(solution)/shard_map/wgrad/pallas_call | solution.py:877
  198.1 11.2 %filter_grad.1 = (f32[64,128]{1,0:T(8,128)}, f32[48,64]{1,0:T(8,128)}, f32[64,2]{1,0:T(8,128)}, f32[1,128]{1,0:T(1,128)}) custom-call(bf16[32,256,128]{2,1,0:T(8,128)(2,1)} %get-tuple-element.139.refs_0_, bf16[32,256,128]{2,1,0:T(8,128)(2,1)} %get-tuple-element.140.refs_1_, bf16[32,128,128]{2,1,0:T(8,128)(2,1)} %bitcast.24.refs_0_.refs_2_, ...), custom_call_target="tpu_custom_call" | custom-call | flops 536870912 | bytes 2097152 | tf_op jit(solution)/shard_map/filter_grad/pallas_call | solution.py:279
  211.4 11.8 %leave.1 = (bf16[3,4,512,256]{3,2,1,0:T(8,128)(2,1)}, f32[16,1024]{1,0:T(8,128)}) custom-call(bf16[8,528,128]{2,1,0:T(8,128)(2,1)} %copy-done.11, bf16[512,1024]{1,0:T(8,128)(2,1)} %get-tuple-element.137.ggate, bf16[16,1024]{1,0:T(8,128)(2,1)} %copy-done.19, bf16[3,528,1024]{2,1,0:T(8,128)(2,1)} %get-tuple-element.117.proj, ...), custom_call_target="tpu_custom_call" | custom-call | flops 3932160 | bytes 1179648 | tf_op jit(solution)/shard_map/leave/pallas_call | solution.py:753
  236.2 11.3 %tokens_back.1 = (f32[512,1024]{1,0:T(8,128)}, f32[2,1024]{1,0:T(2,128)}) custom-call(bf16[3,4,512,256]{3,2,1,0:T(8,128)(2,1)} %get-tuple-element.155.gproj, bf16[1024,3072]{1,0:T(8,128)(2,1)} %weight.1, bf16[512,1024]{1,0:T(8,128)(2,1)} %bitcast.95, bf16[512,1024]{1,0:T(8,128)(2,1)} %get-tuple-element.129.gres, f32[1,1024]{1,0:T(1,128)} %bitcast.120), custom_call_target="tpu_custom_call" | custom-call | flops 402653184 | bytes 1835008 | tf_op jit(solution)/shard_map/tokens_back/pallas_call | solution.py:801
  253.7 10.2 %all-to-all-done.5.refs_4_.refs_5_.refs_6_.refs_11_.refs_12_.refs_13_.refs_18_.refs_19_.refs_20_.refs_25_.refs_26_.refs_27_ = bf16[12,512,256]{2,1,0:T(8,128)(2,1)S(1)} async-done(((bf16[12,512,256]{2,1,0:T(8,128)(2,1)}), bf16[12,512,256]{2,1,0:T(8,128)(2,1)S(1)}, u32[]{:S(2)}, u32[]{:S(2)}) %all-to-all-start.5) | async-done | bytes 3145760 | tf_op jit(solution)/shard_map/all_to_all | solution.py:1021
  266.3 9.0 %wgrad.7 = (bf16[4,128,768]{2,1,0:T(8,128)(2,1)}, bf16[4,128,768]{2,1,0:T(8,128)(2,1)}) custom-call(s32[8]{0:T(128)} %broadcast_xor_fusion.1.row_order, s32[12]{0:T(128)} %pad_add_fusion.units, bf16[512,1024]{1,0:T(8,128)(2,1)} %get-tuple-element.121.refs_0_.refs_1_.refs_2_.refs_3_, bf16[512,1024]{1,0:T(8,128)(2,1)} %get-tuple-element.121.refs_0_.refs_1_.refs_2_.refs_3_, ...), custom_call_target="tpu_custom_call" | custom-call | flops 402653184 | bytes 1310720 | tf_op jit(solution)/shard_map/wgrad/pallas_call | solution.py:877
  285.5 9.9 %block_out.1 = bf16[512,1024]{1,0:T(8,128)(2,1)} custom-call(bf16[512,4096]{1,0:T(8,128)(2,1)} %get-tuple-element.179.refs_0_.refs_1_.act, bf16[4096,1024]{1,0:T(8,128)(2,1)} %down.3, bf16[512,1024]{1,0:T(8,128)(2,1)} %get-tuple-element.180.resid, f32[1,1024]{1,0:T(1,128)} %bitcast.129), custom_call_target="tpu_custom_call" | custom-call | flops 536870912 | bytes 1966080 | tf_op jit(solution)/shard_map/block_out/pallas_call | solution.py:510
  302.7 10.6 %collective-permute-done.27 = bf16[1,640,256]{2,1,0:T(8,128)(2,1)S(1)} collective-permute-done((bf16[1,640,256]{2,1,0:T(8,128)(2,1)S(1)}, bf16[1,640,256]{2,1,0:T(8,128)(2,1)S(1)}, u32[]{:S(2)}, u32[]{:S(2)}) %collective-permute-start.27) | collective-permute-done | bytes 327712 | tf_op jit(solution)/shard_map/ppermute | solution.py:416
  321.6 8.1 %collective-permute-done.26 = bf16[1,128,768]{2,1,0:T(8,128)(2,1)S(1)} collective-permute-done((bf16[1,128,768]{2,1,0:T(8,128)(2,1)S(1)}, bf16[1,128,768]{2,1,0:T(8,128)(2,1)S(1)}, u32[]{:S(2)}, u32[]{:S(2)}) %collective-permute-start.26) | collective-permute-done | bytes 196640 | tf_op jit(solution)/shard_map/ppermute | solution.py:416
  333.8 10.9 %collective-permute-done.25 = f32[232,128]{1,0:T(8,128)S(1)} collective-permute-done((f32[232,128]{1,0:T(8,128)S(1)}, f32[232,128]{1,0:T(8,128)S(1)}, u32[]{:S(2)}, u32[]{:S(2)}) %collective-permute-start.25) | collective-permute-done | bytes 118816 | tf_op jit(solution)/shard_map/ppermute | solution.py:416
  (203 shorter events, 100.8 us)
Async XLA Ops:
  3.5 14.6 %all-to-all-start = ((f32[8,32,128]{2,1,0:T(8,128)}), f32[8,32,128]{2,1,0:T(8,128)S(1)}, u32[]{:S(2)}, u32[]{:S(2)}) async-start(f32[8,32,128]{2,1,0:T(8,128)} %broadcast_in_dim.60), calls=%async_computation | async-start | bytes 262144 | tf_op jit(solution)/shard_map/all_to_all | solution.py:927
  32.5 32.1 %all-to-all-start.1 = ((bf16[8,512,128]{2,1,0:T(8,128)(2,1)}), bf16[8,512,128]{2,1,0:T(8,128)(2,1)S(1)}, u32[]{:S(2)}, u32[]{:S(2)}) async-start(bf16[8,512,128]{2,1,0:T(8,128)(2,1)} %get-tuple-element.113), calls=%async_computation.1 | async-start | bytes 2097152 | tf_op jit(solution)/shard_map/all_to_all | solution.py:948
  38.5 37.0 %collective-permute-start.1 = (bf16[512,1024]{1,0:T(8,128)(2,1)S(1)}, bf16[512,1024]{1,0:T(8,128)(2,1)S(1)}, u32[]{:S(2)}, u32[]{:S(2)}) collective-permute-start(bf16[512,1024]{1,0:T(8,128)(2,1)S(1)} %copy-done.5), channel_id=1, source_target_pairs={{0,16},{8,24},{16,0},{24,8},{1,17},{9,25},{17,1},{25,9},{2,18},{10... | collective-permute-start | bytes 3145736 | tf_op jit(solution)/shard_map/ppermute | solution.py:416
  56.9 18.6 %collective-permute-start = (bf16[3,16,1024]{2,1,0:T(8,128)(2,1)}, bf16[3,16,1024]{2,1,0:T(8,128)(2,1)}, u32[]{:S(2)}, u32[]{:S(2)}) collective-permute-start(bf16[3,16,1024]{2,1,0:T(8,128)(2,1)} %slice.233), channel_id=1, source_target_pairs={{1,0},{2,1},{3,2},{4,3},{5,4},{6,5},{7,6},{9,8},{10,9},{11,10},{12... | collective-permute-start | bytes 294920 | tf_op jit(solution)/shard_map/ppermute | solution.py:943
  75.6 32.2 %all-to-all-start.2 = ((bf16[8,512,128]{2,1,0:T(8,128)(2,1)}), bf16[8,512,128]{2,1,0:T(8,128)(2,1)}, u32[]{:S(2)}, u32[]{:S(2)}) async-start(bf16[8,512,128]{2,1,0:T(8,128)(2,1)} %get-tuple-element.119), calls=%async_computation.2 | async-start | bytes 2097152 | tf_op jit(solution)/shard_map/all_to_all | solution.py:952
  138.4 41.3 %collective-permute-start.5 = (bf16[1,512,4096]{2,1,0:T(8,128)(2,1)}, bf16[1,512,4096]{2,1,0:T(8,128)(2,1)}, u32[]{:S(2)}, u32[]{:S(2)}) collective-permute-start(bf16[1,512,4096]{2,1,0:T(8,128)(2,1)} %bitcast.89), channel_id=1, source_target_pairs={{0,8},{8,0},{16,24},{24,16},{1,9},{9,1},{17,25},{25,17},{2,10},{10... | collective-permute-start | bytes 12582920 | tf_op jit(solution)/shard_map/ppermute | solution.py:416
  138.8 30.7 %all-to-all-start.3 = ((bf16[8,512,128]{2,1,0:T(8,128)(2,1)}), bf16[8,512,128]{2,1,0:T(8,128)(2,1)}, u32[]{:S(2)}, u32[]{:S(2)}) async-start(bf16[8,512,128]{2,1,0:T(8,128)(2,1)} %get-tuple-element.127), calls=%async_computation.3 | async-start | bytes 2097152 | tf_op jit(solution)/shard_map/all_to_all | solution.py:948
  143.8 35.8 %collective-permute-start.6 = (bf16[512,1024]{1,0:T(8,128)(2,1)S(1)}, bf16[512,1024]{1,0:T(8,128)(2,1)}, u32[]{:S(2)}, u32[]{:S(2)}) collective-permute-start(bf16[512,1024]{1,0:T(8,128)(2,1)S(1)} %copy-done.8), channel_id=1, source_target_pairs={{0,8},{8,0},{16,24},{24,16},{1,9},{9,1},{17,25},{25,17},{2,10},{10... | collective-permute-start | bytes 3145736 | tf_op jit(solution)/shard_map/ppermute | solution.py:416
  161.6 61.7 %collective-permute-start.11 = (bf16[8,640,256]{2,1,0:T(8,128)(2,1)}, bf16[8,640,256]{2,1,0:T(8,128)(2,1)}, u32[]{:S(2)}, u32[]{:S(2)}) collective-permute-start(bf16[8,640,256]{2,1,0:T(8,128)(2,1)} %get-tuple-element.153), channel_id=1, source_target_pairs={{0,16},{8,24},{16,0},{24,8},{1,17},{9,25},{17,1},{25,9},{2,18},{10... | collective-permute-start | bytes 7864328 | tf_op jit(solution)/shard_map/ppermute | solution.py:416
  163.1 16.5 %collective-permute-start.10 = (bf16[16,1024]{1,0:T(8,128)(2,1)S(1)}, bf16[16,1024]{1,0:T(8,128)(2,1)S(1)}, u32[]{:S(2)}, u32[]{:S(2)}) collective-permute-start(bf16[16,1024]{1,0:T(8,128)(2,1)S(1)} %slice.234), channel_id=1, source_target_pairs={{1,0},{2,1},{3,2},{4,3},{5,4},{6,5},{7,6},{9,8},{10,9},{11,10},{12... | collective-permute-start | bytes 98312 | tf_op jit(solution)/shard_map/ppermute | solution.py:980
  179.7 30.3 %all-to-all-start.4 = ((bf16[8,528,128]{2,1,0:T(8,128)(2,1)}), bf16[8,528,128]{2,1,0:T(8,128)(2,1)S(1)}, u32[]{:S(2)}, u32[]{:S(2)}) async-start(bf16[8,528,128]{2,1,0:T(8,128)(2,1)} %get-tuple-element.138), calls=%async_computation.4 | async-start | bytes 2162688 | tf_op jit(solution)/shard_map/all_to_all | solution.py:952
  210.0 13.3 %collective-permute-start.12 = (bf16[4,128,512]{2,1,0:T(8,128)(2,1)S(1)}, bf16[4,128,512]{2,1,0:T(8,128)(2,1)}, u32[]{:S(2)}, u32[]{:S(2)}) collective-permute-start(bf16[4,128,512]{2,1,0:T(8,128)(2,1)S(1)} %copy-done.29), channel_id=1, source_target_pairs={{0,2},{1,3},{2,0},{3,1},{4,6},{5,7},{6,4},{7,5},{8,10},{9,11},{10,... | collective-permute-start | bytes 1572872 | tf_op jit(solution)/shard_map/ppermute | solution.py:416
  223.3 40.6 %all-to-all-start.5 = ((bf16[12,512,256]{2,1,0:T(8,128)(2,1)}), bf16[12,512,256]{2,1,0:T(8,128)(2,1)S(1)}, u32[]{:S(2)}, u32[]{:S(2)}) async-start(bf16[12,512,256]{2,1,0:T(8,128)(2,1)} %bitcast.92), calls=%async_computation.5 | async-start | bytes 6291456 | tf_op jit(solution)/shard_map/all_to_all | solution.py:1021
  227.3 26.4 %collective-permute-start.14 = (bf16[4,128,1024]{2,1,0:T(8,128)(2,1)}, bf16[4,128,1024]{2,1,0:T(8,128)(2,1)}, u32[]{:S(2)}, u32[]{:S(2)}) collective-permute-start(bf16[4,128,1024]{2,1,0:T(8,128)(2,1)} %get-tuple-element.165), channel_id=1, source_target_pairs={{0,2},{1,3},{2,0},{3,1},{4,6},{5,7},{6,4},{7,5},{8,10},{9,11},{10,... | collective-permute-start | bytes 3145736 | tf_op jit(solution)/shard_map/ppermute | solution.py:416
  233.8 41.5 %collective-permute-start.16 = (bf16[4,640,256]{2,1,0:T(8,128)(2,1)}, bf16[4,640,256]{2,1,0:T(8,128)(2,1)}, u32[]{:S(2)}, u32[]{:S(2)}) collective-permute-start(bf16[4,640,256]{2,1,0:T(8,128)(2,1)} %get-tuple-element.200), channel_id=1, source_target_pairs={{0,1},{1,0},{2,3},{3,2},{4,5},{5,4},{6,7},{7,6},{8,9},{9,8},{10,11... | collective-permute-start | bytes 3932168 | tf_op jit(solution)/shard_map/ppermute | solution.py:416
  235.5 39.7 %collective-permute-start.17 = (bf16[4,128,512]{2,1,0:T(8,128)(2,1)}, bf16[4,128,512]{2,1,0:T(8,128)(2,1)}, u32[]{:S(2)}, u32[]{:S(2)}) collective-permute-start(bf16[4,128,512]{2,1,0:T(8,128)(2,1)} %get-tuple-element.176), channel_id=1, source_target_pairs={{0,2},{1,3},{2,0},{3,1},{4,6},{5,7},{6,4},{7,5},{8,10},{9,11},{10,... | collective-permute-start | bytes 1572872 | tf_op jit(solution)/shard_map/ppermute | solution.py:416
  275.2 20.5 %collective-permute-start.18 = (bf16[4,128,768]{2,1,0:T(8,128)(2,1)}, bf16[4,128,768]{2,1,0:T(8,128)(2,1)}, u32[]{:S(2)}, u32[]{:S(2)}) collective-permute-start(bf16[4,128,768]{2,1,0:T(8,128)(2,1)} %get-tuple-element.177), channel_id=1, source_target_pairs={{0,1},{1,0},{2,3},{3,2},{4,5},{5,4},{6,7},{7,6},{8,9},{9,8},{10,11... | collective-permute-start | bytes 2359304 | tf_op jit(solution)/shard_map/ppermute | solution.py:416
  279.3 16.4 %collective-permute-start.19 = (bf16[2,640,256]{2,1,0:T(8,128)(2,1)}, bf16[2,640,256]{2,1,0:T(8,128)(2,1)}, u32[]{:S(2)}, u32[]{:S(2)}) collective-permute-start(bf16[2,640,256]{2,1,0:T(8,128)(2,1)} %get-tuple-element.202), channel_id=1, source_target_pairs={{0,2},{1,3},{2,0},{3,1},{4,6},{5,7},{6,4},{7,5},{8,10},{9,11},{10,... | collective-permute-start | bytes 1966088 | tf_op jit(solution)/shard_map/ppermute | solution.py:416
  285.1 30.7 %collective-permute-start.21 = (bf16[4,128,1024]{2,1,0:T(8,128)(2,1)}, bf16[4,128,1024]{2,1,0:T(8,128)(2,1)S(1)}, u32[]{:S(2)}, u32[]{:S(2)}) collective-permute-start(bf16[4,128,1024]{2,1,0:T(8,128)(2,1)} %get-tuple-element.205), channel_id=1, source_target_pairs={{0,16},{8,24},{16,0},{24,8},{1,17},{9,25},{17,1},{25,9},{2,18},{10... | collective-permute-start | bytes 3145736 | tf_op jit(solution)/shard_map/ppermute | solution.py:416
  296.8 16.5 %collective-permute-start.27 = (bf16[1,640,256]{2,1,0:T(8,128)(2,1)S(1)}, bf16[1,640,256]{2,1,0:T(8,128)(2,1)S(1)}, u32[]{:S(2)}, u32[]{:S(2)}) collective-permute-start(bf16[1,640,256]{2,1,0:T(8,128)(2,1)S(1)} %add_convert_fusion.10), channel_id=1, source_target_pairs={{0,4},{1,5},{2,6},{3,7},{4,0},{5,1},{6,2},{7,3},{8,12},{9,13},{10,... | collective-permute-start | bytes 983048 | tf_op jit(solution)/shard_map/ppermute | solution.py:416
  299.2 16.6 %collective-permute-start.22 = (f32[304,128]{1,0:T(8,128)S(1)}, f32[304,128]{1,0:T(8,128)S(1)}, u32[]{:S(2)}, u32[]{:S(2)}) collective-permute-start(f32[304,128]{1,0:T(8,128)S(1)} %pad_maximum_fusion.3), channel_id=1, source_target_pairs={{0,16},{8,24},{16,0},{24,8},{1,17},{9,25},{17,1},{25,9},{2,18},{10... | collective-permute-start | bytes 466952 | tf_op jit(solution)/shard_map/ppermute | solution.py:416
  302.0 15.7 %collective-permute-start.20 = (bf16[2,128,768]{2,1,0:T(8,128)(2,1)S(1)}, bf16[2,128,768]{2,1,0:T(8,128)(2,1)S(1)}, u32[]{:S(2)}, u32[]{:S(2)}) collective-permute-start(bf16[2,128,768]{2,1,0:T(8,128)(2,1)S(1)} %get-tuple-element.208), channel_id=1, source_target_pairs={{0,2},{1,3},{2,0},{3,1},{4,6},{5,7},{6,4},{7,5},{8,10},{9,11},{10,... | collective-permute-start | bytes 1179656 | tf_op jit(solution)/shard_map/ppermute | solution.py:416
  330.7 14.0 %collective-permute-start.25 = (f32[232,128]{1,0:T(8,128)S(1)}, f32[232,128]{1,0:T(8,128)S(1)}, u32[]{:S(2)}, u32[]{:S(2)}) collective-permute-start(f32[232,128]{1,0:T(8,128)S(1)} %slice_add_fusion), channel_id=1, source_target_pairs={{0,4},{1,5},{2,6},{3,7},{4,0},{5,1},{6,2},{7,3},{8,12},{9,13},{10,... | collective-permute-start | bytes 356360 | tf_op jit(solution)/shard_map/ppermute | solution.py:416
  330.8 18.3 %collective-permute-start.28 = (bf16[1,128,1024]{2,1,0:T(8,128)(2,1)S(1)}, bf16[1,128,1024]{2,1,0:T(8,128)(2,1)S(1)}, u32[]{:S(2)}, u32[]{:S(2)}) collective-permute-start(bf16[1,128,1024]{2,1,0:T(8,128)(2,1)S(1)} %add_convert_fusion.12), channel_id=1, source_target_pairs={{0,4},{1,5},{2,6},{3,7},{4,0},{5,1},{6,2},{7,3},{8,12},{9,13},{10,... | collective-permute-start | bytes 786440 | tf_op jit(solution)/shard_map/ppermute | solution.py:416
  (43 other events, 419.0 us)

commit v4 on v3

--- a/solution.py
+++ b/solution.py
@@ -15,7 +15,7 @@
 BLOCK = 128
 LANES = 128
 ROWS = 16
-CHUNK = 64
+CHUNK = 128
 GRANT = 60 << 20
 COST = 8
 F32 = jnp.float32
@@ -921,15 +921,15 @@
     down_shift = [(i + 1, i) for i in range(seq - 1)]
 
     x, dy = tokens[0], cotangent[0]
-    mine = jnp.concatenate([short_weight.reshape(9 * chans), short_bias.reshape(3 * chans), x[rows - 2 :].reshape(-1).astype(F32)])
-    used = mine.size
-    mine = jnp.pad(mine, (0, -used % (8 * LANES)))
+    edge = 2 * width // chans
+    mine = jnp.concatenate(
+        [short_weight.reshape(9, chans), short_bias, x[rows - 2 :].astype(F32).reshape(edge, chans)], axis=0
+    )
     got = lax.all_to_all(
-        jnp.broadcast_to(mine.reshape(1, -1, LANES), (seq, mine.size // LANES, LANES)),
-        "seq", split_axis=0, concat_axis=0, tiled=True,
-    ).reshape(seq, -1)
-    all_taps = got[:, : 12 * chans].reshape(seq, 12, chans).transpose(1, 0, 2).reshape(12, width)
-    before = pick(got, jnp.maximum(me - 1, 0), 0)[12 * chans : used].reshape(2, width)
+        jnp.broadcast_to(mine[None], (seq, 12 + edge, chans)), "seq", split_axis=0, concat_axis=0, tiled=True
+    ).reshape(seq, 12 + edge, chans)
+    all_taps = got[:, :12].transpose(1, 0, 2).reshape(12, width)
+    before = pick(got, jnp.maximum(me - 1, 0), 0)[12:].reshape(2, width)
     before = jnp.concatenate([jnp.zeros((PRE - 2, width), BF16), before.astype(BF16)], axis=0)
 
     row = lambda v: v[None, :]
@@ -1016,10 +1016,11 @@
     grad_proj, leave_sums = leave(grad_inner, grad_gate, gate_after, proj, proj_after, all_taps)
     grad_proj, tall_got, up_gots[0] = tie(grad_proj, tall_got, up_gots[0])
     tall_send, tall_kept = halve(tall_kept, tall_got)
-    tall_got = swap(tall_send, "seq", bits[0])
     proj_units = grad_proj.reshape((-1,) + grad_proj.shape[2:])
     proj_all = lax.all_to_all(proj_units, "dp", split_axis=0, concat_axis=0, tiled=True)
     up_gots.append(swap(up_sends[1], "seq", up_bits[0]))
+    grad_proj, tall_send = tie(grad_proj, tall_send)
+    tall_got = swap(tall_send, "seq", bits[0])
     grad_tokens, token_sums = tokens_back(grad_proj, in_weight, x, grad_attn, row(norm1_gain))
 
     shared = (token_sums, leave_sums, mid_sums, gup_sum, dy_sum, grad_filter_in, grad_filter_in_bias, grad_freq)
@@ -1028,56 +1029,55 @@
     rows_shared = packed.shape[0]
     packed = jnp.concatenate([packed, extra], axis=0)
     packed = packed + swap(packed, "dp", 1)
-    packed, up_gots[1], proj_all = tie(packed, up_gots[1], proj_all)
-    packed, extra = packed[:rows_shared], packed[rows_shared:]
+    packed, up_gots[1] = tie(packed, up_gots[1])
+    small = swap(packed, "dp", 2)
     up_gots.append(swap(up_sends[2], "seq", up_bits[0]))
-    small = swap(packed, "seq", bits[0])
+    cut = ff // 4
+    part = up_gots[1].shape[2] // 2
+    up_send = add(up_kept[..., :cut], jnp.concatenate([up_gots[0], up_gots[1][..., :part]], axis=2))
+    up_send, act = tie(up_send, act)
+    up_got = swap(up_send, "dp", 2)
+    block_output = block_out(act, down_weight, resid, row(down_bias))
+    block_output, proj_all = tie(block_output, proj_all)
     dp_me = lax.axis_index("dp")
     share = proj_units.shape[0] // 4
     ahead = jnp.arange(share, dtype=jnp.int32)
     in_units = [jnp.bitwise_xor(dp_me, w) * share + ahead for w in range(4)]
     in_send, in_kept = wgrad(normed_all, [proj_all] * 4, order, in_units, proj_units.shape[2], "y", 4)
 
-    in_send, small, tall_got, up_gots, act = tie(in_send, small, tall_got, up_gots, act)
+    in_send, tall_got, up_gots = tie(in_send, tall_got, up_gots)
     in_got = swap(in_send, "seq", bits[0])
-    cut = ff // 4
-    part = up_gots[1].shape[2] // 2
-    up_send = add(up_kept[..., :cut], jnp.concatenate([up_gots[0], up_gots[1][..., :part]], axis=2))
-    up_got = swap(up_send, "dp", 2)
     tall_send, tall_kept = halve(tall_kept, tall_got)
     tall_got = swap(tall_send, "seq", bits[1])
-    both = jnp.concatenate([packed + small, extra], axis=0)
-    small = swap(both, "dp", 2)
-    block_output = block_out(act, down_weight, resid, row(down_bias))
     up_kept = add(up_kept[..., cut:], jnp.concatenate([up_gots[1][..., part:], up_gots[2]], axis=2))
-
-    in_got, tall_got, block_output, up_kept = tie(in_got, tall_got, block_output, up_kept)
+    up_got, up_kept, tall_send, small = tie(up_got, up_kept, tall_send, small)
+    up_send, up_kept = halve(up_kept, up_got)
+    up_got = swap(up_send, "seq", up_bits[1])
+    packed = packed + small
+    packed, extra = packed[:rows_shared], packed[rows_shared:]
+    small = swap(packed, "seq", bits[0])
+
+    in_got, tall_got, up_send, small = tie(in_got, tall_got, up_send, small)
     in_send, in_kept = halve(in_kept, in_got)
     in_got = swap(in_send, "seq", bits[1])
     tall_send, tall_kept = halve(tall_kept, tall_got)
     tall_got = swap(tall_send, "seq", bits[2])
-
-    in_got, up_got, small = tie(in_got, up_got, small)
-    in_send, in_kept = halve(in_kept, in_got)
-    in_got = swap(in_send, "seq", bits[2])
-    up_send, up_kept = halve(up_kept, up_got)
-    up_got = swap(up_send, "seq", up_bits[1])
-    both = both + small
-    packed, extra = both[:rows_shared], both[rows_shared:]
+    packed = packed + small
     small = swap(packed, "seq", bits[1])
 
     for i in range(2, len(bits)):
-        up_got, small = tie(up_got, small)
+        in_send, up_got = tie(in_send, up_got)
+        up_send, up_kept = halve(up_kept, up_got)
+        up_got = swap(up_send, "seq", up_bits[i])
+        in_got, tall_got, up_send, small = tie(in_got, tall_got, up_send, small)
         if i > 2:
-            in_got, tall_got = tie(in_got, tall_got)
-            in_send, in_kept = halve(in_kept, in_got)
-            in_got = swap(in_send, "seq", bits[i])
             tall_send, tall_kept = halve(tall_kept, tall_got)
             tall_got = swap(tall_send, "seq", bits[i])
-        up_send, up_kept = halve(up_kept, up_got)
-        up_got = swap(up_send, "seq", up_bits[i])
+        in_send, in_kept = halve(in_kept, in_got)
+        in_got = swap(in_send, "seq", bits[i])
         packed = packed + small
         small = swap(packed, "seq", bits[i])
+    up_got, in_got, small = tie(up_got, in_got, small)
     grad_up, packed = last(up_kept, up_got), packed + small
     grad_in, both = last(in_kept, in_got), last(tall_kept, tall_got)
     grad_down, grad_out_weight = both[:wide], both[wide:]

time: 352 us -> 347 us (0.986)
  waiting for transfers between devices: 67.8 us -> 61.9 us
  starting transfers between devices: 58.7 us -> 63.3 us
    all_to_all x1, waiting for transfers between devices: 10.2 us -> 0.01 us  [on_device(): lax.all_to_all(proj_units, 'dp', split_axis=0, concat_axis=0, tiled=True)]
    ppermute x27, starting transfers between devices: 24 us -> 28.5 us  [swap(): return lax.ppermute(value, axis, [(i, i ^ bit) for i in range(size)])]
    ppermute x27, waiting for transfers between devices: 37.8 us -> 42.2 us  [swap(): return lax.ppermute(value, axis, [(i, i ^ bit) for i in range(size)])]
    convert_element_type x8 -> x9, other arithmetic: 13.6 us -> 12.7 us  [add(): return (left.astype(F32) + right.astype(F32)).astype(BF16)]
  transfers between devices with their start and end apart: 35 -> 35, of which waited for: 15 -> 15; matrix products, arithmetic and copies ran while one was open for 14% -> 12% of each run, Pallas kernels for 35% -> 35%
where the time goes in v4:
time: 347 us; the launch traced here: 345 us
  Pallas kernels  163 us (47%)
  starting transfers between devices  63.3 us (18%)
  waiting for transfers between devices  61.9 us (18%)
  other arithmetic  21.9 us (6%)
  local copies, waits for them, and re-layouts  20 us (6%)
  matrix products  14.2 us (4%)
    ppermute x27, waiting for transfers between devices, swap(): return lax.ppermute(value, axis, [(i, i ^ bit) for i in range(size)])  42.2 us
    pallas_call x4, Pallas kernels, vmem_call(): pl.pallas_call(body, in_specs=[pl.BlockSpec(memory_space=pl.ANY)] * count...  37.7 us
    pallas_call x4, Pallas kernels, wgrad(): pl.pallas_call(functools.partial(wgrad_kernel, sides=sides, lefts=lefts,...  34.7 us
    pallas_call x1, Pallas kernels, middle(): pl.pallas_call(middle_kernel, grid=(ff // block,), in_specs=[whole(nb, ro...  29.4 us
    ppermute x27, starting transfers between devices, swap(): return lax.ppermute(value, axis, [(i, i ^ bit) for i in range(size)])  28.5 us
    all_to_all x2, waiting for transfers between devices, to_tokens(): got = lax.all_to_all(value, 'seq', split_axis=0, concat_axis=0, tiled=True)  13.4 us
    convert_element_type x9, other arithmetic, add(): return (left.astype(F32) + right.astype(F32)).astype(BF16)  12.7 us
    pallas_call x1, Pallas kernels, enter(): pl.pallas_call(enter_kernel, grid=(steps,), in_specs=[pl.BlockSpec(memory...  11.9 us
  transfers between devices with their start and end apart: 35, of which 15 were waited for; matrix products, arithmetic and copies ran while one was open for 12% of the time, Pallas kernels for 35%

profile of v4, /device:TPU:0, one launch (start us, length us, event | category | flops | bytes accessed | tf_op | source)
XLA Modules:
  0.0 345.1 jit_solution(15933583155308555472)
XLA Ops:
  3.5 7.3 %all-to-all-start = ((f32[8,28,128]{2,1,0:T(8,128)}), f32[8,28,128]{2,1,0:T(8,128)S(1)}, u32[]{:S(2)}, u32[]{:S(2)}) async-start(f32[8,28,128]{2,1,0:T(8,128)} %broadcast_in_dim.58), calls=%async_computation | async-start | bytes 262144 | tf_op jit(solution)/shard_map/all_to_all | solution.py:928
  10.8 6.2 %tables.1 = (bf16[32,256,256]{2,1,0:T(8,128)(2,1)}, bf16[32,256,256]{2,1,0:T(8,128)(2,1)}) custom-call(f32[32,1,128]{2,1,0:T(1,128)} %constant.59.clone.alpha_cos, f32[32,1,128]{2,1,0:T(1,128)} %constant.60.clone.alpha_sin, f32[128,128]{1,0:T(8,128)} %constant.61.clone.beta_cos, f32[128,128]{1,0:T(8,128)} %constant.62.clone.beta_sin), custom_call_target="tpu_custom_call" | custom-call | flops 1048576 | bytes 1048576 | tf_op jit(solution)/shard_map/tables/pallas_call | solution.py:145
  19.4 11.9 %enter.1 = (bf16[8,512,128]{2,1,0:T(8,128)(2,1)}, bf16[512,1024]{1,0:T(8,128)(2,1)}, bf16[3,528,1024]{2,1,0:T(8,128)(2,1)}, bf16[512,1024]{1,0:T(8,128)(2,1)}) custom-call(s32[1]{0:T(128)} %bitcast.2.first, bf16[512,1024]{1,0:T(8,128)(2,1)} %bitcast.79, bf16[16,1024]{1,0:T(8,128)(2,1)} %concatenate.39.before, f32[1,1024]{1,0:T(1,128)} %bitcast.101, ...), custom_call_target="tpu_custom_call" | custom-call | flops 402653184 | bytes 1835008 | tf_op jit(solution)/shard_map/enter/pallas_call | solution.py:681
  39.1 5.8 %multiply_cosine_fusion = (f32[64,4096]{1,0:T(8,128)}, bf16[64,4096]{1,0:T(8,128)(2,1)}, f32[64,4096]{1,0:T(8,128)S(1)}) fusion(f32[64]{0:T(128)S(1)} %copy-done.24, f32[64]{0:T(128)S(1)} %copy-done.27, f32[33,64]{1,0:T(8,128)S(1)} %copy-done, f32[16,4096]{1,0:T(8,128)S(1)} %get-tuple-element.230, f32[16,4096]{1,0:T(8,128)S(1)} %get-tuple-element.229, ...), kind=kOutput, calls=%fused_computation.12 | convolution fusion | flops 104865792 | bytes 3171072 | tf_op jit(solution)/shard_map/dot_general | solution.py:961
  46.0 8.3 %convolution_multiply_fusion = f32[4096,128]{1,0:T(8,128)} fusion(f32[64,128]{1,0:T(8,128)S(1)} %copy-done.16, f32[64,4096]{1,0:T(8,128)S(1)} %get-tuple-element.231.refs_8_, f32[128]{0:T(128)S(1)} %copy-done.26, f32[4096]{0:T(1024)S(1)} %multiply_negate_fusion, f32[64]{0:T(128)S(1)} %copy-done.24), kind=kOutput, calls=%fused_computation | convolution fusion | flops 403963904 | bytes 3195648 | tf_op jit(solution)/shard_map/hn,hc->nc/dot_general | solution.py:965
  57.1 6.4 %spectrum.1.refs_1_ = bf16[32,256,128]{2,1,0:T(8,128)(2,1)} custom-call(f32[32,128,128]{2,1,0:T(8,128)} %bitcast.87, bf16[32,256,256]{2,1,0:T(8,128)(2,1)} %get-tuple-element.120.refs_1_.refs_3_), custom_call_target="tpu_custom_call" | custom-call | flops 536870912 | bytes 2097152 | tf_op jit(solution)/shard_map/spectrum/pallas_call | solution.py:279
  64.5 10.0 %convolve.1 = (bf16[8,512,128]{2,1,0:T(8,128)(2,1)}, bf16[32,256,128]{2,1,0:T(8,128)(2,1)}) custom-call(bf16[32,128,128]{2,1,0:T(8,128)(2,1)} %bitcast.82, bf16[32,256,128]{2,1,0:T(8,128)(2,1)} %spectrum.1.refs_1_, f32[1,128]{1,0:T(1,128)} %bitcast.112, bf16[32,256,256]{2,1,0:T(8,128)(2,1)} %get-tuple-element.120.refs_1_.refs_3_, ...), custom_call_target="tpu_custom_call" | custom-call | flops 536870912 | bytes 2097152 | tf_op jit(solution)/shard_map/convolve/pallas_call | solution.py:279
  74.5 7.8 %all-to-all-start.2 = ((bf16[8,512,128]{2,1,0:T(8,128)(2,1)}), bf16[8,512,128]{2,1,0:T(8,128)(2,1)}, u32[]{:S(2)}, u32[]{:S(2)}) async-start(bf16[8,512,128]{2,1,0:T(8,128)(2,1)} %get-tuple-element.125), calls=%async_computation.2 | async-start | bytes 2097152 | tf_op jit(solution)/shard_map/all_to_all | solution.py:952
  82.9 10.9 %back_act.1 = (bf16[512,4096]{1,0:T(8,128)(2,1)}, f32[1,1024]{1,0:T(1,128)}) custom-call(bf16[512,1024]{1,0:T(8,128)(2,1)} %bitcast.12.dy, bf16[4096,1024]{1,0:T(8,128)(2,1)} %down.3), custom_call_target="tpu_custom_call" | custom-call | flops 536870912 | bytes 1703936 | tf_op jit(solution)/shard_map/back_act/pallas_call | solution.py:486
  93.9 12.9 %all-to-all-done.2.conv = bf16[8,512,128]{2,1,0:T(8,128)(2,1)} async-done(((bf16[8,512,128]{2,1,0:T(8,128)(2,1)}), bf16[8,512,128]{2,1,0:T(8,128)(2,1)}, u32[]{:S(2)}, u32[]{:S(2)}) %all-to-all-start.2) | async-done | bytes 1048608 | tf_op jit(solution)/shard_map/all_to_all | solution.py:952
  106.7 29.4 %middle.1 = (bf16[512,4096]{1,0:T(8,128)(2,1)}, bf16[512,4096]{1,0:T(8,128)(2,1)}, f32[1,4096]{1,0:T(1,128)}, bf16[512,1024]{1,0:T(8,128)(2,1)}, bf16[512,1024]{...) custom-call(bf16[8,512,128]{2,1,0:T(8,128)(2,1)} %all-to-all-done.2., ...), custom_call_target="tpu_custom_call" | custom-call | flops 1342177280 | bytes 4456448 | tf_op jit(solution)/shard_map/middle/pallas_call | solution.py:620
  143.7 9.8 %wgrad.4 = (bf16[8,640,256]{2,1,0:T(8,128)(2,1)}, bf16[8,640,256]{2,1,0:T(8,128)(2,1)}) custom-call(s32[8]{0:T(128)} %broadcast_xor_fusion.row_order, s32[4]{0:T(128)} %pad_add_fusion.units, bf16[512,4096]{1,0:T(8,128)(2,1)} %get-tuple-element.177.refs_0_.refs_1_.act, bf16[512,4096]{1,0:T(8,128)(2,1)} %get-tuple-element.177.refs_0_.refs_1_.act, ...), custom_call_target="tpu_custom_call" | custom-call | flops 536870912 | bytes 2228224 | tf_op jit(solution)/shard_map/wgrad/pallas_call | solution.py:877
  162.3 5.2 %all-to-all-done.3 = bf16[8,512,128]{2,1,0:T(8,128)(2,1)} async-done(((bf16[8,512,128]{2,1,0:T(8,128)(2,1)}), bf16[8,512,128]{2,1,0:T(8,128)(2,1)}, u32[]{:S(2)}, u32[]{:S(2)}) %all-to-all-start.3) | async-done | bytes 1048608 | tf_op jit(solution)/shard_map/all_to_all | solution.py:948
  167.4 10.1 %correlate.1 = (bf16[8,528,128]{2,1,0:T(8,128)(2,1)}, bf16[32,256,128]{2,1,0:T(8,128)(2,1)}) custom-call(bf16[32,128,128]{2,1,0:T(8,128)(2,1)} %bitcast.21.refs_0_.refs_2_, bf16[32,256,128]{2,1,0:T(8,128)(2,1)} %spectrum.1.refs_1_, f32[1,128]{1,0:T(1,128)} %bitcast.113, bf16[32,256,256]{2,1,0:T(8,128)(2,1)} %get-tuple-element.120.refs_1_.refs_3_, ...), custom_call_target="tpu_custom_call" | custom-call | flops 536870912 | bytes 2097152 | tf_op jit(solution)/shard_map/correlate/pallas_call | solution.py:279
  185.1 11.0 %wgrad.6 = (bf16[4,128,512]{2,1,0:T(8,128)(2,1)}, bf16[4,128,1024]{2,1,0:T(8,128)(2,1)}, bf16[4,128,512]{2,1,0:T(8,128)(2,1)}, bf16[4,128,2048]{2,1,0:T(8,128)(2,1)}) custom-call(s32[8]{0:T(128)} %broadcast_xor_fusion.1.row_order, s32[4]{0:T(128)} %pad_add_fusion.units, bf16[512,1024]{1,0:T(8,128)(2,1)} %get-tuple-element.143.refs_0_.refs_1_.refs_2_.refs_3_, ...), custom_call_target="tpu_custom_call" | custom-call | flops 536870912 | bytes 1835008 | tf_op jit(solution)/shard_map/wgrad/pallas_call | solution.py:877
  196.1 11.2 %filter_grad.1 = (f32[64,128]{1,0:T(8,128)}, f32[48,64]{1,0:T(8,128)}, f32[64,2]{1,0:T(8,128)}, f32[1,128]{1,0:T(1,128)}) custom-call(bf16[32,256,128]{2,1,0:T(8,128)(2,1)} %get-tuple-element.149.refs_0_, bf16[32,256,128]{2,1,0:T(8,128)(2,1)} %get-tuple-element.150.refs_1_, bf16[32,128,128]{2,1,0:T(8,128)(2,1)} %bitcast.21.refs_0_.refs_2_, ...), custom_call_target="tpu_custom_call" | custom-call | flops 536870912 | bytes 2097152 | tf_op jit(solution)/shard_map/filter_grad/pallas_call | solution.py:279
  209.4 11.3 %leave.1 = (bf16[3,4,512,256]{3,2,1,0:T(8,128)(2,1)}, f32[16,1024]{1,0:T(8,128)}) custom-call(bf16[8,528,128]{2,1,0:T(8,128)(2,1)} %copy-done.11, bf16[512,1024]{1,0:T(8,128)(2,1)} %get-tuple-element.142.ggate, bf16[16,1024]{1,0:T(8,128)(2,1)} %copy-done.19, bf16[3,528,1024]{2,1,0:T(8,128)(2,1)} %get-tuple-element.123.proj, ...), custom_call_target="tpu_custom_call" | custom-call | flops 3932160 | bytes 1179648 | tf_op jit(solution)/shard_map/leave/pallas_call | solution.py:753
  232.0 10.5 %tokens_back.1 = (f32[512,1024]{1,0:T(8,128)}, f32[2,1024]{1,0:T(2,128)}) custom-call(bf16[3,4,512,256]{3,2,1,0:T(8,128)(2,1)} %get-tuple-element.165.gproj, bf16[1024,3072]{1,0:T(8,128)(2,1)} %weight.1, bf16[512,1024]{1,0:T(8,128)(2,1)} %bitcast.81, bf16[512,1024]{1,0:T(8,128)(2,1)} %get-tuple-element.134.gres, f32[1,1024]{1,0:T(1,128)} %bitcast.102), custom_call_target="tpu_custom_call" | custom-call | flops 402653184 | bytes 1835008 | tf_op jit(solution)/shard_map/tokens_back/pallas_call | solution.py:801
  246.3 5.5 %collective-permute-done.14 = bf16[4,128,1024]{2,1,0:T(8,128)(2,1)} collective-permute-done((bf16[4,128,1024]{2,1,0:T(8,128)(2,1)}, bf16[4,128,1024]{2,1,0:T(8,128)(2,1)}, u32[]{:S(2)}, u32[]{:S(2)}) %collective-permute-start.14) | collective-permute-done | bytes 1048608 | tf_op jit(solution)/shard_map/ppermute | solution.py:416
  258.2 9.9 %block_out.1 = bf16[512,1024]{1,0:T(8,128)(2,1)} custom-call(bf16[512,4096]{1,0:T(8,128)(2,1)} %get-tuple-element.177.refs_0_.refs_1_.act, bf16[4096,1024]{1,0:T(8,128)(2,1)} %down.3, bf16[512,1024]{1,0:T(8,128)(2,1)} %get-tuple-element.178.resid, f32[1,1024]{1,0:T(1,128)} %bitcast.111), custom_call_target="tpu_custom_call" | custom-call | flops 536870912 | bytes 1966080 | tf_op jit(solution)/shard_map/block_out/pallas_call | solution.py:510
  269.7 9.0 %wgrad.7 = (bf16[4,128,768]{2,1,0:T(8,128)(2,1)}, bf16[4,128,768]{2,1,0:T(8,128)(2,1)}) custom-call(s32[8]{0:T(128)} %broadcast_xor_fusion.row_order, s32[12]{0:T(128)} %pad_add_fusion.1.units, bf16[512,1024]{1,0:T(8,128)(2,1)} %get-tuple-element.183.refs_0_.refs_1_.refs_2_.refs_3_, bf16[512,1024]{1,0:T(8,128)(2,1)} %get-tuple-element.183.refs_0_.refs_1_.refs_2_.refs_3_, ...), custom_call_target="tpu_custom_call" | custom-call | flops 402653184 | bytes 1310720 | tf_op jit(solution)/shard_map/wgrad/pallas_call | solution.py:877
  292.3 9.7 %collective-permute-done.21 = f32[232,128]{1,0:T(8,128)S(1)} collective-permute-done((f32[232,128]{1,0:T(8,128)S(1)}, f32[232,128]{1,0:T(8,128)S(1)}, u32[]{:S(2)}, u32[]{:S(2)}) %collective-permute-start.21) | collective-permute-done | bytes 118816 | tf_op jit(solution)/shard_map/ppermute | solution.py:416
  314.6 8.9 %collective-permute-done.25 = f32[232,128]{1,0:T(8,128)S(1)} collective-permute-done((f32[232,128]{1,0:T(8,128)S(1)}, f32[232,128]{1,0:T(8,128)S(1)}, u32[]{:S(2)}, u32[]{:S(2)}) %collective-permute-start.25) | collective-permute-done | bytes 118816 | tf_op jit(solution)/shard_map/ppermute | solution.py:416
  328.4 5.5 %collective-permute-done.26 = bf16[1,128,1024]{2,1,0:T(8,128)(2,1)S(1)} collective-permute-done((bf16[1,128,1024]{2,1,0:T(8,128)(2,1)S(1)}, bf16[1,128,1024]{2,1,0:T(8,128)(2,1)S(1)}, u32[]{:S(2)}, u32[]{:S(2)}) %collective-permute-start.26) | collective-permute-done | bytes 262176 | tf_op jit(solution)/shard_map/ppermute | solution.py:416
  (202 shorter events, 109.2 us)
Async XLA Ops:
  3.5 14.6 %all-to-all-start = ((f32[8,28,128]{2,1,0:T(8,128)}), f32[8,28,128]{2,1,0:T(8,128)S(1)}, u32[]{:S(2)}, u32[]{:S(2)}) async-start(f32[8,28,128]{2,1,0:T(8,128)} %broadcast_in_dim.58), calls=%async_computation | async-start | bytes 262144 | tf_op jit(solution)/shard_map/all_to_all | solution.py:928
  31.4 32.1 %all-to-all-start.1 = ((bf16[8,512,128]{2,1,0:T(8,128)(2,1)}), bf16[8,512,128]{2,1,0:T(8,128)(2,1)S(1)}, u32[]{:S(2)}, u32[]{:S(2)}) async-start(bf16[8,512,128]{2,1,0:T(8,128)(2,1)} %get-tuple-element.119), calls=%async_computation.1 | async-start | bytes 2097152 | tf_op jit(solution)/shard_map/all_to_all | solution.py:948
  37.5 37.0 %collective-permute-start.1 = (bf16[512,1024]{1,0:T(8,128)(2,1)S(1)}, bf16[512,1024]{1,0:T(8,128)(2,1)S(1)}, u32[]{:S(2)}, u32[]{:S(2)}) collective-permute-start(bf16[512,1024]{1,0:T(8,128)(2,1)S(1)} %copy-done.5), channel_id=1, source_target_pairs={{0,16},{8,24},{16,0},{24,8},{1,17},{9,25},{17,1},{25,9},{2,18},{10... | collective-permute-start | bytes 3145736 | tf_op jit(solution)/shard_map/ppermute | solution.py:416
  55.8 18.6 %collective-permute-start = (bf16[3,16,1024]{2,1,0:T(8,128)(2,1)}, bf16[3,16,1024]{2,1,0:T(8,128)(2,1)}, u32[]{:S(2)}, u32[]{:S(2)}) collective-permute-start(bf16[3,16,1024]{2,1,0:T(8,128)(2,1)} %slice.227), channel_id=1, source_target_pairs={{1,0},{2,1},{3,2},{4,3},{5,4},{6,5},{7,6},{9,8},{10,9},{11,10},{12... | collective-permute-start | bytes 294920 | tf_op jit(solution)/shard_map/ppermute | solution.py:943
  74.5 32.2 %all-to-all-start.2 = ((bf16[8,512,128]{2,1,0:T(8,128)(2,1)}), bf16[8,512,128]{2,1,0:T(8,128)(2,1)}, u32[]{:S(2)}, u32[]{:S(2)}) async-start(bf16[8,512,128]{2,1,0:T(8,128)(2,1)} %get-tuple-element.125), calls=%async_computation.2 | async-start | bytes 2097152 | tf_op jit(solution)/shard_map/all_to_all | solution.py:952
  136.3 41.4 %collective-permute-start.5 = (bf16[1,512,4096]{2,1,0:T(8,128)(2,1)}, bf16[1,512,4096]{2,1,0:T(8,128)(2,1)}, u32[]{:S(2)}, u32[]{:S(2)}) collective-permute-start(bf16[1,512,4096]{2,1,0:T(8,128)(2,1)} %bitcast.75), channel_id=1, source_target_pairs={{0,8},{8,0},{16,24},{24,16},{1,9},{9,1},{17,25},{25,17},{2,10},{10... | collective-permute-start | bytes 12582920 | tf_op jit(solution)/shard_map/ppermute | solution.py:416
  136.8 30.7 %all-to-all-start.3 = ((bf16[8,512,128]{2,1,0:T(8,128)(2,1)}), bf16[8,512,128]{2,1,0:T(8,128)(2,1)}, u32[]{:S(2)}, u32[]{:S(2)}) async-start(bf16[8,512,128]{2,1,0:T(8,128)(2,1)} %get-tuple-element.132), calls=%async_computation.3 | async-start | bytes 2097152 | tf_op jit(solution)/shard_map/all_to_all | solution.py:948
  141.7 35.9 %collective-permute-start.6 = (bf16[512,1024]{1,0:T(8,128)(2,1)S(1)}, bf16[512,1024]{1,0:T(8,128)(2,1)}, u32[]{:S(2)}, u32[]{:S(2)}) collective-permute-start(bf16[512,1024]{1,0:T(8,128)(2,1)S(1)} %copy-done.8), channel_id=1, source_target_pairs={{0,8},{8,0},{16,24},{24,16},{1,9},{9,1},{17,25},{25,17},{2,10},{10... | collective-permute-start | bytes 3145736 | tf_op jit(solution)/shard_map/ppermute | solution.py:416
  159.4 61.6 %collective-permute-start.11 = (bf16[8,640,256]{2,1,0:T(8,128)(2,1)}, bf16[8,640,256]{2,1,0:T(8,128)(2,1)}, u32[]{:S(2)}, u32[]{:S(2)}) collective-permute-start(bf16[8,640,256]{2,1,0:T(8,128)(2,1)} %get-tuple-element.159), channel_id=1, source_target_pairs={{0,16},{8,24},{16,0},{24,8},{1,17},{9,25},{17,1},{25,9},{2,18},{10... | collective-permute-start | bytes 7864328 | tf_op jit(solution)/shard_map/ppermute | solution.py:416
  161.0 16.6 %collective-permute-start.10 = (bf16[16,1024]{1,0:T(8,128)(2,1)S(1)}, bf16[16,1024]{1,0:T(8,128)(2,1)S(1)}, u32[]{:S(2)}, u32[]{:S(2)}) collective-permute-start(bf16[16,1024]{1,0:T(8,128)(2,1)S(1)} %slice.228), channel_id=1, source_target_pairs={{1,0},{2,1},{3,2},{4,3},{5,4},{6,5},{7,6},{9,8},{10,9},{11,10},{12... | collective-permute-start | bytes 98312 | tf_op jit(solution)/shard_map/ppermute | solution.py:980
  177.6 30.3 %all-to-all-start.4 = ((bf16[8,528,128]{2,1,0:T(8,128)(2,1)}), bf16[8,528,128]{2,1,0:T(8,128)(2,1)S(1)}, u32[]{:S(2)}, u32[]{:S(2)}) async-start(bf16[8,528,128]{2,1,0:T(8,128)(2,1)} %get-tuple-element.148), calls=%async_computation.4 | async-start | bytes 2162688 | tf_op jit(solution)/shard_map/all_to_all | solution.py:952
  221.0 47.0 %all-to-all-start.5 = ((bf16[12,512,256]{2,1,0:T(8,128)(2,1)}), bf16[12,512,256]{2,1,0:T(8,128)(2,1)S(1)}, u32[]{:S(2)}, u32[]{:S(2)}) async-start(bf16[12,512,256]{2,1,0:T(8,128)(2,1)} %bitcast.78), calls=%async_computation.5 | async-start | bytes 6291456 | tf_op jit(solution)/shard_map/all_to_all | solution.py:1020
  225.4 26.4 %collective-permute-start.14 = (bf16[4,128,1024]{2,1,0:T(8,128)(2,1)}, bf16[4,128,1024]{2,1,0:T(8,128)(2,1)}, u32[]{:S(2)}, u32[]{:S(2)}) collective-permute-start(bf16[4,128,1024]{2,1,0:T(8,128)(2,1)} %get-tuple-element.175), channel_id=1, source_target_pairs={{0,2},{1,3},{2,0},{3,1},{4,6},{5,7},{6,4},{7,5},{8,10},{9,11},{10,... | collective-permute-start | bytes 3145736 | tf_op jit(solution)/shard_map/ppermute | solution.py:416
  243.2 35.5 %collective-permute-start.16 = (bf16[4,640,256]{2,1,0:T(8,128)(2,1)}, bf16[4,640,256]{2,1,0:T(8,128)(2,1)}, u32[]{:S(2)}, u32[]{:S(2)}) collective-permute-start(bf16[4,640,256]{2,1,0:T(8,128)(2,1)} %get-tuple-element.189), channel_id=1, source_target_pairs={{0,1},{1,0},{2,3},{3,2},{4,5},{5,4},{6,7},{7,6},{8,9},{9,8},{10,11... | collective-permute-start | bytes 3932168 | tf_op jit(solution)/shard_map/ppermute | solution.py:416
  244.9 33.8 %collective-permute-start.17 = (bf16[4,128,512]{2,1,0:T(8,128)(2,1)}, bf16[4,128,512]{2,1,0:T(8,128)(2,1)}, u32[]{:S(2)}, u32[]{:S(2)}) collective-permute-start(bf16[4,128,512]{2,1,0:T(8,128)(2,1)} %get-tuple-element.190), channel_id=1, source_target_pairs={{0,2},{1,3},{2,0},{3,1},{4,6},{5,7},{6,4},{7,5},{8,10},{9,11},{10,... | collective-permute-start | bytes 1572872 | tf_op jit(solution)/shard_map/ppermute | solution.py:416
  255.6 32.0 %collective-permute-start.15 = (bf16[4,128,1024]{2,1,0:T(8,128)(2,1)}, bf16[4,128,1024]{2,1,0:T(8,128)(2,1)}, u32[]{:S(2)}, u32[]{:S(2)}) collective-permute-start(bf16[4,128,1024]{2,1,0:T(8,128)(2,1)} %add_convert_fusion.3), channel_id=1, source_target_pairs={{0,16},{8,24},{16,0},{24,8},{1,17},{9,25},{17,1},{25,9},{2,18},{10... | collective-permute-start | bytes 3145736 | tf_op jit(solution)/shard_map/ppermute | solution.py:416
  257.9 29.7 %collective-permute-start.18 = (f32[304,128]{1,0:T(8,128)S(1)}, f32[304,128]{1,0:T(8,128)S(1)}, u32[]{:S(2)}, u32[]{:S(2)}) collective-permute-start(f32[304,128]{1,0:T(8,128)S(1)} %fusion.7), channel_id=1, source_target_pairs={{0,16},{8,24},{16,0},{24,8},{1,17},{9,25},{17,1},{25,9},{2,18},{10... | collective-permute-start | bytes 466952 | tf_op jit(solution)/shard_map/ppermute | solution.py:416
  278.7 23.3 %collective-permute-start.19 = (bf16[4,128,768]{2,1,0:T(8,128)(2,1)}, bf16[4,128,768]{2,1,0:T(8,128)(2,1)S(1)}, u32[]{:S(2)}, u32[]{:S(2)}) collective-permute-start(bf16[4,128,768]{2,1,0:T(8,128)(2,1)} %get-tuple-element.195), channel_id=1, source_target_pairs={{0,1},{1,0},{2,3},{3,2},{4,5},{5,4},{6,7},{7,6},{8,9},{9,8},{10,11... | collective-permute-start | bytes 2359304 | tf_op jit(solution)/shard_map/ppermute | solution.py:416
  283.7 18.3 %collective-permute-start.20 = (bf16[2,640,256]{2,1,0:T(8,128)(2,1)S(1)}, bf16[2,640,256]{2,1,0:T(8,128)(2,1)S(1)}, u32[]{:S(2)}, u32[]{:S(2)}) collective-permute-start(bf16[2,640,256]{2,1,0:T(8,128)(2,1)S(1)} %get-tuple-element.214), channel_id=1, source_target_pairs={{0,2},{1,3},{2,0},{3,1},{4,6},{5,7},{6,4},{7,5},{8,10},{9,11},{10,... | collective-permute-start | bytes 1966088 | tf_op jit(solution)/shard_map/ppermute | solution.py:416
  291.5 18.9 %collective-permute-start.24 = (bf16[2,128,1024]{2,1,0:T(8,128)(2,1)S(1)}, bf16[2,128,1024]{2,1,0:T(8,128)(2,1)S(1)}, u32[]{:S(2)}, u32[]{:S(2)}) collective-permute-start(bf16[2,128,1024]{2,1,0:T(8,128)(2,1)S(1)} %get-tuple-element.216), channel_id=1, source_target_pairs={{0,1},{1,0},{2,3},{3,2},{4,5},{5,4},{6,7},{7,6},{8,9},{9,8},{10,11... | collective-permute-start | bytes 1572872 | tf_op jit(solution)/shard_map/ppermute | solution.py:416
  302.1 21.5 %collective-permute-start.23 = (bf16[1,640,256]{2,1,0:T(8,128)(2,1)S(1)}, bf16[1,640,256]{2,1,0:T(8,128)(2,1)S(1)}, u32[]{:S(2)}, u32[]{:S(2)}) collective-permute-start(bf16[1,640,256]{2,1,0:T(8,128)(2,1)S(1)} %add_convert_fusion.11), channel_id=1, source_target_pairs={{0,4},{1,5},{2,6},{3,7},{4,0},{5,1},{6,2},{7,3},{8,12},{9,13},{10,... | collective-permute-start | bytes 983048 | tf_op jit(solution)/shard_map/ppermute | solution.py:416
  305.0 18.5 %collective-permute-start.22 = (bf16[2,128,768]{2,1,0:T(8,128)(2,1)S(1)}, bf16[2,128,768]{2,1,0:T(8,128)(2,1)S(1)}, u32[]{:S(2)}, u32[]{:S(2)}) collective-permute-start(bf16[2,128,768]{2,1,0:T(8,128)(2,1)S(1)} %get-tuple-element.218), channel_id=1, source_target_pairs={{0,2},{1,3},{2,0},{3,1},{4,6},{5,7},{6,4},{7,5},{8,10},{9,11},{10,... | collective-permute-start | bytes 1179656 | tf_op jit(solution)/shard_map/ppermute | solution.py:416
  312.2 21.7 %collective-permute-start.26 = (bf16[1,128,1024]{2,1,0:T(8,128)(2,1)S(1)}, bf16[1,128,1024]{2,1,0:T(8,128)(2,1)S(1)}, u32[]{:S(2)}, u32[]{:S(2)}) collective-permute-start(bf16[1,128,1024]{2,1,0:T(8,128)(2,1)S(1)} %add_convert_fusion.13), channel_id=1, source_target_pairs={{0,4},{1,5},{2,6},{3,7},{4,0},{5,1},{6,2},{7,3},{8,12},{9,13},{10,... | collective-permute-start | bytes 786440 | tf_op jit(solution)/shard_map/ppermute | solution.py:416
  323.6 15.3 %collective-permute-start.27 = (bf16[1,128,768]{2,1,0:T(8,128)(2,1)S(1)}, bf16[1,128,768]{2,1,0:T(8,128)(2,1)S(1)}, u32[]{:S(2)}, u32[]{:S(2)}) collective-permute-start(bf16[1,128,768]{2,1,0:T(8,128)(2,1)S(1)} %add_convert_fusion.15), channel_id=1, source_target_pairs={{0,4},{1,5},{2,6},{3,7},{4,0},{5,1},{6,2},{7,3},{8,12},{9,13},{10,... | collective-permute-start | bytes 589832 | tf_op jit(solution)/shard_map/ppermute | solution.py:416
  (43 other events, 413.7 us)

commit v5 on v4

--- a/solution.py
+++ b/solution.py
@@ -15,7 +15,7 @@
 BLOCK = 128
 LANES = 128
 ROWS = 16
-CHUNK = 128
+CHUNK = 256
 GRANT = 60 << 20
 COST = 8
 F32 = jnp.float32
@@ -162,7 +162,7 @@
         back[k] = mxu(inverse[k], prod[k])
         return carry
 
-    lax.fori_loop(0, prod.shape[0], body, 0, unroll=8)
+    lax.fori_loop(0, prod.shape[0], body, 0, unroll=16)
 
 
 def spectrum_kernel(signal, forward, spectrum, mid):
@@ -176,7 +176,7 @@
         spectrum[k] = mxu(forward[k], mid[k]).astype(BF16)
         return carry
 
-    lax.fori_loop(0, count, body, 0, unroll=8)
+    lax.fori_loop(0, count, body, 0, unroll=16)
 
 
 def conv_kernel(signal, kernel_spec, bias, forward, inverse, result, spectrum, mid, prod, back, *, conjugate):
@@ -200,7 +200,7 @@
         prod[k, BLOCK:, :] = (a_re * b_im + a_im * b_re).astype(BF16)
         return carry
 
-    lax.fori_loop(0, count, body, 0, unroll=8)
+    lax.fori_loop(0, count, body, 0, unroll=16)
     have_inverse()
     turn_back(prod, inverse, back)
     gain = bias[...]
@@ -1077,9 +1077,10 @@
         in_got = swap(in_send, "seq", bits[i])
         packed = packed + small
         small = swap(packed, "seq", bits[i])
-    up_got, in_got, small = tie(up_got, in_got, small)
-    grad_up, packed = last(up_kept, up_got), packed + small
-    grad_in, both = last(in_kept, in_got), last(tall_kept, tall_got)
+    up_got, in_got = tie(up_got, in_got)
+    grad_in, grad_up, both = last(in_kept, in_got), last(up_kept, up_got), last(tall_kept, tall_got)
+    small, grad_in, grad_up = tie(small, grad_in, grad_up)
+    packed = packed + small
     grad_down, grad_out_weight = both[:wide], both[wide:]
     channel = unpack(extra, channel)
     shared = unpack(packed, shared)

time: 347 us -> 358 us (1.032)
  starting transfers between devices: 63.3 us -> 74.4 us
    all_to_all x2, starting transfers between devices: 11.5 us -> 23.4 us  [to_tokens(): got = lax.all_to_all(value, 'seq', split_axis=0, concat_axis=0, tiled=True)]
  transfers between devices with their start and end apart: 35 -> 35, of which waited for: 15 -> 15; matrix products, arithmetic and copies ran while one was open for 12% -> 12% of each run, Pallas kernels for 35% -> 34%
where the time goes in v5:
time: 358 us; the launch traced here: 354 us
  Pallas kernels  160 us (45%)
  starting transfers between devices  74.4 us (21%)
  waiting for transfers between devices  62.2 us (17%)
  other arithmetic  21.9 us (6%)
  local copies, waits for them, and re-layouts  20 us (6%)
  matrix products  14.2 us (4%)
    ppermute x27, waiting for transfers between devices, swap(): return lax.ppermute(value, axis, [(i, i ^ bit) for i in range(size)])  42.5 us
    pallas_call x4, Pallas kernels, vmem_call(): pl.pallas_call(body, in_specs=[pl.BlockSpec(memory_space=pl.ANY)] * count...  36 us
    pallas_call x4, Pallas kernels, wgrad(): pl.pallas_call(functools.partial(wgrad_kernel, sides=sides, lefts=lefts,...  34.7 us
    pallas_call x1, Pallas kernels, middle(): pl.pallas_call(middle_kernel, grid=(ff // block,), in_specs=[whole(nb, ro...  29.2 us
    ppermute x27, starting transfers between devices, swap(): return lax.ppermute(value, axis, [(i, i ^ bit) for i in range(size)])  27.8 us
    all_to_all x2, starting transfers between devices, to_tokens(): got = lax.all_to_all(value, 'seq', split_axis=0, concat_axis=0, tiled=True)  23.4 us
    all_to_all x2, waiting for transfers between devices, to_tokens(): got = lax.all_to_all(value, 'seq', split_axis=0, concat_axis=0, tiled=True)  13.5 us
    convert_element_type x9, other arithmetic, add(): return (left.astype(F32) + right.astype(F32)).astype(BF16)  12.8 us
  transfers between devices with their start and end apart: 35, of which 15 were waited for; matrix products, arithmetic and copies ran while one was open for 12% of the time, Pallas kernels for 34%

profile of v5, /device:TPU:0, one launch (start us, length us, event | category | flops | bytes accessed | tf_op | source)
XLA Modules:
  0.0 354.2 jit_solution(1893608971062236219)
XLA Ops:
  3.5 7.3 %all-to-all-start = ((f32[8,28,128]{2,1,0:T(8,128)}), f32[8,28,128]{2,1,0:T(8,128)S(1)}, u32[]{:S(2)}, u32[]{:S(2)}) async-start(f32[8,28,128]{2,1,0:T(8,128)} %broadcast_in_dim.58), calls=%async_computation | async-start | bytes 262144 | tf_op jit(solution)/shard_map/all_to_all | solution.py:928
  10.8 6.2 %tables.1 = (bf16[32,256,256]{2,1,0:T(8,128)(2,1)}, bf16[32,256,256]{2,1,0:T(8,128)(2,1)}) custom-call(f32[32,1,128]{2,1,0:T(1,128)} %constant.59.clone.alpha_cos, f32[32,1,128]{2,1,0:T(1,128)} %constant.60.clone.alpha_sin, f32[128,128]{1,0:T(8,128)} %constant.61.clone.beta_cos, f32[128,128]{1,0:T(8,128)} %constant.62.clone.beta_sin), custom_call_target="tpu_custom_call" | custom-call | flops 1048576 | bytes 1048576 | tf_op jit(solution)/shard_map/tables/pallas_call | solution.py:145
  19.4 11.6 %enter.1 = (bf16[8,512,128]{2,1,0:T(8,128)(2,1)}, bf16[512,1024]{1,0:T(8,128)(2,1)}, bf16[3,528,1024]{2,1,0:T(8,128)(2,1)}, bf16[512,1024]{1,0:T(8,128)(2,1)}) custom-call(s32[1]{0:T(128)} %bitcast.2.first, bf16[512,1024]{1,0:T(8,128)(2,1)} %bitcast.79, bf16[16,1024]{1,0:T(8,128)(2,1)} %concatenate.39.before, f32[1,1024]{1,0:T(1,128)} %bitcast.101, ...), custom_call_target="tpu_custom_call" | custom-call | flops 402653184 | bytes 1835008 | tf_op jit(solution)/shard_map/enter/pallas_call | solution.py:681
  38.8 5.8 %multiply_cosine_fusion = (f32[64,4096]{1,0:T(8,128)}, bf16[64,4096]{1,0:T(8,128)(2,1)}, f32[64,4096]{1,0:T(8,128)S(1)}) fusion(f32[64]{0:T(128)S(1)} %copy-done.24, f32[64]{0:T(128)S(1)} %copy-done.27, f32[33,64]{1,0:T(8,128)S(1)} %copy-done, f32[16,4096]{1,0:T(8,128)S(1)} %get-tuple-element.234, f32[16,4096]{1,0:T(8,128)S(1)} %get-tuple-element.233, ...), kind=kOutput, calls=%fused_computation.12 | convolution fusion | flops 104865792 | bytes 3171072 | tf_op jit(solution)/shard_map/dot_general | solution.py:961
  45.6 8.3 %convolution_multiply_fusion = f32[4096,128]{1,0:T(8,128)} fusion(f32[64,128]{1,0:T(8,128)S(1)} %copy-done.16, f32[64,4096]{1,0:T(8,128)S(1)} %get-tuple-element.235.refs_8_, f32[128]{0:T(128)S(1)} %copy-done.26, f32[4096]{0:T(1024)S(1)} %multiply_negate_fusion, f32[64]{0:T(128)S(1)} %copy-done.24), kind=kOutput, calls=%fused_computation | convolution fusion | flops 403963904 | bytes 3195648 | tf_op jit(solution)/shard_map/hn,hc->nc/dot_general | solution.py:965
  56.8 6.1 %spectrum.1.refs_1_ = bf16[32,256,128]{2,1,0:T(8,128)(2,1)} custom-call(f32[32,128,128]{2,1,0:T(8,128)} %bitcast.87, bf16[32,256,256]{2,1,0:T(8,128)(2,1)} %get-tuple-element.122.refs_1_.refs_3_), custom_call_target="tpu_custom_call" | custom-call | flops 536870912 | bytes 2097152 | tf_op jit(solution)/shard_map/spectrum/pallas_call | solution.py:279
  63.8 9.4 %convolve.1 = (bf16[8,512,128]{2,1,0:T(8,128)(2,1)}, bf16[32,256,128]{2,1,0:T(8,128)(2,1)}) custom-call(bf16[32,128,128]{2,1,0:T(8,128)(2,1)} %bitcast.82, bf16[32,256,128]{2,1,0:T(8,128)(2,1)} %spectrum.1.refs_1_, f32[1,128]{1,0:T(1,128)} %bitcast.112, bf16[32,256,256]{2,1,0:T(8,128)(2,1)} %get-tuple-element.122.refs_1_.refs_3_, ...), custom_call_target="tpu_custom_call" | custom-call | flops 536870912 | bytes 2097152 | tf_op jit(solution)/shard_map/convolve/pallas_call | solution.py:279
  73.3 8.1 %all-to-all-start.2 = ((bf16[8,512,128]{2,1,0:T(8,128)(2,1)}), bf16[8,512,128]{2,1,0:T(8,128)(2,1)}, u32[]{:S(2)}, u32[]{:S(2)}) async-start(bf16[8,512,128]{2,1,0:T(8,128)(2,1)} %get-tuple-element.127), calls=%async_computation.2 | async-start | bytes 2097152 | tf_op jit(solution)/shard_map/all_to_all | solution.py:952
  82.1 10.9 %back_act.1 = (bf16[512,4096]{1,0:T(8,128)(2,1)}, f32[1,1024]{1,0:T(1,128)}) custom-call(bf16[512,1024]{1,0:T(8,128)(2,1)} %bitcast.12.dy, bf16[4096,1024]{1,0:T(8,128)(2,1)} %down.3), custom_call_target="tpu_custom_call" | custom-call | flops 536870912 | bytes 1703936 | tf_op jit(solution)/shard_map/back_act/pallas_call | solution.py:486
  93.0 12.7 %all-to-all-done.2.conv = bf16[8,512,128]{2,1,0:T(8,128)(2,1)} async-done(((bf16[8,512,128]{2,1,0:T(8,128)(2,1)}), bf16[8,512,128]{2,1,0:T(8,128)(2,1)}, u32[]{:S(2)}, u32[]{:S(2)}) %all-to-all-start.2) | async-done | bytes 1048608 | tf_op jit(solution)/shard_map/all_to_all | solution.py:952
  105.7 29.2 %middle.1 = (bf16[512,4096]{1,0:T(8,128)(2,1)}, bf16[512,4096]{1,0:T(8,128)(2,1)}, f32[1,4096]{1,0:T(1,128)}, bf16[512,1024]{1,0:T(8,128)(2,1)}, bf16[512,1024]{...) custom-call(bf16[8,512,128]{2,1,0:T(8,128)(2,1)} %all-to-all-done.2., ...), custom_call_target="tpu_custom_call" | custom-call | flops 1342177280 | bytes 4456448 | tf_op jit(solution)/shard_map/middle/pallas_call | solution.py:620
  142.5 9.8 %wgrad.4 = (bf16[8,640,256]{2,1,0:T(8,128)(2,1)}, bf16[8,640,256]{2,1,0:T(8,128)(2,1)}) custom-call(s32[8]{0:T(128)} %broadcast_xor_fusion.row_order, s32[4]{0:T(128)} %pad_add_fusion.units, bf16[512,4096]{1,0:T(8,128)(2,1)} %get-tuple-element.179.refs_0_.refs_1_.act, bf16[512,4096]{1,0:T(8,128)(2,1)} %get-tuple-element.179.refs_0_.refs_1_.act, ...), custom_call_target="tpu_custom_call" | custom-call | flops 536870912 | bytes 2228224 | tf_op jit(solution)/shard_map/wgrad/pallas_call | solution.py:877
  166.2 9.6 %correlate.1 = (bf16[8,528,128]{2,1,0:T(8,128)(2,1)}, bf16[32,256,128]{2,1,0:T(8,128)(2,1)}) custom-call(bf16[32,128,128]{2,1,0:T(8,128)(2,1)} %bitcast.21.refs_0_.refs_2_, bf16[32,256,128]{2,1,0:T(8,128)(2,1)} %spectrum.1.refs_1_, f32[1,128]{1,0:T(1,128)} %bitcast.113, bf16[32,256,256]{2,1,0:T(8,128)(2,1)} %get-tuple-element.122.refs_1_.refs_3_, ...), custom_call_target="tpu_custom_call" | custom-call | flops 536870912 | bytes 2097152 | tf_op jit(solution)/shard_map/correlate/pallas_call | solution.py:279
  175.9 15.3 %all-to-all-start.4 = ((bf16[8,528,128]{2,1,0:T(8,128)(2,1)}), bf16[8,528,128]{2,1,0:T(8,128)(2,1)S(1)}, u32[]{:S(2)}, u32[]{:S(2)}) async-start(bf16[8,528,128]{2,1,0:T(8,128)(2,1)} %get-tuple-element.150), calls=%async_computation.4 | async-start | bytes 2162688 | tf_op jit(solution)/shard_map/all_to_all | solution.py:952
  194.9 11.0 %wgrad.6 = (bf16[4,128,512]{2,1,0:T(8,128)(2,1)}, bf16[4,128,1024]{2,1,0:T(8,128)(2,1)}, bf16[4,128,512]{2,1,0:T(8,128)(2,1)}, bf16[4,128,2048]{2,1,0:T(8,128)(2,1)}) custom-call(s32[8]{0:T(128)} %broadcast_xor_fusion.1.row_order, s32[4]{0:T(128)} %pad_add_fusion.units, bf16[512,1024]{1,0:T(8,128)(2,1)} %get-tuple-element.145.refs_0_.refs_1_.refs_2_.refs_3_, ...), custom_call_target="tpu_custom_call" | custom-call | flops 536870912 | bytes 1835008 | tf_op jit(solution)/shard_map/wgrad/pallas_call | solution.py:877
  205.9 10.9 %filter_grad.1 = (f32[64,128]{1,0:T(8,128)}, f32[48,64]{1,0:T(8,128)}, f32[64,2]{1,0:T(8,128)}, f32[1,128]{1,0:T(1,128)}) custom-call(bf16[32,256,128]{2,1,0:T(8,128)(2,1)} %get-tuple-element.151.refs_0_, bf16[32,256,128]{2,1,0:T(8,128)(2,1)} %get-tuple-element.152.refs_1_, bf16[32,128,128]{2,1,0:T(8,128)(2,1)} %bitcast.21.refs_0_.refs_2_, ...), custom_call_target="tpu_custom_call" | custom-call | flops 536870912 | bytes 2097152 | tf_op jit(solution)/shard_map/filter_grad/pallas_call | solution.py:279
  218.7 11.3 %leave.1 = (bf16[3,4,512,256]{3,2,1,0:T(8,128)(2,1)}, f32[16,1024]{1,0:T(8,128)}) custom-call(bf16[8,528,128]{2,1,0:T(8,128)(2,1)} %copy-done.11, bf16[512,1024]{1,0:T(8,128)(2,1)} %get-tuple-element.144.ggate, bf16[16,1024]{1,0:T(8,128)(2,1)} %copy-done.19, bf16[3,528,1024]{2,1,0:T(8,128)(2,1)} %get-tuple-element.125.proj, ...), custom_call_target="tpu_custom_call" | custom-call | flops 3932160 | bytes 1179648 | tf_op jit(solution)/shard_map/leave/pallas_call | solution.py:753
  241.1 10.4 %tokens_back.1 = (f32[512,1024]{1,0:T(8,128)}, f32[2,1024]{1,0:T(2,128)}) custom-call(bf16[3,4,512,256]{3,2,1,0:T(8,128)(2,1)} %get-tuple-element.167.gproj, bf16[1024,3072]{1,0:T(8,128)(2,1)} %weight.1, bf16[512,1024]{1,0:T(8,128)(2,1)} %bitcast.81, bf16[512,1024]{1,0:T(8,128)(2,1)} %get-tuple-element.136.gres, f32[1,1024]{1,0:T(1,128)} %bitcast.102), custom_call_target="tpu_custom_call" | custom-call | flops 402653184 | bytes 1835008 | tf_op jit(solution)/shard_map/tokens_back/pallas_call | solution.py:801
  255.2 5.7 %collective-permute-done.14 = bf16[4,128,1024]{2,1,0:T(8,128)(2,1)} collective-permute-done((bf16[4,128,1024]{2,1,0:T(8,128)(2,1)}, bf16[4,128,1024]{2,1,0:T(8,128)(2,1)}, u32[]{:S(2)}, u32[]{:S(2)}) %collective-permute-start.14) | collective-permute-done | bytes 1048608 | tf_op jit(solution)/shard_map/ppermute | solution.py:416
  267.4 9.9 %block_out.1 = bf16[512,1024]{1,0:T(8,128)(2,1)} custom-call(bf16[512,4096]{1,0:T(8,128)(2,1)} %get-tuple-element.179.refs_0_.refs_1_.act, bf16[4096,1024]{1,0:T(8,128)(2,1)} %down.3, bf16[512,1024]{1,0:T(8,128)(2,1)} %get-tuple-element.180.resid, f32[1,1024]{1,0:T(1,128)} %bitcast.111), custom_call_target="tpu_custom_call" | custom-call | flops 536870912 | bytes 1966080 | tf_op jit(solution)/shard_map/block_out/pallas_call | solution.py:510
  278.9 9.0 %wgrad.7 = (bf16[4,128,768]{2,1,0:T(8,128)(2,1)}, bf16[4,128,768]{2,1,0:T(8,128)(2,1)}) custom-call(s32[8]{0:T(128)} %broadcast_xor_fusion.row_order, s32[12]{0:T(128)} %pad_add_fusion.1.units, bf16[512,1024]{1,0:T(8,128)(2,1)} %get-tuple-element.185.refs_0_.refs_1_.refs_2_.refs_3_, bf16[512,1024]{1,0:T(8,128)(2,1)} %get-tuple-element.185.refs_0_.refs_1_.refs_2_.refs_3_, ...), custom_call_target="tpu_custom_call" | custom-call | flops 402653184 | bytes 1310720 | tf_op jit(solution)/shard_map/wgrad/pallas_call | solution.py:877
  301.8 9.4 %collective-permute-done.21 = f32[232,128]{1,0:T(8,128)S(1)} collective-permute-done((f32[232,128]{1,0:T(8,128)S(1)}, f32[232,128]{1,0:T(8,128)S(1)}, u32[]{:S(2)}, u32[]{:S(2)}) %collective-permute-start.21) | collective-permute-done | bytes 118816 | tf_op jit(solution)/shard_map/ppermute | solution.py:416
  324.2 9.6 %collective-permute-done.25 = f32[232,128]{1,0:T(8,128)S(1)} collective-permute-done((f32[232,128]{1,0:T(8,128)S(1)}, f32[232,128]{1,0:T(8,128)S(1)}, u32[]{:S(2)}, u32[]{:S(2)}) %collective-permute-start.25) | collective-permute-done | bytes 118816 | tf_op jit(solution)/shard_map/ppermute | solution.py:416
  338.6 5.2 %collective-permute-done.27 = bf16[1,128,1024]{2,1,0:T(8,128)(2,1)S(1)} collective-permute-done((bf16[1,128,1024]{2,1,0:T(8,128)(2,1)S(1)}, bf16[1,128,1024]{2,1,0:T(8,128)(2,1)S(1)}, u32[]{:S(2)}, u32[]{:S(2)}) %collective-permute-start.27) | collective-permute-done | bytes 262176 | tf_op jit(solution)/shard_map/ppermute | solution.py:416
  (202 shorter events, 110.1 us)
Async XLA Ops:
  3.5 14.6 %all-to-all-start = ((f32[8,28,128]{2,1,0:T(8,128)}), f32[8,28,128]{2,1,0:T(8,128)S(1)}, u32[]{:S(2)}, u32[]{:S(2)}) async-start(f32[8,28,128]{2,1,0:T(8,128)} %broadcast_in_dim.58), calls=%async_computation | async-start | bytes 262144 | tf_op jit(solution)/shard_map/all_to_all | solution.py:928
  31.1 31.8 %all-to-all-start.1 = ((bf16[8,512,128]{2,1,0:T(8,128)(2,1)}), bf16[8,512,128]{2,1,0:T(8,128)(2,1)S(1)}, u32[]{:S(2)}, u32[]{:S(2)}) async-start(bf16[8,512,128]{2,1,0:T(8,128)(2,1)} %get-tuple-element.121), calls=%async_computation.1 | async-start | bytes 2097152 | tf_op jit(solution)/shard_map/all_to_all | solution.py:948
  37.1 36.1 %collective-permute-start.1 = (bf16[512,1024]{1,0:T(8,128)(2,1)S(1)}, bf16[512,1024]{1,0:T(8,128)(2,1)S(1)}, u32[]{:S(2)}, u32[]{:S(2)}) collective-permute-start(bf16[512,1024]{1,0:T(8,128)(2,1)S(1)} %copy-done.5), channel_id=1, source_target_pairs={{0,16},{8,24},{16,0},{24,8},{1,17},{9,25},{17,1},{25,9},{2,18},{10... | collective-permute-start | bytes 3145736 | tf_op jit(solution)/shard_map/ppermute | solution.py:416
  55.5 17.8 %collective-permute-start = (bf16[3,16,1024]{2,1,0:T(8,128)(2,1)}, bf16[3,16,1024]{2,1,0:T(8,128)(2,1)}, u32[]{:S(2)}, u32[]{:S(2)}) collective-permute-start(bf16[3,16,1024]{2,1,0:T(8,128)(2,1)} %slice.227), channel_id=1, source_target_pairs={{1,0},{2,1},{3,2},{4,3},{5,4},{6,5},{7,6},{9,8},{10,9},{11,10},{12... | collective-permute-start | bytes 294920 | tf_op jit(solution)/shard_map/ppermute | solution.py:943
  73.3 32.5 %all-to-all-start.2 = ((bf16[8,512,128]{2,1,0:T(8,128)(2,1)}), bf16[8,512,128]{2,1,0:T(8,128)(2,1)}, u32[]{:S(2)}, u32[]{:S(2)}) async-start(bf16[8,512,128]{2,1,0:T(8,128)(2,1)} %get-tuple-element.127), calls=%async_computation.2 | async-start | bytes 2097152 | tf_op jit(solution)/shard_map/all_to_all | solution.py:952
  135.0 40.8 %collective-permute-start.5 = (bf16[1,512,4096]{2,1,0:T(8,128)(2,1)}, bf16[1,512,4096]{2,1,0:T(8,128)(2,1)}, u32[]{:S(2)}, u32[]{:S(2)}) collective-permute-start(bf16[1,512,4096]{2,1,0:T(8,128)(2,1)} %bitcast.75), channel_id=1, source_target_pairs={{0,8},{8,0},{16,24},{24,16},{1,9},{9,1},{17,25},{25,17},{2,10},{10... | collective-permute-start | bytes 12582920 | tf_op jit(solution)/shard_map/ppermute | solution.py:416
  135.5 30.7 %all-to-all-start.3 = ((bf16[8,512,128]{2,1,0:T(8,128)(2,1)}), bf16[8,512,128]{2,1,0:T(8,128)(2,1)}, u32[]{:S(2)}, u32[]{:S(2)}) async-start(bf16[8,512,128]{2,1,0:T(8,128)(2,1)} %get-tuple-element.134), calls=%async_computation.3 | async-start | bytes 2097152 | tf_op jit(solution)/shard_map/all_to_all | solution.py:948
  140.5 35.3 %collective-permute-start.6 = (bf16[512,1024]{1,0:T(8,128)(2,1)S(1)}, bf16[512,1024]{1,0:T(8,128)(2,1)}, u32[]{:S(2)}, u32[]{:S(2)}) collective-permute-start(bf16[512,1024]{1,0:T(8,128)(2,1)S(1)} %copy-done.8), channel_id=1, source_target_pairs={{0,8},{8,0},{16,24},{24,16},{1,9},{9,1},{17,25},{25,17},{2,10},{10... | collective-permute-start | bytes 3145736 | tf_op jit(solution)/shard_map/ppermute | solution.py:416
  158.2 72.2 %collective-permute-start.11 = (bf16[8,640,256]{2,1,0:T(8,128)(2,1)}, bf16[8,640,256]{2,1,0:T(8,128)(2,1)}, u32[]{:S(2)}, u32[]{:S(2)}) collective-permute-start(bf16[8,640,256]{2,1,0:T(8,128)(2,1)} %get-tuple-element.161), channel_id=1, source_target_pairs={{0,16},{8,24},{16,0},{24,8},{1,17},{9,25},{17,1},{25,9},{2,18},{10... | collective-permute-start | bytes 7864328 | tf_op jit(solution)/shard_map/ppermute | solution.py:416
  159.8 16.0 %collective-permute-start.10 = (bf16[16,1024]{1,0:T(8,128)(2,1)S(1)}, bf16[16,1024]{1,0:T(8,128)(2,1)S(1)}, u32[]{:S(2)}, u32[]{:S(2)}) collective-permute-start(bf16[16,1024]{1,0:T(8,128)(2,1)S(1)} %slice.228), channel_id=1, source_target_pairs={{1,0},{2,1},{3,2},{4,3},{5,4},{6,5},{7,6},{9,8},{10,9},{11,10},{12... | collective-permute-start | bytes 98312 | tf_op jit(solution)/shard_map/ppermute | solution.py:980
  175.9 41.8 %all-to-all-start.4 = ((bf16[8,528,128]{2,1,0:T(8,128)(2,1)}), bf16[8,528,128]{2,1,0:T(8,128)(2,1)S(1)}, u32[]{:S(2)}, u32[]{:S(2)}) async-start(bf16[8,528,128]{2,1,0:T(8,128)(2,1)} %get-tuple-element.150), calls=%async_computation.4 | async-start | bytes 2162688 | tf_op jit(solution)/shard_map/all_to_all | solution.py:952
  230.5 46.8 %all-to-all-start.5 = ((bf16[12,512,256]{2,1,0:T(8,128)(2,1)}), bf16[12,512,256]{2,1,0:T(8,128)(2,1)S(1)}, u32[]{:S(2)}, u32[]{:S(2)}) async-start(bf16[12,512,256]{2,1,0:T(8,128)(2,1)} %bitcast.78), calls=%async_computation.5 | async-start | bytes 6291456 | tf_op jit(solution)/shard_map/all_to_all | solution.py:1020
  234.6 26.3 %collective-permute-start.14 = (bf16[4,128,1024]{2,1,0:T(8,128)(2,1)}, bf16[4,128,1024]{2,1,0:T(8,128)(2,1)}, u32[]{:S(2)}, u32[]{:S(2)}) collective-permute-start(bf16[4,128,1024]{2,1,0:T(8,128)(2,1)} %get-tuple-element.177), channel_id=1, source_target_pairs={{0,2},{1,3},{2,0},{3,1},{4,6},{5,7},{6,4},{7,5},{8,10},{9,11},{10,... | collective-permute-start | bytes 3145736 | tf_op jit(solution)/shard_map/ppermute | solution.py:416
  252.2 35.7 %collective-permute-start.16 = (bf16[4,640,256]{2,1,0:T(8,128)(2,1)}, bf16[4,640,256]{2,1,0:T(8,128)(2,1)}, u32[]{:S(2)}, u32[]{:S(2)}) collective-permute-start(bf16[4,640,256]{2,1,0:T(8,128)(2,1)} %get-tuple-element.191), channel_id=1, source_target_pairs={{0,1},{1,0},{2,3},{3,2},{4,5},{5,4},{6,7},{7,6},{8,9},{9,8},{10,11... | collective-permute-start | bytes 3932168 | tf_op jit(solution)/shard_map/ppermute | solution.py:416
  253.9 34.0 %collective-permute-start.17 = (bf16[4,128,512]{2,1,0:T(8,128)(2,1)}, bf16[4,128,512]{2,1,0:T(8,128)(2,1)}, u32[]{:S(2)}, u32[]{:S(2)}) collective-permute-start(bf16[4,128,512]{2,1,0:T(8,128)(2,1)} %get-tuple-element.192), channel_id=1, source_target_pairs={{0,2},{1,3},{2,0},{3,1},{4,6},{5,7},{6,4},{7,5},{8,10},{9,11},{10,... | collective-permute-start | bytes 1572872 | tf_op jit(solution)/shard_map/ppermute | solution.py:416
  264.7 32.3 %collective-permute-start.15 = (bf16[4,128,1024]{2,1,0:T(8,128)(2,1)}, bf16[4,128,1024]{2,1,0:T(8,128)(2,1)}, u32[]{:S(2)}, u32[]{:S(2)}) collective-permute-start(bf16[4,128,1024]{2,1,0:T(8,128)(2,1)} %add_convert_fusion.3), channel_id=1, source_target_pairs={{0,16},{8,24},{16,0},{24,8},{1,17},{9,25},{17,1},{25,9},{2,18},{10... | collective-permute-start | bytes 3145736 | tf_op jit(solution)/shard_map/ppermute | solution.py:416
  267.4 29.7 %collective-permute-start.18 = (f32[304,128]{1,0:T(8,128)S(1)}, f32[304,128]{1,0:T(8,128)S(1)}, u32[]{:S(2)}, u32[]{:S(2)}) collective-permute-start(f32[304,128]{1,0:T(8,128)S(1)} %fusion.7), channel_id=1, source_target_pairs={{0,16},{8,24},{16,0},{24,8},{1,17},{9,25},{17,1},{25,9},{2,18},{10... | collective-permute-start | bytes 466952 | tf_op jit(solution)/shard_map/ppermute | solution.py:416
  287.9 23.3 %collective-permute-start.19 = (bf16[4,128,768]{2,1,0:T(8,128)(2,1)}, bf16[4,128,768]{2,1,0:T(8,128)(2,1)S(1)}, u32[]{:S(2)}, u32[]{:S(2)}) collective-permute-start(bf16[4,128,768]{2,1,0:T(8,128)(2,1)} %get-tuple-element.197), channel_id=1, source_target_pairs={{0,1},{1,0},{2,3},{3,2},{4,5},{5,4},{6,7},{7,6},{8,9},{9,8},{10,11... | collective-permute-start | bytes 2359304 | tf_op jit(solution)/shard_map/ppermute | solution.py:416
  292.8 18.4 %collective-permute-start.20 = (bf16[2,640,256]{2,1,0:T(8,128)(2,1)S(1)}, bf16[2,640,256]{2,1,0:T(8,128)(2,1)S(1)}, u32[]{:S(2)}, u32[]{:S(2)}) collective-permute-start(bf16[2,640,256]{2,1,0:T(8,128)(2,1)S(1)} %get-tuple-element.218), channel_id=1, source_target_pairs={{0,2},{1,3},{2,0},{3,1},{4,6},{5,7},{6,4},{7,5},{8,10},{9,11},{10,... | collective-permute-start | bytes 1966088 | tf_op jit(solution)/shard_map/ppermute | solution.py:416
  300.8 19.2 %collective-permute-start.24 = (bf16[2,128,1024]{2,1,0:T(8,128)(2,1)S(1)}, bf16[2,128,1024]{2,1,0:T(8,128)(2,1)S(1)}, u32[]{:S(2)}, u32[]{:S(2)}) collective-permute-start(bf16[2,128,1024]{2,1,0:T(8,128)(2,1)S(1)} %get-tuple-element.220), channel_id=1, source_target_pairs={{0,1},{1,0},{2,3},{3,2},{4,5},{5,4},{6,7},{7,6},{8,9},{9,8},{10,11... | collective-permute-start | bytes 1572872 | tf_op jit(solution)/shard_map/ppermute | solution.py:416
  311.3 22.5 %collective-permute-start.23 = (bf16[1,640,256]{2,1,0:T(8,128)(2,1)S(1)}, bf16[1,640,256]{2,1,0:T(8,128)(2,1)S(1)}, u32[]{:S(2)}, u32[]{:S(2)}) collective-permute-start(bf16[1,640,256]{2,1,0:T(8,128)(2,1)S(1)} %add_convert_fusion.11), channel_id=1, source_target_pairs={{0,4},{1,5},{2,6},{3,7},{4,0},{5,1},{6,2},{7,3},{8,12},{9,13},{10,... | collective-permute-start | bytes 983048 | tf_op jit(solution)/shard_map/ppermute | solution.py:416
  314.1 19.7 %collective-permute-start.22 = (bf16[2,128,768]{2,1,0:T(8,128)(2,1)S(1)}, bf16[2,128,768]{2,1,0:T(8,128)(2,1)S(1)}, u32[]{:S(2)}, u32[]{:S(2)}) collective-permute-start(bf16[2,128,768]{2,1,0:T(8,128)(2,1)S(1)} %get-tuple-element.222), channel_id=1, source_target_pairs={{0,2},{1,3},{2,0},{3,1},{4,6},{5,7},{6,4},{7,5},{8,10},{9,11},{10,... | collective-permute-start | bytes 1179656 | tf_op jit(solution)/shard_map/ppermute | solution.py:416
  321.8 22.0 %collective-permute-start.27 = (bf16[1,128,1024]{2,1,0:T(8,128)(2,1)S(1)}, bf16[1,128,1024]{2,1,0:T(8,128)(2,1)S(1)}, u32[]{:S(2)}, u32[]{:S(2)}) collective-permute-start(bf16[1,128,1024]{2,1,0:T(8,128)(2,1)S(1)} %add_convert_fusion.13), channel_id=1, source_target_pairs={{0,4},{1,5},{2,6},{3,7},{4,0},{5,1},{6,2},{7,3},{8,12},{9,13},{10,... | collective-permute-start | bytes 786440 | tf_op jit(solution)/shard_map/ppermute | solution.py:416
  335.0 14.6 %collective-permute-start.26 = (f32[232,128]{1,0:T(8,128)S(1)}, f32[232,128]{1,0:T(8,128)S(1)}, u32[]{:S(2)}, u32[]{:S(2)}) collective-permute-start(f32[232,128]{1,0:T(8,128)S(1)} %add.165), channel_id=1, source_target_pairs={{0,4},{1,5},{2,6},{3,7},{4,0},{5,1},{6,2},{7,3},{8,12},{9,13},{10,... | collective-permute-start | bytes 356360 | tf_op jit(solution)/shard_map/ppermute | solution.py:416
  (43 other events, 445.1 us)
